TPU v7x, 32 devices: a whole 2x2x4 slice. The times are simulated.
32 devices in a mesh: dp: 8 (over z, y), mp: 4 (over x, core).
Axes of the slice: x: 2, y: 2, z: 4, core: 2. Of those that a mesh axis runs over, the one named last changes fastest.
Arguments:
- clean_latent: float32 [64, 1024, 512], P(('dp', 'mp')), may hold values from -6 to 6
- noise_latent: float32 [64, 1024, 512], P(('dp', 'mp')), may hold values from -6 to 6
- codec_tokens: bfloat16 [64, 512, 768], P(('dp', 'mp')), may hold values from -6 to 6
- codec_mask: int32 [64, 512], P(('dp', 'mp')), may hold values from 0 to 1, as said below
- frames: int32 [64], P(('dp', 'mp')), may hold values from 25 to 128, as said below
- timesteps: int32 [64], P(('dp', 'mp')), may hold values from 0 to 999
- out_cotangent: float32 [64, 1024, 512], P(('dp', 'mp')), may hold values from -6 to 6
- master_blocks: float32 [240, 128, 128], P('mp', 'dp'), may hold values from -6 to 6
- norm_params: float32 [6, 512], P(None, ('dp', 'mp'))
- owned_block: int32 [240], replicated, may hold values from 0 to 239, each once
- left_stats: float32 [240, 128, 128], P('mp', 'dp')
- right_stats: float32 [240, 128, 128], P('mp', 'dp')
- left_root: float32 [240, 128, 128], P('mp')
- right_root: float32 [240, 128, 128], P('mp')
Outputs:
- block_output: float32 [64, 1024, 512], P(('dp', 'mp'))
- input_grad: float32 [64, 1024, 512], P(('dp', 'mp'))
- owned_grad: float32 [240, 128, 128], P('mp', 'dp')
- new_left: float32 [240, 128, 128], P('mp', 'dp')
- new_right: float32 [240, 128, 128], P('mp', 'dp')
- new_master: float32 [240, 128, 128], P('mp', 'dp')
- master_copy: bfloat16 [240, 128, 128], P('mp', 'dp')
- norm_grads: float32 [6, 512], P(None, ('dp', 'mp'))
- new_norm: float32 [6, 512], P(None, ('dp', 'mp'))
Inputs may be any that keep to these rules, and one draw needn't show every extreme that they name: frames[c] counts the clip's valid latent frames; cells of later frames are padding. codec_mask[c, l] is 1 only where l < 4 * frames[c], and codec_mask[c, 0] is 1. A permutation: slot s holds block owned_block[s]; slots s of mp index s // (240 / number of mp devices).
All inputs are finite; a program needn't handle non-finite values.
Results may differ from a plain program's by a relative error of at most 0.0095.
The roundings to bfloat16 on the way count: a program that leaves them out, or rounds other values in their place, can miss the bound.
Values may be sent and summed in bfloat16 or wider, within the bound.
No kernel may reach another device: no remote copies, remote signals or barrier semaphores. Data moves between devices by JAX's collectives and lax.ppermute only.
A program may use at most 256 MiB of HBM per device.

v0:
```python
import math

import jax
import jax.numpy as jnp
from jax import lax
from jax.sharding import PartitionSpec as P

LATENT_CHANNELS = 512
GROUPS = 32
HEADS = 8
HEADDIM = 64
CTX = 768
BINS = 8
TSTEPS = 1000
BS = 128
POS = 1024


highest = lax.Precision.HIGHEST
learn_rate = 0.5
out_gain = 8.0


def unblock(blocks, first_block, row_count, col_count):
    amount = row_count // BS * (col_count // BS)
    block_part = blocks[first_block : first_block + amount]
    return (
        block_part.reshape(row_count // BS, col_count // BS, BS, BS)
        .transpose(0, 2, 1, 3)
        .reshape(row_count, col_count)
    )


def matrices(blocks):
    square = LATENT_CHANNELS // BS * (LATENT_CHANNELS // BS)
    conv_taps = jnp.stack(
        [
            unblock(blocks, tap_index * square, LATENT_CHANNELS, LATENT_CHANNELS)
            for tap_index in range(9)
        ]
    )
    offset = 9 * square
    temb_w = unblock(blocks, offset, LATENT_CHANNELS, LATENT_CHANNELS)
    query_w = unblock(blocks, offset + square, LATENT_CHANNELS, LATENT_CHANNELS)
    out_w = unblock(blocks, offset + 2 * square, LATENT_CHANNELS, LATENT_CHANNELS)
    key_w = unblock(blocks, offset + 3 * square, CTX, LATENT_CHANNELS)
    value_w = unblock(
        blocks, offset + 3 * square + CTX // BS * (LATENT_CHANNELS // BS), CTX, LATENT_CHANNELS
    )
    return (conv_taps, temb_w, query_w, out_w, key_w, value_w)


def rebuild_blocks(block_matrix):
    row_count, col_count = block_matrix.shape
    return (
        block_matrix.reshape(row_count // BS, BS, col_count // BS, BS)
        .transpose(0, 2, 1, 3)
        .reshape(-1, BS, BS)
    )


def arrange_blocks(gathered, n_data, n_model):
    slot_count, row_share = (gathered.shape[1], gathered.shape[2])
    blocks = gathered.reshape(n_data, n_model, slot_count, row_share, BS).transpose(1, 2, 0, 3, 4)
    return matrices(blocks.reshape(n_model * slot_count, n_data * row_share, BS))


def group_norm(values, frame_mask, gain_row, shift_row):
    group_width = LATENT_CHANNELS // GROUPS
    grouped = values.reshape(values.shape[:-1] + (GROUPS, group_width))
    mask_wide = frame_mask[..., None, None]
    counted = jnp.sum(frame_mask, axis=-1) * group_width
    group_mean = jnp.sum(grouped * mask_wide, axis=(-3, -1)) / counted[..., None]
    centred = grouped - group_mean[..., None, :, None]
    group_var = jnp.sum(centred * centred * mask_wide, axis=(-3, -1)) / counted[..., None]
    normed = centred * lax.rsqrt(group_var + 1e-05)[..., None, :, None]
    return normed.reshape(values.shape) * gain_row + shift_row


def sinusoid(timesteps):
    half_width = LATENT_CHANNELS // 2
    freqs = jnp.exp(-math.log(10000.0) * jnp.arange(half_width, dtype=jnp.float32) / half_width)
    angles = timesteps.astype(jnp.float32)[:, None] * freqs[None, :]
    return jnp.concatenate([jnp.sin(angles), jnp.cos(angles)], axis=-1)


def bin_masks(sign_back):
    bin_of = jnp.arange(POS, dtype=jnp.int32) % BINS
    masks = []
    for bin_off in range(3):
        moved = bin_of - (bin_off - 1) if sign_back else bin_of + (bin_off - 1)
        masks.append(((moved >= 0) & (moved < BINS)).astype(jnp.bfloat16)[None, :, None])
    return masks


def pad_cells(values):
    return jnp.pad(values, ((0, 0), (BINS + 1, BINS + 1), (0, 0)))


def cell_window(padded, start, mask):
    return lax.slice_in_dim(padded, start, start + POS, axis=1) * mask


def convolve(acts, conv_taps, fwd_masks):
    clip_count = acts.shape[0]
    padded = pad_cells(acts)
    summed = jnp.zeros((clip_count * POS, LATENT_CHANNELS), jnp.float32)
    for tap_index in range(9):
        frame_off, bin_off = divmod(tap_index, 3)
        window = cell_window(padded, frame_off * BINS + bin_off, fwd_masks[bin_off]).reshape(
            -1, LATENT_CHANNELS
        )
        summed = summed + jnp.dot(window, conv_taps[tap_index], preferred_element_type=jnp.float32)
    return (summed.reshape(clip_count, POS, LATENT_CHANNELS), padded)


def attention_scores(queries, key_heads, key_mask):
    scores = jnp.einsum(
        "cphd,clhd->chpl", queries, key_heads, preferred_element_type=jnp.float32
    ) * (1.0 / math.sqrt(HEADDIM))
    return jnp.where(key_mask[:, None, None, :] > 0, scores, -1000000000.0)


def body(
    clean_latent,
    noise_latent,
    codec_tokens,
    codec_mask,
    frames,
    timesteps,
    out_cotangent,
    master_blocks,
    norm_params,
    owned_block,
    left_stats,
    right_stats,
    left_root,
    right_root,
):
    n_data = lax.axis_size("dp")
    n_model = lax.axis_size("mp")
    total_devices = n_data * n_model
    clip_count = clean_latent.shape[0]
    ctx_len = codec_tokens.shape[1]
    slot_count, row_share = (master_blocks.shape[0], master_blocks.shape[1])
    conv_scale = 1.0 / math.sqrt(9 * LATENT_CHANNELS)
    inv_width = 1.0 / math.sqrt(LATENT_CHANNELS)
    inv_context = 1.0 / math.sqrt(CTX)
    out_scale = out_gain / math.sqrt(LATENT_CHANNELS)
    att_scale = 1.0 / math.sqrt(HEADDIM)
    fwd_masks = bin_masks(False)
    back_masks = bin_masks(True)
    master_low = master_blocks.astype(jnp.bfloat16)[None]
    params_low = norm_params.astype(jnp.bfloat16)[None]
    gathered, gathered_params = (
        lax.all_gather(master_low, ("dp", "mp"), axis=0, tiled=True),
        lax.all_gather(params_low, ("dp", "mp"), axis=0, tiled=True),
    )
    forward_set = arrange_blocks(gathered, n_data, n_model)
    params = (
        gathered_params.transpose(1, 0, 2).reshape(gathered_params.shape[1], -1).astype(jnp.float32)
    )
    conv_taps, temb_w, query_w, out_w, key_w, value_w = forward_set
    frame_of = jnp.arange(POS, dtype=jnp.int32) // BINS
    frame_mask = (frame_of[None, :] < frames[:, None]).astype(jnp.float32)
    phases = timesteps.astype(jnp.float32) * (0.5 * math.pi / TSTEPS)
    inputs = frame_mask[:, :, None] * (
        jnp.cos(phases)[:, None, None] * clean_latent
        + jnp.sin(phases)[:, None, None] * noise_latent
    )
    embedding = jax.nn.silu(sinusoid(timesteps)).astype(jnp.bfloat16)
    key_mask = codec_mask.astype(jnp.float32)

    def first_part(latents, gain_row, shift_row):
        return (
            jax.nn.silu(group_norm(latents, frame_mask, gain_row, shift_row))
            * frame_mask[:, :, None]
        )

    def second_part(values, gain_row, shift_row):
        return group_norm(values, frame_mask, gain_row, shift_row)

    first_out, first_pull = jax.vjp(first_part, inputs, params[0], params[1])
    acts = first_out.astype(jnp.bfloat16)
    conv_sum, padded = convolve(acts, conv_taps, fwd_masks)
    conv_out = conv_sum * conv_scale
    temb_out = jnp.dot(embedding, temb_w, preferred_element_type=jnp.float32) * inv_width
    residual = inputs + conv_out + temb_out[:, None, :] + params[2]
    second_out, second_pull = jax.vjp(second_part, residual, params[3], params[4])
    normed = second_out.astype(jnp.bfloat16).reshape(-1, LATENT_CHANNELS)
    queries = (
        (jnp.dot(normed, query_w, preferred_element_type=jnp.float32) * inv_width)
        .astype(jnp.bfloat16)
        .reshape(clip_count, POS, HEADS, HEADDIM)
    )
    context_rows = codec_tokens.reshape(-1, CTX)
    pair_w = jnp.concatenate([key_w, value_w], axis=1)
    key_value = (
        jnp.dot(context_rows, pair_w, preferred_element_type=jnp.float32) * inv_context
    ).astype(jnp.bfloat16)
    key_heads = key_value[:, :LATENT_CHANNELS].reshape(clip_count, ctx_len, HEADS, HEADDIM)
    value_heads = key_value[:, LATENT_CHANNELS:].reshape(clip_count, ctx_len, HEADS, HEADDIM)
    scores = attention_scores(queries, key_heads, key_mask)
    row_max = jnp.max(scores, axis=-1, keepdims=True)
    log_total = row_max + jnp.log(jnp.sum(jnp.exp(scores - row_max), axis=-1, keepdims=True))
    attn_probs = jnp.exp(scores - log_total).astype(jnp.bfloat16)
    mixed_heads = (
        jnp.einsum("chpl,clhd->cphd", attn_probs, value_heads, preferred_element_type=jnp.float32)
        .astype(jnp.bfloat16)
        .reshape(-1, LATENT_CHANNELS)
    )
    projected = (
        jnp.dot(mixed_heads, out_w, preferred_element_type=jnp.float32) * out_scale + params[5]
    )
    block_output = frame_mask[:, :, None] * (
        residual + projected.reshape(clip_count, POS, LATENT_CHANNELS)
    )
    regathered = lax.all_gather(master_low, ("dp", "mp"), axis=0, tiled=True)
    back_set = arrange_blocks(regathered, n_data, n_model)
    conv_back, temb_back, query_back, out_back, key_back, value_back = back_set
    res_grad = frame_mask[:, :, None] * out_cotangent
    out_bias_grad = jnp.sum(res_grad, axis=(0, 1))
    out_low = res_grad.astype(jnp.bfloat16).reshape(-1, LATENT_CHANNELS)
    output_weight_gradient = (
        jnp.einsum("nc,nd->cd", mixed_heads, out_low, preferred_element_type=jnp.float32)
        * out_scale
    )
    mixed_grad = (
        (jnp.einsum("nd,cd->nc", out_low, out_back, preferred_element_type=jnp.float32) * out_scale)
        .astype(jnp.bfloat16)
        .reshape(clip_count, POS, HEADS, HEADDIM)
    )
    scores_again = attention_scores(queries, key_heads, key_mask)
    probs_again = jnp.exp(scores_again - log_total)
    prob_grad = jnp.einsum(
        "cphd,clhd->chpl", mixed_grad, value_heads, preferred_element_type=jnp.float32
    )
    value_grad = jnp.einsum(
        "chpl,cphd->clhd",
        probs_again.astype(jnp.bfloat16),
        mixed_grad,
        preferred_element_type=jnp.float32,
    )
    row_delta = jnp.sum(probs_again * prob_grad, axis=-1, keepdims=True)
    score_grad = (probs_again * (prob_grad - row_delta)).astype(jnp.bfloat16)
    query_grad = (
        (
            jnp.einsum("chpl,clhd->cphd", score_grad, key_heads, preferred_element_type=jnp.float32)
            * att_scale
        )
        .astype(jnp.bfloat16)
        .reshape(-1, LATENT_CHANNELS)
    )
    key_grad = (
        jnp.einsum("chpl,cphd->clhd", score_grad, queries, preferred_element_type=jnp.float32)
        * att_scale
    )
    pair_grad = jnp.concatenate(
        [key_grad.reshape(-1, LATENT_CHANNELS), value_grad.reshape(-1, LATENT_CHANNELS)], axis=1
    ).astype(jnp.bfloat16)
    paired_weight_gradient = (
        jnp.einsum("nc,nd->cd", context_rows, pair_grad, preferred_element_type=jnp.float32)
        * inv_context
    )
    query_weight_gradient = (
        jnp.einsum("nc,nd->cd", normed, query_grad, preferred_element_type=jnp.float32) * inv_width
    )
    normed_grad = (
        jnp.einsum("nd,cd->nc", query_grad, query_back, preferred_element_type=jnp.float32)
        * inv_width
    ).reshape(clip_count, POS, LATENT_CHANNELS)
    resid_norm_grad, gain_two_grad, shift_two_grad = second_pull(normed_grad)
    resid_grad = res_grad + resid_norm_grad
    conv_bias_grad = jnp.sum(resid_grad, axis=(0, 1))
    temb_grad = jnp.sum(resid_grad, axis=1).astype(jnp.bfloat16)
    timestep_embedding_weight_gradient = (
        jnp.einsum("nc,nd->cd", embedding, temb_grad, preferred_element_type=jnp.float32)
        * inv_width
    )
    conv_grad_cells = resid_grad.astype(jnp.bfloat16)
    conv_grad = conv_grad_cells.reshape(-1, LATENT_CHANNELS)
    grad_padded = pad_cells(conv_grad_cells)
    act_sum = jnp.zeros((clip_count * POS, LATENT_CHANNELS), jnp.float32)
    convolution_weight_gradients = []
    for tap_index in range(9):
        frame_off, bin_off = divmod(tap_index, 3)
        window = cell_window(padded, frame_off * BINS + bin_off, fwd_masks[bin_off]).reshape(
            -1, LATENT_CHANNELS
        )
        convolution_weight_gradients.append(
            jnp.einsum("nc,nd->cd", window, conv_grad, preferred_element_type=jnp.float32)
            * conv_scale
        )
        back_window = cell_window(
            grad_padded, (2 - frame_off) * BINS + (2 - bin_off), back_masks[bin_off]
        ).reshape(-1, LATENT_CHANNELS)
        act_sum = act_sum + jnp.einsum(
            "nd,cd->nc", back_window, conv_back[tap_index], preferred_element_type=jnp.float32
        )
    act_grad = act_sum.reshape(clip_count, POS, LATENT_CHANNELS) * conv_scale
    first_grad, gain_one_grad, shift_one_grad = first_pull(act_grad)
    input_grad = resid_grad + first_grad
    local_blocks = jnp.concatenate(
        [
            rebuild_blocks(kernel_tap_gradient)
            for kernel_tap_gradient in convolution_weight_gradients
        ]
        + [
            rebuild_blocks(timestep_embedding_weight_gradient),
            rebuild_blocks(query_weight_gradient),
            rebuild_blocks(output_weight_gradient),
            rebuild_blocks(paired_weight_gradient[:, :LATENT_CHANNELS]),
            rebuild_blocks(paired_weight_gradient[:, LATENT_CHANNELS:]),
        ],
        axis=0,
    )
    param_grads = jnp.stack(
        [
            gain_one_grad,
            shift_one_grad,
            conv_bias_grad,
            gain_two_grad,
            shift_two_grad,
            out_bias_grad,
        ]
    )
    permuted = jnp.take(local_blocks, owned_block, axis=0)
    arranged = (
        permuted.reshape(n_model, slot_count, n_data, row_share, BS)
        .transpose(2, 0, 1, 3, 4)
        .reshape(-1, row_share, BS)
    )
    param_rows = param_grads.shape[0]
    param_arranged = (
        param_grads.reshape(param_rows, total_devices, -1)
        .transpose(1, 0, 2)
        .reshape(total_devices * param_rows, -1)
    )
    owned_rows, norm_grads = (
        lax.psum_scatter(arranged, ("dp", "mp"), scatter_dimension=0, tiled=True),
        lax.psum_scatter(param_arranged, ("dp", "mp"), scatter_dimension=0, tiled=True),
    )
    full_grad = lax.all_gather(owned_rows, "dp", axis=1, tiled=True)
    row_start = lax.axis_index("dp") * row_share
    my_columns = lax.dynamic_slice_in_dim(full_grad, row_start, row_share, 2)
    new_left = 0.5 * left_stats + 0.5 * jnp.einsum(
        "srk,stk->srt", owned_rows, full_grad, precision=highest
    )
    new_right = 0.5 * right_stats + 0.5 * jnp.einsum(
        "skr,skt->srt", my_columns, full_grad, precision=highest
    )
    left_side = jnp.einsum("srk,skt->srt", left_root, full_grad, precision=highest)
    update = jnp.einsum("srk,skt->srt", left_side, right_root, precision=highest)
    update_step = (
        learn_rate
        * update
        * lax.rsqrt(jnp.mean(update * update, axis=(1, 2), keepdims=True) + 1e-06)
    )
    step_rows = lax.dynamic_slice_in_dim(update_step, row_start, row_share, 1)
    all_steps = lax.all_gather(step_rows, "mp", axis=0, tiled=True)
    natural = jnp.zeros_like(all_steps).at[owned_block].set(all_steps)
    my_steps = lax.dynamic_slice_in_dim(natural, lax.axis_index("mp") * slot_count, slot_count, 0)
    new_master = master_blocks - my_steps
    small_rate = 0.5 / math.sqrt(clip_count * total_devices * POS)
    new_norm = norm_params - small_rate * norm_grads
    return (
        block_output,
        input_grad,
        owned_rows,
        new_left,
        new_right,
        new_master,
        new_master.astype(jnp.bfloat16),
        norm_grads,
        new_norm,
    )


def solution(mesh):
    in_specs = (
        P(("dp", "mp"), None, None),
        P(("dp", "mp"), None, None),
        P(("dp", "mp"), None, None),
        P(("dp", "mp"), None),
        P(("dp", "mp")),
        P(("dp", "mp")),
        P(("dp", "mp"), None, None),
        P("mp", "dp", None),
        P(None, ("dp", "mp")),
        P(),
        P("mp", "dp", None),
        P("mp", "dp", None),
        P("mp", None, None),
        P("mp", None, None),
    )
    out_specs = (
        P(("dp", "mp"), None, None),
        P(("dp", "mp"), None, None),
        P("mp", "dp", None),
        P("mp", "dp", None),
        P("mp", "dp", None),
        P("mp", "dp", None),
        P("mp", "dp", None),
        P(None, ("dp", "mp")),
        P(None, ("dp", "mp")),
    )
    return jax.shard_map(body, mesh=mesh, in_specs=in_specs, out_specs=out_specs, check_vma=False)
```

profile of v0, /device:TPU:0, one launch (start us, length us, event | category | flops | bytes accessed | tf_op | source)
XLA Modules:
  0.0 915.2 jit_solution(10260683018698444591)
XLA Ops:
  11.8 43.9 %all-gather.2 = bf16[32,6,16]{2,1,0:T(8,128)(2,1)S(1)} all-gather(bf16[1,6,16]{2,1,0:T(8,128)(2,1)S(1)} %convert_bitcast_fusion.2), channel_id=2, replica_groups=mesh['dp'=8,'mp'=4] {'dp','mp'}, dimensions={0}, use_global_device_ids=true | all-gather | bytes 6336 | tf_op jit(solution)/shard_map/all_gather | solution.py:157
  75.9 9.2 %slice_multiply_fusion.8 = (bf16[2,1024,512]{2,1,0:T(8,128)(2,1)}, bf16[2,1024,512]{2,1,0:T(8,128)(2,1)}, bf16[2,1024,512]{2,1,0:T(8,128)(2,1)}, bf16[2,1024,512...) fusion(bf16[1024]{0:T(1024)(128)(2,1)S(1)} %get-tuple-element.1, ...), kind=kLoop, calls=%fused_computation.65 | loop fusion | flops 28311552 | bytes 18880512 | tf_op jit(solution)/shard_map/mul | solution.py:101
  152.3 14.6 %add_multiply_fusion.1 = f32[2048,512]{1,0:T(8,128)} fusion(f32[2048,512]{1,0:T(8,128)} %fusion.55, f32[2048,512]{1,0:T(8,128)} %fusion.59, f32[2048,512]{1,0:T(8,128)} %fusion.63, f32[2048,512]{1,0:T(8,128)S(1)} %fusion.67, f32[2048,512]{1,0:T(8,128)} %fusion.71, f32[2048,512]{1,0:T(8,128)} %fusion.75, f32[2048,512]{1,0:T(8,128)} %fusion.83, ...), kind=kOutput, calls=%fused_computation.37 | convolution fusion | flops 1083179008 | bytes 40370176 | tf_op jit(solution)/shard_map/dot_general | solution.py:113
  216.8 15.6 %fusion = (f32[2,8,1024]{2,1,0:T(8,128)S(1)}, f32[2,8,1024,512]{2,3,1,0:T(8,128)}) fusion(pred[2,512]{1,0:T(4,128)(4,1)S(1)} %convert_compare_fusion, bf16[2,1024,8,64]{1,3,2,0:T(8,128)(2,1)} %copy.281, bf16[2,512,8,64]{1,0,3,2:T(2,128)(2,1)S(1)} %copy-done.26), kind=kOutput, calls=%fused_computation.7 | convolution fusion | flops 1098891264 | bytes 36766720 | tf_op jit(solution)/shard_map/cphd,clhd->chpl/dot_general | solution.py:118
  232.4 14.5 %exponential_reduce_fusion = f32[2,8,1024]{2,1,0:T(8,128)S(1)} fusion(f32[2,8,1024,512]{2,3,1,0:T(8,128)} %get-tuple-element.105, f32[2,8,1024]{2,1,0:T(8,128)S(1)} %get-tuple-element.104, pred[2,512]{1,0:T(4,128)(4,1)S(1)} %convert_compare_fusion), kind=kLoop, calls=%fused_computation.5 | loop fusion | flops 33538048 | bytes 33686528 | tf_op jit(solution)/shard_map/reduce_sum | solution.py:205
  246.9 16.1 %fusion.21 = bf16[2,512,8,64]{1,3,2,0:T(8,128)(2,1)} fusion(bf16[2,1024,8,64]{1,3,2,0:T(8,128)(2,1)} %copy.288, f32[2,8,1024,512]{2,3,1,0:T(8,128)} %get-tuple-element.105, f32[2,8,1024]{2,1,0:T(8,128)S(1)} %log_add_fusion, pred[2,512]{1,0:T(4,128)(4,1)S(1)} %convert_compare_fusion), kind=kOutput, calls=%fused_computation.79 | convolution fusion | flops 1107820544 | bytes 36766720 | tf_op jit(solution)/shard_map/chpl,cphd->clhd/dot_general | solution.py:238
  263.0 15.9 %convert_bitcast_fusion = bf16[2,1024,8,64]{1,3,2,0:T(8,128)(2,1)} fusion(bf16[2,512,8,64]{1,0,3,2:T(2,128)(2,1)} %reshape.643, f32[2,8,1024,512]{2,3,1,0:T(8,128)} %get-tuple-element.105, f32[2,8,1024]{2,1,0:T(8,128)S(1)} %log_add_fusion, pred[2,512]{1,0:T(4,128)(4,1)S(1)} %convert_compare_fusion), kind=kOutput, calls=%fused_computation.64 | convolution fusion | flops 1108344832 | bytes 36766720 | tf_op jit(solution)/shard_map/chpl,clhd->cphd/dot_general | solution.py:208
  278.9 24.1 %multiply_reduce_fusion = (f32[2,8,1024]{2,1,0:T(8,128)S(1)}, f32[2,8,1024,512]{2,3,1,0:T(8,128)}) fusion(f32[2,8,1024,512]{2,3,1,0:T(8,128)} %get-tuple-element.105, f32[2,8,1024]{2,1,0:T(8,128)S(1)} %log_add_fusion, pred[2,512]{1,0:T(4,128)(4,1)S(1)} %convert_compare_fusion, bf16[2,1024,8,64]{1,3,2,0:T(8,128)(2,1)S(1)} %copy-done.25, ...), kind=kOutput, calls=%fused_computation.3 | convolution fusion | flops 1115668480 | bytes 70386688 | tf_op jit(solution)/shard_map/cphd,clhd->chpl/dot_general | solution.py:235
  303.0 28.0 %multiply_convert_fusion = bf16[2,8,1024,512]{2,3,1,0:T(8,128)(2,1)} fusion(f32[2,8,1024,512]{2,3,1,0:T(8,128)} %get-tuple-element.107, f32[2,8,1024,512]{2,3,1,0:T(8,128)} %get-tuple-element.105, f32[2,8,1024]{2,1,0:T(8,128)S(1)} %get-tuple-element.106, f32[2,8,1024]{2,1,0:T(8,128)S(1)} %log_add_fusion, pred[2,512]{1,0:T(4,128)(4,1)S(1)} %convert_compare_fusion), kind=kLoop, calls=%fused_computation.2 | loop fusion | flops 50331648 | bytes 84018176 | tf_op jit(solution)/shard_map/convert_element_type | solution.py:245
  331.0 12.6 %fusion.22 = bf16[2,512,8,64]{1,3,2,0:T(8,128)(2,1)} fusion(bf16[2,1024,8,64]{1,3,2,0:T(8,128)(2,1)} %copy.281, bf16[2,8,1024,512]{2,3,1,0:T(8,128)(2,1)} %multiply_convert_fusion), kind=kOutput, calls=%fused_computation.80 | convolution fusion | flops 1074790400 | bytes 19922944 | tf_op jit(solution)/shard_map/chpl,cphd->clhd/dot_general | solution.py:255
  343.6 8.8 fusion.17
  382.9 8.9 fusion.4
  392.2 9.4 %fusion.143 = (f32[512]{0:T(512)S(1)}, bf16[2,512]{1,0:T(2,128)(2,1)S(1)}, f32[2,1024,512]{2,1,0:T(8,128)S(1)}, f32[2,1024,512]{2,1,0:T(8,128)}) fusion(f32[2,512]{1,0:T(2,128)S(1)} %broadcast_in_dim.112, f32[2,512]{1,0:T(2,128)S(1)} %broadcast_in_dim.108, f32[2,1024,512]{2,1,0:T(8,128)} %get-tuple-element.44, f32[2,512]{1,0:T(2,128)S(1)} %sub.89, ...), kind=kLoop, calls=%fused_computation.271 | loop fusion | flops 15727104 | bytes 25196544 | tf_op jit(solution)/shard_map/reduce_sum | solution.py:274
  523.0 17.2 %gather_fusion = f32[240,128,128]{2,1,0:T(8,128)} fusion(f32[240,128,128]{2,1,0:T(8,128)} %constant_dynamic-update-slice_fusion, s32[1024]{0:T(1024)} %pad_clamp_fusion), kind=kCustom, calls=%fused_computation | custom fusion | bytes 31458240 | tf_op jit(solution)/shard_map/jit(_take)/gather | solution.py:327
  540.2 11.1 %select_bitcast_fusion = f32[8,4,60,16,128]{4,3,0,2,1:T(8,128)} fusion(f32[4,60,8,16,128]{4,3,2,1,0:T(8,128)} %bitcast.343, pred[4,60]{1,0:T(4,128)(4,1)S(1)} %copy-done.107), kind=kLoop, calls=%fused_computation.9 | loop fusion | flops 3932160 | bytes 31457520 | tf_op jit(solution)/shard_map/transpose | solution.py:330
  551.3 13.0 %copy.331 = f32[8,4,60,16,128]{4,3,2,1,0:T(8,128)} copy(f32[8,4,60,16,128]{4,3,0,2,1:T(8,128)} %select_bitcast_fusion) | data formatting | bytes 31457280 | tf_op jit(solution)/shard_map/transpose | solution.py:330
  567.2 166.4 %reduce-scatter.2.cloned.1.call-done = f32[60,16,128]{2,1,0:T(8,128)} async-done(((f32[1920,16,128]{2,1,0:T(8,128)}), f32[60,16,128]{2,1,0:T(8,128)}) %reduce-scatter.2.cloned.1.call-update) | async-done | bytes 491536 | tf_op jit(solution)/shard_map/reduce_scatter | solution.py:340
  736.7 8.7 slice_multiply_fusion
  766.5 13.9 %add_add_fusion.4 = f32[2048,512]{1,0:T(8,128)} fusion(f32[2048,512]{1,0:T(8,128)} %fusion.53, f32[2048,512]{1,0:T(8,128)} %fusion.57, f32[2048,512]{1,0:T(8,128)} %fusion.61, f32[2048,512]{1,0:T(8,128)S(1)} %fusion.65, f32[2048,512]{1,0:T(8,128)} %fusion.69, f32[2048,512]{1,0:T(8,128)S(1)} %fusion.73, f32[2048,512]{1,0:T(8,128)} %fusion.81, ...), kind=kOutput, calls=%fused_computation.25 | convolution fusion | flops 1082130432 | bytes 40370176 | tf_op jit(solution)/shard_map/nd,cd->nc/dot_general | solution.py:297
  786.9 20.4 %all-gather.7.cloned.1.call-done = f32[60,128,128]{2,1,0:T(8,128)} async-done(((f32[60,16,128]{2,1,0:T(8,128)}), f32[60,128,128]{2,1,0:T(8,128)}) %all-gather.7.cloned.1.call-update) | async-done | bytes 3932176 | tf_op jit(solution)/shard_map/all_gather | solution.py:343
  826.1 39.4 %all-reduce.2 = f32[192,16]{1,0:T(8,128)S(1)} all-reduce(f32[192,16]{1,0:T(8,128)S(1)} %reshape.700), channel_id=5, replica_groups=mesh['dp'=8,'mp'=4] {'dp','mp'}, use_global_device_ids=true, to_apply=%region_29.30.clone | all-reduce | flops 3072 | bytes 24576
  866.2 7.2 add_add_fusion.3
  873.4 8.2 fusion.35
  888.7 17.7 %scatter_fusion = f32[240,16,128]{2,1,0:T(8,128)S(1)} fusion(f32[240,16,128]{2,1,0:T(8,128)S(1)} %broadcast_in_dim.124, s32[240]{0:T(256)S(1)} %copy-done.97, f32[240,16,128]{2,1,0:T(8,128)} %all-gather.9.cloned.1.call-done), kind=kCustom, calls=%fused_computation.1 | custom fusion | bytes 5899200 | tf_op jit(solution)/shard_map/scatter | solution.py:361
  (442 shorter events, 355.4 us)
Async XLA Ops:
  7.2 94.4 %copy-start = (bf16[2,512,768]{2,1,0:T(8,128)(2,1)S(1)}, bf16[2,512,768]{2,1,0:T(8,128)(2,1)}, u32[]{:S(2)}) copy-start(bf16[2,512,768]{2,1,0:T(8,128)(2,1)} %param.16) | copy-start | bytes 4718596
  7.2 82.5 %all-gather.11.cloned.1.call-start = ((), (), s32[]{:S(2)}) async-start(), calls=%async_computation.4 | async-start | bytes 8110080 | tf_op jit(solution)/shard_map/all_gather | solution.py:156
  9.1 724.4 %reduce-scatter.2.cloned.1.call-start = ((), (), s32[]{:S(2)}) async-start(), calls=%async_computation.1 | async-start | bytes 16220160 | tf_op jit(solution)/shard_map/reduce_scatter | solution.py:340
  57.1 14.3 %copy-start.84 = (f32[512]{0:T(512)}, f32[512]{0:T(512)S(1)}, u32[]{:S(2)}) copy-start(f32[512]{0:T(512)S(1)} %mul.637) | copy-start | bytes 6148
  57.3 14.2 %copy-start.89 = (f32[512]{0:T(512)}, f32[512]{0:T(512)S(1)}, u32[]{:S(2)}) copy-start(f32[512]{0:T(512)S(1)} %add.284) | copy-start | bytes 6148
  58.9 119.4 %copy-start.70 = (f32[2,1024]{1,0:T(2,128)}, f32[2,1024]{1,0:T(2,128)S(1)}, u32[]{:S(2)}) copy-start(f32[2,1024]{1,0:T(2,128)S(1)} %compare_convert_fusion) | copy-start | bytes 24580
  71.4 80.6 %copy-start.98 = (f32[2,256]{1,0:T(2,128)}, f32[2,256]{1,0:T(2,128)S(1)}, u32[]{:S(2)}) copy-start(f32[2,256]{1,0:T(2,128)S(1)} %get-tuple-element.100) | copy-start | bytes 6148
  71.5 80.6 %copy-start.100 = (f32[2,256]{1,0:T(2,128)}, f32[2,256]{1,0:T(2,128)S(1)}, u32[]{:S(2)}) copy-start(f32[2,256]{1,0:T(2,128)S(1)} %get-tuple-element.101) | copy-start | bytes 6148
  104.6 14.7 %copy-start.59 = (bf16[16,128,128]{2,1,0:T(8,128)(2,1)S(1)}, bf16[16,128,128]{2,1,0:T(8,128)(2,1)}, u32[]{:S(2)}) copy-start(bf16[16,128,128]{2,1,0:T(8,128)(2,1)} %get-tuple-element.59) | copy-start | bytes 1572868
  107.6 14.0 %copy-start.57 = (bf16[16,128,128]{2,1,0:T(8,128)(2,1)S(1)}, bf16[16,128,128]{2,1,0:T(8,128)(2,1)}, u32[]{:S(2)}) copy-start(bf16[16,128,128]{2,1,0:T(8,128)(2,1)} %get-tuple-element.61) | copy-start | bytes 1572868
  152.3 14.6 %copy-start.3 = (f32[2,1024,512]{2,1,0:T(8,128)S(1)}, f32[2,1024,512]{2,1,0:T(8,128)}, u32[]{:S(2)}) copy-start(f32[2,1024,512]{2,1,0:T(8,128)} %get-tuple-element.50) | copy-start | bytes 12582916
  152.3 14.6 %copy-start.7 = (f32[2,1024,512]{2,1,0:T(8,128)S(1)}, f32[2,1024,512]{2,1,0:T(8,128)}, u32[]{:S(2)}) copy-start(f32[2,1024,512]{2,1,0:T(8,128)} %param.20) | copy-start | bytes 12582916
  263.0 15.9 %copy-start.25 = (bf16[2,1024,8,64]{1,3,2,0:T(8,128)(2,1)S(1)}, bf16[2,1024,8,64]{1,3,2,0:T(8,128)(2,1)}, u32[]{:S(2)}) copy-start(bf16[2,1024,8,64]{1,3,2,0:T(8,128)(2,1)} %copy.288) | copy-start | bytes 6291460
  263.0 15.9 %copy-start.27 = (bf16[2,512,8,64]{1,0,3,2:T(2,128)(2,1)S(1)}, bf16[2,512,8,64]{1,0,3,2:T(2,128)(2,1)}, u32[]{:S(2)}) copy-start(bf16[2,512,8,64]{1,0,3,2:T(2,128)(2,1)} %reshape.643) | copy-start | bytes 3145732
  404.4 18.6 %copy-start.1 = (bf16[2,1024,512]{2,1,0:T(8,128)(2,1)}, bf16[2,1024,512]{2,1,0:T(8,128)(2,1)S(1)}, u32[]{:S(2)}) copy-start(bf16[2,1024,512]{2,1,0:T(8,128)(2,1)S(1)} %get-tuple-element.40) | copy-start | bytes 6291460
  523.0 17.2 %copy-start.107 = (pred[4,60]{1,0:T(4,128)(4,1)S(1)}, pred[4,60]{1,0:T(4,128)(4,1)}, u32[]{:S(2)}) copy-start(pred[4,60]{1,0:T(4,128)(4,1)} %broadcast_in_dim.120) | copy-start | bytes 724
  564.3 169.3 %copy-start.43 = (bf16[4,4,128,128]{3,1,2,0:T(4,128)(2,1)S(1)}, bf16[4,4,128,128]{3,1,2,0:T(4,128)(2,1)}, u32[]{:S(2)}) copy-start(bf16[4,4,128,128]{3,1,2,0:T(4,128)(2,1)} %copy.271) | copy-start | bytes 1572868
  564.3 242.9 %all-gather.7.cloned.1.call-start = ((), (), s32[]{:S(2)}) async-start(), calls=%async_computation.2 | async-start | bytes 4423680 | tf_op jit(solution)/shard_map/all_gather | solution.py:343
  733.6 155.0 %all-gather.9.cloned.1.call-start = ((), (), s32[]{:S(2)}) async-start(), calls=%async_computation.3 | async-start | bytes 2457600 | tf_op jit(solution)/shard_map/all_gather | solution.py:360
  766.5 13.9 %copy-start.80 = (f32[2,512]{1,0:T(2,128)S(1)}, f32[2,512]{1,0:T(2,128)}, u32[]{:S(2)}) copy-start(f32[2,512]{1,0:T(2,128)} %copy-done.79) | copy-start | bytes 12292
  766.5 13.9 %copy-start.85 = (f32[512]{0:T(512)S(1)}, f32[512]{0:T(512)}, u32[]{:S(2)}) copy-start(f32[512]{0:T(512)} %copy-done.84) | copy-start | bytes 6148
  766.5 14.0 %copy-start.88 = (f32[2,1024]{1,0:T(2,128)S(1)}, f32[2,1024]{1,0:T(2,128)}, u32[]{:S(2)}) copy-start(f32[2,1024]{1,0:T(2,128)} %get-tuple-element.98) | copy-start | bytes 24580
  766.5 14.0 %copy-start.90 = (f32[512]{0:T(512)S(1)}, f32[512]{0:T(512)}, u32[]{:S(2)}) copy-start(f32[512]{0:T(512)} %copy-done.89) | copy-start | bytes 6148
  819.7 45.9 %copy-start.95 = (f32[6,16]{1,0:T(8,128)S(1)}, f32[6,16]{1,0:T(8,128)}, u32[]{:S(2)}) copy-start(f32[6,16]{1,0:T(8,128)} %param.22) | copy-start | bytes 1156
  (88 other events, 459.1 us)
Sparse Core Ops, SparseCore 0:
  11.5 78.0 all-gather.10
  564.4 169.1 reduce-scatter.1
  736.2 71.0 all-gather.6
  819.8 20.5 all-gather.8
where the time goes:
time: 927 us; the launch traced here: 915 us
  matrix products  244 us (26%)
  local copies, waits for them, and re-layouts  233 us (25%)
  waiting for transfers between devices  191 us (21%)
  other arithmetic  149 us (16%)
  blocking collectives  83.3 us (9%)
  between operations  15.1 us (2%)
    reduce_scatter x1, waiting for transfers between devices, body(): lax.psum_scatter(arranged, ('dp', 'mp'), scatter_dimension=0, tiled=True)  166 us
    reshape x26, local copies, waits for them, and re-layouts, rebuild_blocks(): block_matrix.reshape(row_count // BS, BS, col_count // BS, BS)  62.4 us
    all_gather x1, blocking collectives, body(): lax.all_gather(params_low, ('dp', 'mp'), axis=0, tiled=True)  43.9 us
    dot_general x9, matrix products, convolve(): jnp.dot(window, conv_taps[tap_index], preferred_element_type=jnp.float32)  40.9 us
    unnamed x1, blocking collectives  39.4 us
    dot_general x9, matrix products, body(): jnp.einsum('nd,cd->nc', back_window, conv_back[tap_index], preferred_elem...  37.9 us
    convert_element_type x1, other arithmetic, body(): score_grad = (probs_again * (prob_grad - row_delta)).astype(jnp.bfloat16)  28 us
    dot_general x1, matrix products, body(): jnp.einsum('cphd,clhd->chpl', mixed_grad, value_heads, preferred_element_...  24.1 us
  transfers between devices with their start and end apart: 4, of which 3 were waited for; matrix products, arithmetic and copies ran while one was open for 13% of the time, Pallas kernels for 0%

commit v1 on v0

v1 whole, which is shorter than its diff:
```python
import functools
import math

import jax
import jax.numpy as jnp
from jax import lax
from jax.experimental import pallas as pl
from jax.experimental.pallas import tpu as pltpu
from jax.sharding import PartitionSpec as P

LATENT_CHANNELS = 512
GROUPS = 32
HEADS = 8
HEADDIM = 64
CTX = 768
BINS = 8
TSTEPS = 1000
BS = 128
POS = 1024
CH = LATENT_CHANNELS

highest = lax.Precision.HIGHEST
learn_rate = 0.5
out_gain = 8.0
eps = 1e-05

CONV_SCALE = 1.0 / math.sqrt(9 * CH)
INV_WIDTH = 1.0 / math.sqrt(CH)
INV_CTX = 1.0 / math.sqrt(CTX)
OUT_SCALE = out_gain / math.sqrt(CH)
ATT_SCALE = 1.0 / math.sqrt(HEADDIM)

SQ = (CH // BS) * (CH // BS)
KV = (CTX // BS) * (CH // BS)
TEMB0 = 9 * SQ
QUERY0 = TEMB0 + SQ
OUT0 = QUERY0 + SQ
KEY0 = OUT0 + SQ
VALUE0 = KEY0 + KV
NBLK = VALUE0 + KV

F32 = jnp.float32
BF16 = jnp.bfloat16
VMEM_LIMIT = 60 * 1024 * 1024


def nt(a, b):
    return lax.dot_general(a, b, (((1,), (1,)), ((), ())), preferred_element_type=F32)


def nn(a, b):
    return lax.dot_general(a, b, (((1,), (0,)), ((), ())), preferred_element_type=F32)


def mat(ref, base, nr, nc):
    rows = [jnp.concatenate([ref[base + a * nc + b] for b in range(nc)], axis=1) for a in range(nr)]
    return jnp.concatenate(rows, axis=0)


def row_iota(start, count):
    return lax.broadcasted_iota(jnp.int32, (count, 1), 0) + start


def fold8(x):
    return jnp.sum(x.reshape(-1, 8, x.shape[-1]), axis=0)


def group_sums(rows8, gmat):
    total = jnp.broadcast_to(jnp.sum(rows8, axis=0, keepdims=True), (8, CH))
    return lax.dot_general(
        total, gmat, (((1,), (0,)), ((), ())), preferred_element_type=F32, precision=highest
    )[0:1]


def group_matrix():
    i = lax.broadcasted_iota(jnp.int32, (CH, CH), 0) // (CH // GROUPS)
    j = lax.broadcasted_iota(jnp.int32, (CH, CH), 1) // (CH // GROUPS)
    return (i == j).astype(F32)


def shift_bins(tile, step):
    if step == 0:
        return tile
    t = tile.reshape(-1, 8, tile.shape[-1])
    rolled = pltpu.roll(t, (8 - step) % 8, 1)
    b = lax.broadcasted_iota(jnp.int32, (1, 8, 1), 1) + step
    keep = (b >= 0) & (b < 8)
    return jnp.where(keep, rolled, 0.0).reshape(tile.shape)


def write_windows(pad, e_ref, o_ref, sign):
    T = 64

    def body(i, carry):
        r = pl.multiple_of(i * T, T)
        mid = pad[pl.ds(r + 8, T), :]
        low = pad[pl.ds(r, T), :]
        for d in range(3):
            step = sign * (d - 1)
            e_ref[0, d, pl.ds(r, T), :] = shift_bins(mid, step).astype(BF16)
            o_ref[0, d, pl.ds(r, T), :] = shift_bins(low, step).astype(BF16)
        return carry

    lax.fori_loop(0, POS // T, body, 0)
    last = pad[POS : POS + 16, :]
    for d in range(3):
        o_ref[0, d, POS : POS + 16, :] = shift_bins(last, sign * (d - 1)).astype(BF16)


def window(e_ref, o_ref, df, db, r, n, lead=(0,)):
    if df == 1:
        return e_ref[lead + (db, pl.ds(r, n), slice(None))]
    off = 0 if df == 0 else 16
    return o_ref[lead + (db, pl.ds(pl.multiple_of(r + off, 16), n), slice(None))]


def pre_kernel(frames_s, trig_s, clean, noise, cot, inp, outlow, stats, obias):
    c = pl.program_id(0)
    rows = frames_s[c] * BINS
    cs, sn = trig_s[0, c], trig_s[1, c]
    T = 64
    zero = jnp.zeros((8, CH), F32)
    gmat = group_matrix()
    inv_n = 1.0 / (rows * (CH // GROUPS)).astype(F32)

    def first(i, carry):
        s0, s1 = carry
        r = pl.multiple_of(i * T, T)
        m = row_iota(r, T) < rows
        x = jnp.where(m, cs * clean[0, pl.ds(r, T), :] + sn * noise[0, pl.ds(r, T), :], 0.0)
        inp[0, pl.ds(r, T), :] = x
        g = jnp.where(m, cot[0, pl.ds(r, T), :], 0.0)
        outlow[0, pl.ds(r, T), :] = g.astype(BF16)
        return (s0 + fold8(x), s1 + fold8(g))

    s0, s1 = lax.fori_loop(0, POS // T, first, (zero, zero))
    mean = group_sums(s0, gmat) * inv_n

    def second(i, s):
        r = pl.multiple_of(i * T, T)
        m = row_iota(r, T) < rows
        d = jnp.where(m, inp[0, pl.ds(r, T), :] - mean, 0.0)
        return s + fold8(d * d)

    s2 = lax.fori_loop(0, POS // T, second, zero)
    rstd = lax.rsqrt(group_sums(s2, gmat) * inv_n + eps)
    stats[0] = jnp.concatenate([mean, rstd, jnp.zeros((6, CH), F32)], axis=0)
    obias[0] = s1


def pre(frames, trig, clean, noise, cot):
    n = clean.shape[0]
    big = pl.BlockSpec((1, POS, CH), lambda c, *_: (c, 0, 0))
    small = pl.BlockSpec((1, 8, CH), lambda c, *_: (c, 0, 0))
    return pl.pallas_call(
        pre_kernel,
        out_shape=(
            jax.ShapeDtypeStruct((n, POS, CH), F32),
            jax.ShapeDtypeStruct((n, POS, CH), BF16),
            jax.ShapeDtypeStruct((n, 8, CH), F32),
            jax.ShapeDtypeStruct((n, 8, CH), F32),
        ),
        grid_spec=pltpu.PrefetchScalarGridSpec(
            num_scalar_prefetch=2, grid=(n,), in_specs=[big, big, big], out_specs=[big, big, small, small]
        ),
        compiler_params=pltpu.CompilerParams(vmem_limit_bytes=VMEM_LIMIT),
        cost_estimate=pl.CostEstimate(flops=n * POS * CH * 20, bytes_accessed=n * POS * CH * 18, transcendentals=0),
        name="inputs_stats",
    )(frames, trig, clean, noise, cot)


def acts_kernel(frames_s, inp, stats, params, e_ref, o_ref, pad):
    c = pl.program_id(0)
    rows = frames_s[c] * BINS
    T = 64
    mean, rstd = stats[0, 0:1], stats[0, 1:2]
    scale = rstd * params[0:1]
    shift = params[1:2]
    pad[0:8, :] = jnp.zeros((8, CH), F32)
    pad[8 + POS :, :] = jnp.zeros((8, CH), F32)

    def body(i, carry):
        r = pl.multiple_of(i * T, T)
        m = row_iota(r, T) < rows
        y = (inp[0, pl.ds(r, T), :] - mean) * scale + shift
        a = jnp.where(m, y * jax.nn.sigmoid(y), 0.0)
        pad[pl.ds(r + 8, T), :] = a
        return carry

    lax.fori_loop(0, POS // T, body, 0)
    write_windows(pad, e_ref, o_ref, 1)


def acts_windows(frames, inp, stats, params):
    n = inp.shape[0]
    return pl.pallas_call(
        acts_kernel,
        out_shape=(
            jax.ShapeDtypeStruct((n, 3, POS, CH), BF16),
            jax.ShapeDtypeStruct((n, 3, POS + 16, CH), BF16),
        ),
        grid_spec=pltpu.PrefetchScalarGridSpec(
            num_scalar_prefetch=1,
            grid=(n,),
            in_specs=[
                pl.BlockSpec((1, POS, CH), lambda c, *_: (c, 0, 0)),
                pl.BlockSpec((1, 8, CH), lambda c, *_: (c, 0, 0)),
                pl.BlockSpec((8, CH), lambda c, *_: (0, 0)),
            ],
            out_specs=[
                pl.BlockSpec((1, 3, POS, CH), lambda c, *_: (c, 0, 0, 0)),
                pl.BlockSpec((1, 3, POS + 16, CH), lambda c, *_: (c, 0, 0, 0)),
            ],
            scratch_shapes=[pltpu.VMEM((POS + 16, CH), F32)],
        ),
        compiler_params=pltpu.CompilerParams(vmem_limit_bytes=VMEM_LIMIT),
        cost_estimate=pl.CostEstimate(
            flops=n * POS * CH * 30, bytes_accessed=n * POS * CH * 16, transcendentals=n * POS * CH
        ),
        name="acts",
    )(frames, inp, stats, params)


def conv_kernel(frames_s, e_ref, o_ref, inp, emb, params, w, res, normed, stats):
    c = pl.program_id(0)
    rows = frames_s[c] * BINS
    R = 256
    T = 64
    zero = jnp.zeros((8, CH), F32)
    gmat = group_matrix()
    inv_n = 1.0 / (rows * (CH // GROUPS)).astype(F32)
    temb = nn(emb[0], mat(w, TEMB0, 4, 4))[0:1] * INV_WIDTH
    add = temb + params[2:3]

    def tile(i, s):
        r = pl.multiple_of(i * R, R)
        acc = jnp.zeros((R, CH), F32)
        for t in range(9):
            df, db = divmod(t, 3)
            acc = acc + nn(window(e_ref, o_ref, df, db, r, R), mat(w, t * SQ, 4, 4))
        v = inp[0, pl.ds(r, R), :] + acc * CONV_SCALE + add
        res[0, pl.ds(r, R), :] = v
        return s + fold8(jnp.where(row_iota(r, R) < rows, v, 0.0))

    s = lax.fori_loop(0, POS // R, tile, zero)
    mean = group_sums(s, gmat) * inv_n

    def second(i, s):
        r = pl.multiple_of(i * T, T)
        d = jnp.where(row_iota(r, T) < rows, res[0, pl.ds(r, T), :] - mean, 0.0)
        return s + fold8(d * d)

    s2 = lax.fori_loop(0, POS // T, second, zero)
    rstd = lax.rsqrt(group_sums(s2, gmat) * inv_n + eps)
    scale = rstd * params[3:4]
    shift = params[4:5]

    def third(i, carry):
        r = pl.multiple_of(i * T, T)
        normed[0, pl.ds(r, T), :] = ((res[0, pl.ds(r, T), :] - mean) * scale + shift).astype(BF16)
        return carry

    lax.fori_loop(0, POS // T, third, 0)
    stats[0] = jnp.concatenate([mean, rstd, jnp.zeros((6, CH), F32)], axis=0)


def whole(shape):
    return pl.BlockSpec(shape, lambda *_: (0,) * len(shape), pipeline_mode=pl.Buffered(1))


def per_clip(shape):
    return pl.BlockSpec((1,) + shape, lambda c, *_: (c,) + (0,) * len(shape))


def conv_forward(frames, e, o, inp, emb, params, w):
    n = inp.shape[0]
    return pl.pallas_call(
        conv_kernel,
        out_shape=(
            jax.ShapeDtypeStruct((n, POS, CH), F32),
            jax.ShapeDtypeStruct((n, POS, CH), BF16),
            jax.ShapeDtypeStruct((n, 8, CH), F32),
        ),
        grid_spec=pltpu.PrefetchScalarGridSpec(
            num_scalar_prefetch=1,
            grid=(n,),
            in_specs=[
                per_clip((3, POS, CH)),
                per_clip((3, POS + 16, CH)),
                per_clip((POS, CH)),
                per_clip((16, CH)),
                whole((8, CH)),
                pl.BlockSpec((QUERY0, BS, BS), lambda *_: (0, 0, 0), pipeline_mode=pl.Buffered(1)),
            ],
            out_specs=[per_clip((POS, CH)), per_clip((POS, CH)), per_clip((8, CH))],
        ),
        compiler_params=pltpu.CompilerParams(vmem_limit_bytes=VMEM_LIMIT),
        cost_estimate=pl.CostEstimate(
            flops=n * POS * CH * CH * 18, bytes_accessed=n * POS * CH * 22 + 5000000, transcendentals=0
        ),
        name="conv_forward",
    )(frames, e, o, inp, emb, params, w)


def attn_kernel(
    frames_s, normed, tokens, tok_t, kmask, outlow, res, params, w,
    block_out, dq_ref, dw_ref,
    q_s, do_s, kv_s, qt_s, dot_s, mixed_s, dkt_s, dvt_s, dkv_acc,
):
    c = pl.program_id(0)
    rows = frames_s[c] * BINS
    R = 256
    query_w = mat(w, 0, 4, 4)
    out_w = mat(w, SQ, 4, 4)
    key_w = mat(w, 2 * SQ, CTX // BS, 4)
    value_w = mat(w, 2 * SQ + KV, CTX // BS, 4)

    def project(i, carry):
        r = pl.multiple_of(i * R, R)
        q = (nn(normed[0, pl.ds(r, R), :], query_w) * INV_WIDTH).astype(BF16)
        q_s[pl.ds(r, R), :] = q
        qt_s[:, pl.ds(r, R)] = q.T
        d = (nt(outlow[0, pl.ds(r, R), :], out_w) * OUT_SCALE).astype(BF16)
        do_s[pl.ds(r, R), :] = d
        dot_s[:, pl.ds(r, R)] = d.T
        return carry

    lax.fori_loop(0, POS // R, project, 0)
    kv_s[0] = ((nn(tokens[0], key_w) * INV_CTX).astype(BF16).astype(F32) * ATT_SCALE).astype(BF16)
    kv_s[1] = (nn(tokens[0], value_w) * INV_CTX).astype(BF16)
    valid = kmask[0, 0:1, :] > 0.0
    lane = lax.broadcasted_iota(jnp.int32, (1, BS), 1)
    first = lane < HEADDIM

    for slab in range(HEADS // 2):
        cols = slice(slab * BS, (slab + 1) * BS)
        k2, v2 = kv_s[0, :, cols], kv_s[1, :, cols]
        none = jnp.zeros_like(k2)
        ks = (jnp.where(first, k2, none), jnp.where(first, none, k2))
        vs = (jnp.where(first, v2, none), jnp.where(first, none, v2))
        dkv_acc[...] = jnp.zeros_like(dkv_acc)

        def tile(i, carry):
            r = pl.multiple_of(i * R, R)
            q = q_s[pl.ds(r, R), cols]
            d = do_s[pl.ds(r, R), cols]
            o = jnp.zeros((R, BS), F32)
            dq = jnp.zeros((R, BS), F32)
            for h in range(2):
                s = jnp.where(valid, nt(q, ks[h]), -1000000000.0)
                e = jnp.exp(s - jnp.max(s, axis=-1, keepdims=True))
                p = e * (1.0 / jnp.sum(e, axis=-1, keepdims=True))
                pb = p.astype(BF16)
                dp = nt(d, vs[h])
                delta = jnp.sum(p * dp, axis=-1, keepdims=True)
                ds = (p * (dp - delta)).astype(BF16)
                o = o + nn(pb, vs[h])
                dq = dq + nn(ds, ks[h])
                half = slice(slab * BS + h * HEADDIM, slab * BS + (h + 1) * HEADDIM)
                mine = slice(h * HEADDIM, (h + 1) * HEADDIM)
                dkv_acc[0, mine, :] += nn(qt_s[half, pl.ds(r, R)], ds)
                dkv_acc[1, mine, :] += nn(dot_s[half, pl.ds(r, R)], pb)
            mixed_s[pl.ds(r, R), cols] = o.astype(BF16)
            dq_ref[0, pl.ds(r, R), cols] = dq.astype(BF16)
            return carry

        lax.fori_loop(0, POS // R, tile, 0)
        dkt_s[cols, :] = (dkv_acc[0] * ATT_SCALE).astype(BF16)
        dvt_s[cols, :] = dkv_acc[1].astype(BF16)

    def project_out(i, carry):
        r = pl.multiple_of(i * R, R)
        proj = nn(mixed_s[pl.ds(r, R), :], out_w) * OUT_SCALE + params[5:6]
        m = row_iota(r, R) < rows
        block_out[0, pl.ds(r, R), :] = jnp.where(m, res[0, pl.ds(r, R), :] + proj, 0.0)
        return carry

    lax.fori_loop(0, POS // R, project_out, 0)

    @pl.when(c == 0)
    def _():
        dw_ref[...] = jnp.zeros_like(dw_ref)

    dw_ref[0:CH, :] += nn(normed[0].T, dq_ref[0])
    dw_ref[CH : 2 * CH, :] += nn(mixed_s[...].T, outlow[0])
    dw_ref[2 * CH : 2 * CH + CTX, :] += nt(tok_t[0], dkt_s[...])
    dw_ref[2 * CH + CTX :, :] += nt(tok_t[0], dvt_s[...])


def attention(frames, normed, tokens, tok_t, kmask, outlow, res, params, w):
    n = normed.shape[0]
    ctx_len = tokens.shape[1]
    amount = 2 * SQ + 2 * KV
    return pl.pallas_call(
        attn_kernel,
        out_shape=(
            jax.ShapeDtypeStruct((n, POS, CH), F32),
            jax.ShapeDtypeStruct((n, POS, CH), BF16),
            jax.ShapeDtypeStruct((2 * CH + 2 * CTX, CH), F32),
        ),
        grid_spec=pltpu.PrefetchScalarGridSpec(
            num_scalar_prefetch=1,
            grid=(n,),
            in_specs=[
                per_clip((POS, CH)),
                per_clip((ctx_len, CTX)),
                per_clip((CTX, ctx_len)),
                per_clip((8, ctx_len)),
                per_clip((POS, CH)),
                per_clip((POS, CH)),
                whole((8, CH)),
                whole((amount, BS, BS)),
            ],
            out_specs=[
                per_clip((POS, CH)),
                per_clip((POS, CH)),
                pl.BlockSpec((2 * CH + 2 * CTX, CH), lambda *_: (0, 0)),
            ],
            scratch_shapes=[
                pltpu.VMEM((POS, CH), BF16),
                pltpu.VMEM((POS, CH), BF16),
                pltpu.VMEM((2, ctx_len, CH), BF16),
                pltpu.VMEM((CH, POS), BF16),
                pltpu.VMEM((CH, POS), BF16),
                pltpu.VMEM((POS, CH), BF16),
                pltpu.VMEM((CH, ctx_len), BF16),
                pltpu.VMEM((CH, ctx_len), BF16),
                pltpu.VMEM((2, BS, ctx_len), F32),
            ],
        ),
        compiler_params=pltpu.CompilerParams(vmem_limit_bytes=VMEM_LIMIT),
        cost_estimate=pl.CostEstimate(
            flops=n * POS * CH * (6 * CH * 2 + 24 * ctx_len),
            bytes_accessed=n * POS * CH * 16,
            transcendentals=n * POS * HEADS * ctx_len,
        ),
        name="attention",
    )(frames, normed, tokens, tok_t, kmask, outlow, res, params, w)


def norm2_kernel(frames_s, dq_ref, res, stats, cot, params, w, rgrad, e_ref, o_ref, sums, ng_s, pad):
    c = pl.program_id(0)
    rows = frames_s[c] * BINS
    R = 256
    T = 64
    zero = jnp.zeros((8, CH), F32)
    gmat = group_matrix()
    inv_n = 1.0 / (rows * (CH // GROUPS)).astype(F32)
    mean, rstd = stats[0, 0:1], stats[0, 1:2]
    gain = params[3:4]
    query_w = mat(w, 0, 4, 4)

    def first(i, carry):
        s0, s1 = carry
        r = pl.multiple_of(i * R, R)
        ng = nt(dq_ref[0, pl.ds(r, R), :], query_w) * INV_WIDTH
        m = row_iota(r, R) < rows
        ng = jnp.where(m, ng, 0.0)
        ng_s[pl.ds(r, R), :] = ng
        x = jnp.where(m, (res[0, pl.ds(r, R), :] - mean) * rstd, 0.0)
        return (s0 + fold8(ng), s1 + fold8(ng * x))

    s0, s1 = lax.fori_loop(0, POS // R, first, (zero, zero))
    mh = group_sums(s0 * gain, gmat) * inv_n
    mhx = group_sums(s1 * gain, gmat) * inv_n
    pad[0:8, :] = zero
    pad[8 + POS :, :] = zero

    def second(i, s):
        r = pl.multiple_of(i * T, T)
        m = row_iota(r, T) < rows
        x = (res[0, pl.ds(r, T), :] - mean) * rstd
        d = rstd * (gain * ng_s[pl.ds(r, T), :] - mh - x * mhx)
        g = jnp.where(m, cot[0, pl.ds(r, T), :] + d, 0.0)
        rgrad[0, pl.ds(r, T), :] = g
        pad[pl.ds(r + 8, T), :] = g
        return s + fold8(g)

    s2 = lax.fori_loop(0, POS // T, second, zero)
    sums[0, 0:8] = s2
    sums[0, 8:16] = s1
    sums[0, 16:24] = s0
    write_windows(pad, e_ref, o_ref, -1)


def norm2_backward(frames, dq, res, stats, cot, params, w):
    n = dq.shape[0]
    return pl.pallas_call(
        norm2_kernel,
        out_shape=(
            jax.ShapeDtypeStruct((n, POS, CH), F32),
            jax.ShapeDtypeStruct((n, 3, POS, CH), BF16),
            jax.ShapeDtypeStruct((n, 3, POS + 16, CH), BF16),
            jax.ShapeDtypeStruct((n, 24, CH), F32),
        ),
        grid_spec=pltpu.PrefetchScalarGridSpec(
            num_scalar_prefetch=1,
            grid=(n,),
            in_specs=[
                per_clip((POS, CH)),
                per_clip((POS, CH)),
                per_clip((8, CH)),
                per_clip((POS, CH)),
                whole((8, CH)),
                whole((SQ, BS, BS)),
            ],
            out_specs=[
                per_clip((POS, CH)),
                per_clip((3, POS, CH)),
                per_clip((3, POS + 16, CH)),
                per_clip((24, CH)),
            ],
            scratch_shapes=[pltpu.VMEM((POS, CH), F32), pltpu.VMEM((POS + 16, CH), F32)],
        ),
        compiler_params=pltpu.CompilerParams(vmem_limit_bytes=VMEM_LIMIT),
        cost_estimate=pl.CostEstimate(
            flops=n * POS * CH * CH * 2, bytes_accessed=n * POS * CH * 26, transcendentals=0
        ),
        name="norm2_backward",
    )(frames, dq, res, stats, cot, params, w)


def tap_kernel(at, e_ref, o_ref, out):
    n = e_ref.shape[0]
    for df in range(3):
        acc = None
        for c in range(n):
            g = window(e_ref, o_ref, 2 - df, 0, 0, POS, (c,))
            part = nn(at[:, c * POS : (c + 1) * POS], g)
            acc = part if acc is None else acc + part
        acc = (acc * CONV_SCALE).astype(BF16)
        for a in range(4):
            for b in range(4):
                out[df, 0, a * 4 + b] = acc[a * BS : (a + 1) * BS, b * BS : (b + 1) * BS]


def tap_gradients(at, e, o):
    n = e.shape[0]
    return pl.pallas_call(
        tap_kernel,
        out_shape=jax.ShapeDtypeStruct((3, 3, SQ, BS, BS), BF16),
        grid_spec=pltpu.PrefetchScalarGridSpec(
            num_scalar_prefetch=0,
            grid=(3,),
            in_specs=[
                whole((CH, n * POS)),
                pl.BlockSpec((n, 1, POS, CH), lambda d: (0, d, 0, 0)),
                pl.BlockSpec((n, 1, POS + 16, CH), lambda d: (0, d, 0, 0)),
            ],
            out_specs=pl.BlockSpec((3, 1, SQ, BS, BS), lambda d: (0, d, 0, 0, 0)),
        ),
        compiler_params=pltpu.CompilerParams(vmem_limit_bytes=VMEM_LIMIT),
        cost_estimate=pl.CostEstimate(
            flops=n * POS * CH * CH * 18, bytes_accessed=n * POS * CH * 14 + 5000000, transcendentals=0
        ),
        name="tap_gradients",
    )(at, e, o)


def input_kernel(frames_s, e_ref, o_ref, inp, stats, rgrad, params, w, out, sums, ag_s):
    c = pl.program_id(0)
    rows = frames_s[c] * BINS
    R = 256
    T = 64
    zero = jnp.zeros((8, CH), F32)
    gmat = group_matrix()
    inv_n = 1.0 / (rows * (CH // GROUPS)).astype(F32)
    mean, rstd = stats[0, 0:1], stats[0, 1:2]
    gain, shift = params[0:1], params[1:2]

    def conv(i, carry):
        r = pl.multiple_of(i * R, R)
        acc = jnp.zeros((R, CH), F32)
        for t in range(9):
            df, db = divmod(t, 3)
            acc = acc + nt(window(e_ref, o_ref, 2 - df, db, r, R), mat(w, t * SQ, 4, 4))
        ag_s[pl.ds(r, R), :] = acc * CONV_SCALE
        return carry

    lax.fori_loop(0, POS // R, conv, 0)

    def first(i, carry):
        s0, s1 = carry
        r = pl.multiple_of(i * T, T)
        m = row_iota(r, T) < rows
        x = (inp[0, pl.ds(r, T), :] - mean) * rstd
        y = x * gain + shift
        sg = jax.nn.sigmoid(y)
        dy = jnp.where(m, ag_s[pl.ds(r, T), :] * (sg * (1.0 + y * (1.0 - sg))), 0.0)
        ag_s[pl.ds(r, T), :] = dy
        return (s0 + fold8(dy), s1 + fold8(dy * x))

    s0, s1 = lax.fori_loop(0, POS // T, first, (zero, zero))
    mh = group_sums(s0 * gain, gmat) * inv_n
    mhx = group_sums(s1 * gain, gmat) * inv_n

    def second(i, carry):
        r = pl.multiple_of(i * T, T)
        m = row_iota(r, T) < rows
        x = (inp[0, pl.ds(r, T), :] - mean) * rstd
        d = rstd * (gain * ag_s[pl.ds(r, T), :] - mh - x * mhx)
        out[0, pl.ds(r, T), :] = jnp.where(m, rgrad[0, pl.ds(r, T), :] + d, 0.0)
        return carry

    lax.fori_loop(0, POS // T, second, 0)
    sums[0, 0:8] = s1
    sums[0, 8:16] = s0


def input_backward(frames, e, o, inp, stats, rgrad, params, w):
    n = inp.shape[0]
    return pl.pallas_call(
        input_kernel,
        out_shape=(
            jax.ShapeDtypeStruct((n, POS, CH), F32),
            jax.ShapeDtypeStruct((n, 16, CH), F32),
        ),
        grid_spec=pltpu.PrefetchScalarGridSpec(
            num_scalar_prefetch=1,
            grid=(n,),
            in_specs=[
                per_clip((3, POS, CH)),
                per_clip((3, POS + 16, CH)),
                per_clip((POS, CH)),
                per_clip((8, CH)),
                per_clip((POS, CH)),
                whole((8, CH)),
                pl.BlockSpec((TEMB0, BS, BS), lambda *_: (0, 0, 0), pipeline_mode=pl.Buffered(1)),
            ],
            out_specs=[per_clip((POS, CH)), per_clip((16, CH))],
            scratch_shapes=[pltpu.VMEM((POS, CH), F32)],
        ),
        compiler_params=pltpu.CompilerParams(vmem_limit_bytes=VMEM_LIMIT),
        cost_estimate=pl.CostEstimate(
            flops=n * POS * CH * CH * 18, bytes_accessed=n * POS * CH * 24, transcendentals=n * POS * CH
        ),
        name="input_backward",
    )(frames, e, o, inp, stats, rgrad, params, w)


def to_blocks(matrix):
    r, k = matrix.shape
    return matrix.reshape(r // BS, BS, k // BS, BS).transpose(0, 2, 1, 3).reshape(-1, BS, BS)


def sinusoid(timesteps):
    half_width = CH // 2
    freqs = jnp.exp(-math.log(10000.0) * jnp.arange(half_width, dtype=F32) / half_width)
    angles = timesteps.astype(F32)[:, None] * freqs[None, :]
    return jnp.concatenate([jnp.sin(angles), jnp.cos(angles)], axis=-1)


def body(
    clean_latent, noise_latent, codec_tokens, codec_mask, frames, timesteps, out_cotangent,
    master_blocks, norm_params, owned_block, left_stats, right_stats, left_root, right_root,
):
    n_data = lax.axis_size("dp")
    n_model = lax.axis_size("mp")
    total_devices = n_data * n_model
    clip_count = clean_latent.shape[0]
    ctx_len = codec_tokens.shape[1]
    slot_count, row_share = (master_blocks.shape[0], master_blocks.shape[1])
    master_low = master_blocks.astype(BF16)[None]
    params_low = norm_params.astype(BF16)[None]
    gathered = lax.all_gather(master_low, ("dp", "mp"), axis=0, tiled=True)
    gathered_params = lax.all_gather(params_low, ("dp", "mp"), axis=0, tiled=True)
    params = gathered_params.transpose(1, 0, 2).reshape(gathered_params.shape[1], -1).astype(F32)
    params = jnp.pad(params, ((0, 2), (0, 0)))
    blocks = (
        gathered.reshape(n_data, n_model, slot_count, row_share, BS)
        .transpose(1, 2, 0, 3, 4)
        .reshape(n_model * slot_count, BS, BS)
    )

    phases = timesteps.astype(F32) * (0.5 * math.pi / TSTEPS)
    trig = jnp.stack([jnp.cos(phases), jnp.sin(phases)])
    embedding = jax.nn.silu(sinusoid(timesteps)).astype(BF16)
    emb_rows = jnp.broadcast_to(embedding[:, None, :], (clip_count, 16, CH))
    kmask = jnp.broadcast_to(codec_mask.astype(F32)[:, None, :], (clip_count, 8, ctx_len))
    tok_t = codec_tokens.transpose(0, 2, 1)

    inp, outlow, stats1, obias = pre(frames, trig, clean_latent, noise_latent, out_cotangent)
    e1, o1 = acts_windows(frames, inp, stats1, params)
    at = e1[:, 1].reshape(-1, CH).T
    res, normed, stats2 = conv_forward(frames, e1, o1, inp, emb_rows, params, blocks)
    block_output, dq, dw_att = attention(
        frames, normed, codec_tokens, tok_t, kmask, outlow, res, params, blocks[QUERY0:]
    )
    rgrad, e2, o2, sums2 = norm2_backward(frames, dq, res, stats2, out_cotangent, params, blocks[QUERY0:OUT0])
    dtaps = tap_gradients(at, e2, o2)
    input_grad, sums1 = input_backward(frames, e2, o2, inp, stats1, rgrad, params, blocks)

    clip_sums = jnp.sum(sums2[:, 0:8], axis=1)
    temb_grad = clip_sums.astype(BF16)
    dtemb = jnp.einsum("nc,nd->cd", embedding, temb_grad, preferred_element_type=F32) * INV_WIDTH
    att_scales = jnp.concatenate(
        [jnp.full((CH, 1), INV_WIDTH), jnp.full((CH, 1), OUT_SCALE), jnp.full((2 * CTX, 1), INV_CTX)]
    ).astype(F32)
    dw_att = (dw_att * att_scales).astype(BF16)
    local_blocks = jnp.concatenate(
        [
            dtaps.reshape(TEMB0, BS, BS),
            to_blocks(dtemb.astype(BF16)),
            to_blocks(dw_att),
        ],
        axis=0,
    )
    param_grads = jnp.stack(
        [
            jnp.sum(sums1[:, 0:8], axis=(0, 1)),
            jnp.sum(sums1[:, 8:16], axis=(0, 1)),
            jnp.sum(clip_sums, axis=0),
            jnp.sum(sums2[:, 8:16], axis=(0, 1)),
            jnp.sum(sums2[:, 16:24], axis=(0, 1)),
            jnp.sum(obias, axis=(0, 1)),
        ]
    )
    permuted = jnp.take(local_blocks, owned_block, axis=0)
    arranged = (
        permuted.reshape(n_model, slot_count, n_data, row_share, BS)
        .transpose(2, 0, 1, 3, 4)
        .reshape(-1, row_share, BS)
    )
    param_rows = param_grads.shape[0]
    param_arranged = (
        param_grads.reshape(param_rows, total_devices, -1)
        .transpose(1, 0, 2)
        .reshape(total_devices * param_rows, -1)
    )
    owned_low = lax.psum_scatter(arranged, ("dp", "mp"), scatter_dimension=0, tiled=True)
    norm_grads = lax.psum_scatter(param_arranged, ("dp", "mp"), scatter_dimension=0, tiled=True)
    owned_rows = owned_low.astype(F32)
    full_grad = lax.all_gather(owned_low, "dp", axis=1, tiled=True).astype(F32)
    row_start = lax.axis_index("dp") * row_share
    my_columns = lax.dynamic_slice_in_dim(full_grad, row_start, row_share, 2)
    new_left = 0.5 * left_stats + 0.5 * jnp.einsum("srk,stk->srt", owned_rows, full_grad)
    new_right = 0.5 * right_stats + 0.5 * jnp.einsum("skr,skt->srt", my_columns, full_grad)
    left_side = jnp.einsum("srk,skt->srt", left_root, full_grad)
    update = jnp.einsum("srk,skt->srt", left_side, right_root)
    update_step = (
        learn_rate * update * lax.rsqrt(jnp.mean(update * update, axis=(1, 2), keepdims=True) + 1e-06)
    )
    step_rows = lax.dynamic_slice_in_dim(update_step, row_start, row_share, 1)
    all_steps = lax.all_gather(step_rows, "mp", axis=0, tiled=True)
    natural = jnp.zeros_like(all_steps).at[owned_block].set(all_steps)
    my_steps = lax.dynamic_slice_in_dim(natural, lax.axis_index("mp") * slot_count, slot_count, 0)
    new_master = master_blocks - my_steps
    small_rate = 0.5 / math.sqrt(clip_count * total_devices * POS)
    new_norm = norm_params - small_rate * norm_grads
    return (
        block_output, input_grad, owned_rows, new_left, new_right, new_master,
        new_master.astype(BF16), norm_grads, new_norm,
    )


def solution(mesh):
    cells = P(("dp", "mp"), None, None)
    rows = P("mp", "dp", None)
    in_specs = (
        cells, cells, cells, P(("dp", "mp"), None), P(("dp", "mp")), P(("dp", "mp")), cells,
        rows, P(None, ("dp", "mp")), P(), rows, rows, P("mp", None, None), P("mp", None, None),
    )
    out_specs = (
        cells, cells, rows, rows, rows, rows, rows, P(None, ("dp", "mp")), P(None, ("dp", "mp")),
    )
    return jax.shard_map(body, mesh=mesh, in_specs=in_specs, out_specs=out_specs, check_vma=False)
```

time: 927 us -> 542 us (0.58); the launches traced: 915 us -> 541 us
  matrix products: 244 us -> 12.8 us
  local copies, waits for them, and re-layouts: 233 us -> 56.4 us
  Pallas kernels: 0 us -> 167 us
  other arithmetic: 149 us -> 28 us
  waiting for transfers between devices: 191 us -> 179 us
    dot_general x47 -> x4, matrix products: 244 us -> 12.8 us  [the longest x1 7.08 us: body(): update = jnp.einsum('srk,skt->srt', left_side, right_root)]
    pallas_call x0 -> x7, Pallas kernels: none -> 167 us  [the longest x1 68.7 us: attention(): pl.pallas_call(attn_kernel, out_shape=(jax.ShapeDtypeStruct((n, POS, CH),...]
    reshape x48 -> x3, local copies, waits for them, and re-layouts: 118 us -> 9.23 us  [the longest x1 5.51 us: body(): gathered.reshape(n_data, n_model, slot_count, row_share, BS)]
    reduce_sum x17 -> x3, other arithmetic: 64.5 us -> 1.7 us  [the longest x1 0.85 us: body(): jnp.sum(sums1[:, 8:16], axis=(0, 1))]
    reduce_scatter x1, waiting for transfers between devices: 166 us -> 121 us  [body(): lax.psum_scatter(arranged, ('dp', 'mp'), scatter_dimension=0, tiled=True)]
    all_gather x2, waiting for transfers between devices: 24.9 us -> 57.7 us  [the longest x1 50.9 us: body(): full_grad = lax.all_gather(owned_low, 'dp', axis=1, tiled=True).astype(F32)]
    convert_element_type x9 -> x7, other arithmetic: 36.1 us -> 7.76 us  [the longest x1 2.89 us: body(): dw_att = (dw_att * att_scales).astype(BF16)]
    mul x6 -> x0, other arithmetic: 24.8 us -> none  [the longest x4 24 us: cell_window(): return lax.slice_in_dim(padded, start, start + POS, axis=1) * mask]
  transfers between devices with their start and end apart: 4 -> 4, of which waited for: 3 -> 3; matrix products, arithmetic and copies ran while one was open for 13% -> 4% of each run, Pallas kernels for 0% -> 8%
where the time goes in v1:
time: 542 us; the launch traced here: 541 us
  waiting for transfers between devices  179 us (33%)
  Pallas kernels  167 us (31%)
  blocking collectives  82.8 us (15%)
  local copies, waits for them, and re-layouts  56.4 us (10%)
  other arithmetic  28 us (5%)
  between operations  14.1 us (3%)
  matrix products  12.8 us (2%)
    reduce_scatter x1, waiting for transfers between devices, body(): lax.psum_scatter(arranged, ('dp', 'mp'), scatter_dimension=0, tiled=True)  121 us
    pallas_call x1, Pallas kernels, attention(): pl.pallas_call(attn_kernel, out_shape=(jax.ShapeDtypeStruct((n, POS, CH),...  68.7 us
    all_gather x1, waiting for transfers between devices, body(): full_grad = lax.all_gather(owned_low, 'dp', axis=1, tiled=True).astype(F32)  50.9 us
    all_gather x1, blocking collectives, body(): lax.all_gather(params_low, ('dp', 'mp'), axis=0, tiled=True)  43.8 us
    unnamed x1, blocking collectives  39 us
    pallas_call x1, Pallas kernels, input_backward(): pl.pallas_call(input_kernel, out_shape=(jax.ShapeDtypeStruct((n, POS, CH)...  26.2 us
    pallas_call x1, Pallas kernels, conv_forward(): pl.pallas_call(conv_kernel, out_shape=(jax.ShapeDtypeStruct((n, POS, CH),...  23.7 us
    scatter x1, local copies, waits for them, and re-layouts, body(): natural = jnp.zeros_like(all_steps).at[owned_block].set(all_steps)  17.7 us
  transfers between devices with their start and end apart: 4, of which 3 were waited for; matrix products, arithmetic and copies ran while one was open for 4% of the time, Pallas kernels for 8%

profile of v1, /device:TPU:0, one launch (start us, length us, event | category | flops | bytes accessed | tf_op | source)
XLA Modules:
  0.0 540.5 jit_solution(9727133191586707881)
XLA Ops:
  11.9 43.8 %all-gather.2 = bf16[32,6,16]{2,1,0:T(8,128)(2,1)S(1)} all-gather(bf16[1,6,16]{2,1,0:T(8,128)(2,1)S(1)} %convert_bitcast_fusion), channel_id=2, replica_groups=mesh['dp'=8,'mp'=4] {'dp','mp'}, dimensions={0}, use_global_device_ids=true | all-gather | bytes 6336 | tf_op jit(solution)/shard_map/all_gather | solution.py:666
  55.8 2.6 copy.42
  59.1 10.3 %inputs_stats.1 = (f32[2,1024,512]{2,1,0:T(8,128)}, bf16[2,1024,512]{2,1,0:T(8,128)(2,1)}, f32[2,8,512]{2,1,0:T(8,128)}, f32[2,8,512]{2,1,0:T(8,128)}) custom-call(s32[2]{0:T(128)} %frames_s.11, f32[2,2]{1,0:T(2,128)} %pad_maximum_fusion.2.trig_s, f32[2,1024,512]{2,1,0:T(8,128)} %clean.1, f32[2,1024,512]{2,1,0:T(8,128)} %noise.1, f32[2,1024,512]{2,1,0:T(8,128)} %cot.3), custom_call_target="tpu_custom_call" | custom-call | flops 20971520 | bytes 18874368 | tf_op jit(solution)/shard_map/inputs_stats/pallas_call | solution.py:155
  69.9 8.4 %acts.1 = (bf16[2,3,1024,512]{3,2,1,0:T(8,128)(2,1)}, bf16[2,3,1040,512]{3,2,1,0:T(8,128)(2,1)}) custom-call(s32[2]{0:T(128)} %frames_s.11, f32[2,1024,512]{2,1,0:T(8,128)} %get-tuple-element.27.inp, f32[2,8,512]{2,1,0:T(8,128)} %get-tuple-element.28.stats, f32[8,512]{1,0:T(8,128)} %pad_convert_fusion.params), custom_call_target="tpu_custom_call" | custom-call | flops 31457280 | bytes 16777216 | tf_op jit(solution)/shard_map/acts/pallas_call | solution.py:196
  80.1 2.5 copy.52
  82.8 6.8 %all-gather.11.cloned.1.call-done = bf16[1920,16,128]{2,1,0:T(8,128)(2,1)} async-done(((bf16[60,16,128]{2,1,0:T(8,128)(2,1)}), bf16[1920,16,128]{2,1,0:T(8,128)(2,1)}) %all-gather.11.cloned.1.call-update) | async-done | bytes 7864336 | tf_op jit(solution)/shard_map/all_gather | solution.py:665
  89.6 5.5 %copy.41 = bf16[8,4,60,16,128]{4,3,0,2,1:T(8,128)(2,1)S(1)} copy(bf16[8,4,60,16,128]{4,3,2,1,0:T(8,128)(2,1)} %bitcast.42) | data formatting | bytes 15728640 | tf_op jit(solution)/shard_map/reshape | solution.py:670
  100.8 23.7 %conv_forward.1 = (f32[2,1024,512]{2,1,0:T(8,128)}, bf16[2,1024,512]{2,1,0:T(8,128)(2,1)}, f32[2,8,512]{2,1,0:T(8,128)}) custom-call(s32[2]{0:T(128)} %frames_s.11, bf16[2,3,1024,512]{3,2,1,0:T(8,128)(2,1)} %get-tuple-element.29.e_ref, bf16[2,3,1040,512]{3,2,1,0:T(8,128)(2,1)} %get-tuple-element.30.o_ref, f32[2,1024,512]{2,1,0:T(8,128)} %get-tuple-element.27.inp, ...), custom_call_target="tpu_custom_call" | custom-call | flops 9663676416 | bytes 28068672 | tf_op jit(solution)/shard_map/conv_forward/pallas_call | solution.py:277
  125.1 68.7 %attention.1 = (f32[2,1024,512]{2,1,0:T(8,128)}, bf16[2,1024,512]{2,1,0:T(8,128)(2,1)}, f32[2560,512]{1,0:T(8,128)}) custom-call(s32[2]{0:T(128)} %frames_s.11, bf16[2,1024,512]{2,1,0:T(8,128)(2,1)} %get-tuple-element.31.normed, bf16[2,512,768]{2,1,0:T(8,128)(2,1)} %tokens.1, bf16[2,768,512]{2,1,0:T(8,128)(2,1)} %bitcast.47, ...), custom_call_target="tpu_custom_call" | custom-call | flops 19327352832 | bytes 16777216 | tf_op jit(solution)/shard_map/attention/pallas_call | solution.py:394
  193.9 2.9 multiply_convert_fusion
  196.8 2.8 reshape.146
  199.6 2.4 copy.45
  202.0 15.5 %norm2_backward.1 = (f32[2,1024,512]{2,1,0:T(8,128)}, bf16[2,3,1024,512]{3,2,1,0:T(8,128)(2,1)}, bf16[2,3,1040,512]{3,2,1,0:T(8,128)(2,1)}, f32[2,24,512]{2,1,0:T(8,128)}) custom-call(s32[2]{0:T(128)} %frames_s.11, bf16[2,1024,512]{2,1,0:T(8,128)(2,1)} %get-tuple-element.35.dq_ref, f32[2,1024,512]{2,1,0:T(8,128)} %get-tuple-element.33.res, ...), custom_call_target="tpu_custom_call" | custom-call | flops 1073741824 | bytes 27262976 | tf_op jit(solution)/shard_map/norm2_backward/pallas_call | solution.py:488
  220.8 14.6 %tap_gradients.1 = bf16[3,3,16,128,128]{4,3,2,1,0:T(8,128)(2,1)} custom-call(bf16[512,2048]{1,0:T(8,128)(2,1)} %bitcast.45, bf16[2,3,1024,512]{3,2,1,0:T(8,128)(2,1)} %get-tuple-element.37.e_ref, bf16[2,3,1040,512]{3,2,1,0:T(8,128)(2,1)} %get-tuple-element.38.o_ref), custom_call_target="tpu_custom_call" | custom-call | flops 9663676416 | bytes 19680064 | tf_op jit(solution)/shard_map/tap_gradients/pallas_call | solution.py:539
  235.4 6.3 %pad_maximum_fusion = bf16[240,128,128]{2,1,0:T(8,128)(2,1)} fusion(bf16[80,128,128]{2,1,0:T(8,128)(2,1)S(1)} %bitcast.40, bf16[16,128,128]{2,1,0:T(8,128)(2,1)S(1)} %bitcast.44, bf16[144,128,128]{2,1,0:T(8,128)(2,1)} %bitcast.43), kind=kLoop, calls=%fused_computation.2 | loop fusion | flops 7864320 | bytes 15728640 | tf_op jit(solution)/shard_map/concatenate | solution.py:700
  241.7 11.7 %gather_fusion = bf16[240,128,128]{2,1,0:T(8,128)(2,1)} fusion(bf16[240,128,128]{2,1,0:T(8,128)(2,1)} %pad_maximum_fusion, s32[1024]{0:T(1024)S(1)} %pad_clamp_fusion), kind=kCustom, calls=%fused_computation | custom fusion | bytes 15729600 | tf_op jit(solution)/shard_map/jit(_take)/gather | solution.py:718
  253.4 7.0 %copy_select_fusion = bf16[4,60,8,16,128]{4,3,1,0,2:T(8,128)(2,1)} fusion(bf16[4,60,8,16,128]{4,3,2,1,0:T(8,128)(2,1)} %bitcast.34, pred[4,60]{1,0:T(4,128)(4,1)S(1)} %broadcast_in_dim.43), kind=kLoop, calls=%fused_computation.3 | loop fusion | flops 3932160 | bytes 15728880 | tf_op jit(solution)/shard_map/jit(_take)/select_n | solution.py:718
  260.4 121.1 %reduce-scatter.2.cloned.1.call-done = bf16[60,16,128]{2,1,0:T(8,128)(2,1)} async-done(((bf16[1920,16,128]{2,1,0:T(8,128)(2,1)}), bf16[60,16,128]{2,1,0:T(8,128)(2,1)}) %reduce-scatter.2.cloned.1.call-update) | async-done | bytes 245776 | tf_op jit(solution)/shard_map/reduce_scatter | solution.py:730
  381.6 50.9 %all-gather.7.cloned.1.call-done = bf16[60,128,128]{2,1,0:T(8,128)(2,1)} async-done(((bf16[60,16,128]{2,1,0:T(8,128)(2,1)}), bf16[60,128,128]{2,1,0:T(8,128)(2,1)}) %all-gather.7.cloned.1.call-update) | async-done | bytes 1966096 | tf_op jit(solution)/shard_map/all_gather | solution.py:733
  432.5 7.1 %multiply_reduce_fusion = (f32[60]{0:T(128)S(1)}, f32[60,128,128]{2,1,0:T(8,128)}) fusion(f32[60,128,128]{2,1,0:T(8,128)} %param.27, bf16[60,128,128]{2,1,0:T(8,128)(2,1)} %all-gather.7.cloned.1.call-done, f32[60,128,128]{2,1,0:T(8,128)} %param.26), kind=kOutput, calls=%fused_computation.5 | convolution fusion | flops 505282496 | bytes 13762800 | tf_op jit(solution)/shard_map/srk,skt->srt/dot_general | solution.py:739
  441.8 26.2 %input_backward.1 = (f32[2,1024,512]{2,1,0:T(8,128)}, f32[2,16,512]{2,1,0:T(8,128)}) custom-call(s32[2]{0:T(128)} %frames_s.11, bf16[2,3,1024,512]{3,2,1,0:T(8,128)(2,1)} %get-tuple-element.37.e_ref, bf16[2,3,1040,512]{3,2,1,0:T(8,128)(2,1)} %get-tuple-element.38.o_ref, f32[2,1024,512]{2,1,0:T(8,128)} %get-tuple-element.27.inp, ...), custom_call_target="tpu_custom_call" | custom-call | flops 9663676416 | bytes 25165824 | tf_op jit(solution)/shard_map/input_backward/pallas_call | solution.py:612
  469.3 39.0 %all-reduce.1 = f32[192,16]{1,0:T(8,128)S(1)} all-reduce(f32[192,16]{1,0:T(8,128)S(1)} %reshape.149), channel_id=5, replica_groups=mesh['dp'=8,'mp'=4] {'dp','mp'}, use_global_device_ids=true, to_apply=%region_10.11.clone | all-reduce | flops 3072 | bytes 24576
  509.8 3.5 fusion.9
  515.3 17.7 %scatter_fusion = f32[240,16,128]{2,1,0:T(8,128)S(1)} fusion(f32[240,16,128]{2,1,0:T(8,128)S(1)} %broadcast_in_dim.47, s32[240]{0:T(256)S(1)} %compare_select_fusion, f32[240,16,128]{2,1,0:T(8,128)} %all-gather.9.cloned.1.call-done), kind=kCustom, calls=%fused_computation.1 | custom fusion | bytes 5899200 | tf_op jit(solution)/shard_map/scatter | solution.py:745
  (77 shorter events, 25.5 us)
Async XLA Ops:
  7.2 51.3 %copy-start.9 = (s32[2]{0:T(128)S(1)}, s32[2]{0:T(128)}, u32[]{:S(2)}) copy-start(s32[2]{0:T(128)} %param.19) | copy-start | bytes 28
  7.2 82.4 %all-gather.11.cloned.1.call-start = ((), (), s32[]{:S(2)}) async-start(), calls=%async_computation.4 | async-start | bytes 8110080 | tf_op jit(solution)/shard_map/all_gather | solution.py:665
  9.0 372.5 %reduce-scatter.2.cloned.1.call-start = ((), (), s32[]{:S(2)}) async-start(), calls=%async_computation.1 | async-start | bytes 8110080 | tf_op jit(solution)/shard_map/reduce_scatter | solution.py:730
  78.3 4.5 copy-start.8
  95.1 3.3 copy-start
  125.1 68.7 %copy-start.7 = (f32[2560]{0:T(1024)S(1)}, f32[2560]{0:T(1024)}, u32[]{:S(2)}) copy-start(f32[2560]{0:T(1024)} %constant.17.clone.1) | copy-start | bytes 30724
  260.4 172.1 %all-gather.7.cloned.1.call-start = ((), (), s32[]{:S(2)}) async-start(), calls=%async_computation.2 | async-start | bytes 2211840 | tf_op jit(solution)/shard_map/all_gather | solution.py:733
  381.6 133.6 %all-gather.9.cloned.1.call-start = ((), (), s32[]{:S(2)}) async-start(), calls=%async_computation.3 | async-start | bytes 2457600 | tf_op jit(solution)/shard_map/all_gather | solution.py:744
  381.6 60.0 %copy-start.5 = (f32[2,8,512]{2,1,0:T(8,128)S(1)}, f32[2,8,512]{2,1,0:T(8,128)}, u32[]{:S(2)}) copy-start(f32[2,8,512]{2,1,0:T(8,128)} %get-tuple-element.44) | copy-start | bytes 98308
  441.8 66.6 %copy-start.6 = (f32[6,16]{1,0:T(8,128)S(1)}, f32[6,16]{1,0:T(8,128)}, u32[]{:S(2)}) copy-start(f32[6,16]{1,0:T(8,128)} %param.22) | copy-start | bytes 1156
  441.8 67.2 %copy-start.2 = (bf16[60,16,128]{2,1,0:T(8,128)(2,1)S(1)}, bf16[60,16,128]{2,1,0:T(8,128)(2,1)}, u32[]{:S(2)}) copy-start(bf16[60,16,128]{2,1,0:T(8,128)(2,1)} %reduce-scatter.2.cloned.1.call-done) | copy-start | bytes 737284
  441.8 68.0 %copy-start.1 = (bf16[60,128,128]{2,1,0:T(8,128)(2,1)S(1)}, bf16[60,128,128]{2,1,0:T(8,128)(2,1)}, u32[]{:S(2)}) copy-start(bf16[60,128,128]{2,1,0:T(8,128)(2,1)} %all-gather.7.cloned.1.call-done) | copy-start | bytes 5898244
  468.0 45.3 %copy-start.4 = (f32[60,16,128]{2,1,0:T(8,128)S(1)}, f32[60,16,128]{2,1,0:T(8,128)}, u32[]{:S(2)}) copy-start(f32[60,16,128]{2,1,0:T(8,128)} %param.24) | copy-start | bytes 1474564
  515.2 17.9 %copy-start.3 = (f32[60,16,128]{2,1,0:T(8,128)S(1)}, f32[60,16,128]{2,1,0:T(8,128)}, u32[]{:S(2)}) copy-start(f32[60,16,128]{2,1,0:T(8,128)} %param.21) | copy-start | bytes 1474564
Sparse Core Ops, SparseCore 0:
  11.5 78.0 all-gather.10
  260.5 120.9 reduce-scatter.1
  383.8 48.6 all-gather.6
  441.7 20.0 all-gather.8

commit v2 on v1

--- a/solution.py
+++ b/solution.py
@@ -169,10 +169,18 @@
     )(frames, trig, clean, noise, cot)
 
 
-def acts_kernel(frames_s, inp, stats, params, e_ref, o_ref, pad):
+def acts_kernel(frames_s, inp, stats, *refs):
+    pieces, (e_ref, o_ref, params_ref, pad) = refs[:-4], refs[-4:]
     c = pl.program_id(0)
     rows = frames_s[c] * BINS
     T = 64
+    total = None
+    for piece in pieces:
+        for j in range(piece.shape[0]):
+            got = piece[j].astype(F32).reshape(CH // BS, 8, BS)
+            total = got if total is None else total + got
+    params = jnp.concatenate([total[j] for j in range(CH // BS)], axis=1)
+    params_ref[...] = params
     mean, rstd = stats[0, 0:1], stats[0, 1:2]
     scale = rstd * params[0:1]
     shift = params[1:2]
@@ -191,13 +199,16 @@
     write_windows(pad, e_ref, o_ref, 1)
 
 
-def acts_windows(frames, inp, stats, params):
+def acts_windows(frames, inp, stats, pieces):
     n = inp.shape[0]
+    row_share = pieces[0].shape[2]
+    slots = CH // BS * 8 // row_share
     return pl.pallas_call(
         acts_kernel,
         out_shape=(
             jax.ShapeDtypeStruct((n, 3, POS, CH), BF16),
             jax.ShapeDtypeStruct((n, 3, POS + 16, CH), BF16),
+            jax.ShapeDtypeStruct((8, CH), F32),
         ),
         grid_spec=pltpu.PrefetchScalarGridSpec(
             num_scalar_prefetch=1,
@@ -205,11 +216,15 @@
             in_specs=[
                 pl.BlockSpec((1, POS, CH), lambda c, *_: (c, 0, 0)),
                 pl.BlockSpec((1, 8, CH), lambda c, *_: (c, 0, 0)),
-                pl.BlockSpec((8, CH), lambda c, *_: (0, 0)),
+            ]
+            + [
+                pl.BlockSpec((p.shape[0], slots, row_share, BS), lambda c, *_: (0, 0, 0, 0))
+                for p in pieces
             ],
             out_specs=[
                 pl.BlockSpec((1, 3, POS, CH), lambda c, *_: (c, 0, 0, 0)),
                 pl.BlockSpec((1, 3, POS + 16, CH), lambda c, *_: (c, 0, 0, 0)),
+                pl.BlockSpec((8, CH), lambda c, *_: (0, 0)),
             ],
             scratch_shapes=[pltpu.VMEM((POS + 16, CH), F32)],
         ),
@@ -218,11 +233,38 @@
             flops=n * POS * CH * 30, bytes_accessed=n * POS * CH * 16, transcendentals=n * POS * CH
         ),
         name="acts",
-    )(frames, inp, stats, params)
-
-
-def conv_kernel(frames_s, e_ref, o_ref, inp, emb, params, w, res, normed, stats):
+    )(frames, inp, stats, *pieces)
+
+
+def conv_kernel(chunks, frames_s, dest_s, e_ref, o_ref, inp, emb, params, *refs):
+    pieces, (res, normed, stats, w_out, w, sem, sem_out) = refs[: -7], refs[-7:]
     c = pl.program_id(0)
+    per_chunk = len(pieces) // len(chunks)
+    row_share = pieces[0].shape[2]
+
+    @pl.when(c == 0)
+    def _():
+        copies = []
+        for j, (skip, start, count) in enumerate(chunks):
+            for a in range(per_chunk):
+                ref = pieces[j * per_chunk + a]
+                for p in range(ref.shape[0]):
+                    i = a * ref.shape[0] + p
+                    first = dest_s[0, i] + start
+                    row = pl.multiple_of(dest_s[1, i], row_share)
+                    copies.append(
+                        pltpu.make_async_copy(
+                            ref.at[p, pl.ds(skip, count)],
+                            w.at[pl.ds(first, count), pl.ds(row, row_share), :],
+                            sem.at[len(copies)],
+                        )
+                    )
+        for copy in copies:
+            copy.start()
+        for copy in copies:
+            copy.wait()
+        pltpu.make_async_copy(w, w_out, sem_out).start()
+
     rows = frames_s[c] * BINS
     R = 256
     T = 64
@@ -263,6 +305,10 @@
     lax.fori_loop(0, POS // T, third, 0)
     stats[0] = jnp.concatenate([mean, rstd, jnp.zeros((6, CH), F32)], axis=0)
 
+    @pl.when(c == pl.num_programs(0) - 1)
+    def _():
+        pltpu.make_async_copy(w, w_out, sem_out).wait()
+
 
 def whole(shape):
     return pl.BlockSpec(shape, lambda *_: (0,) * len(shape), pipeline_mode=pl.Buffered(1))
@@ -272,17 +318,19 @@
     return pl.BlockSpec((1,) + shape, lambda c, *_: (c,) + (0,) * len(shape))
 
 
-def conv_forward(frames, e, o, inp, emb, params, w):
+def conv_forward(frames, dest, e, o, inp, emb, params, pieces, chunks):
     n = inp.shape[0]
+    copies = sum(p.shape[0] for p in pieces)
     return pl.pallas_call(
-        conv_kernel,
+        functools.partial(conv_kernel, chunks),
         out_shape=(
             jax.ShapeDtypeStruct((n, POS, CH), F32),
             jax.ShapeDtypeStruct((n, POS, CH), BF16),
             jax.ShapeDtypeStruct((n, 8, CH), F32),
+            jax.ShapeDtypeStruct((NBLK, BS, BS), BF16),
         ),
         grid_spec=pltpu.PrefetchScalarGridSpec(
-            num_scalar_prefetch=1,
+            num_scalar_prefetch=2,
             grid=(n,),
             in_specs=[
                 per_clip((3, POS, CH)),
@@ -290,16 +338,26 @@
                 per_clip((POS, CH)),
                 per_clip((16, CH)),
                 whole((8, CH)),
-                pl.BlockSpec((QUERY0, BS, BS), lambda *_: (0, 0, 0), pipeline_mode=pl.Buffered(1)),
+            ]
+            + [pl.BlockSpec(memory_space=pl.ANY)] * len(pieces),
+            out_specs=[
+                per_clip((POS, CH)),
+                per_clip((POS, CH)),
+                per_clip((8, CH)),
+                pl.BlockSpec(memory_space=pl.ANY),
             ],
-            out_specs=[per_clip((POS, CH)), per_clip((POS, CH)), per_clip((8, CH))],
+            scratch_shapes=[
+                pltpu.VMEM((NBLK, BS, BS), BF16),
+                pltpu.SemaphoreType.DMA((copies,)),
+                pltpu.SemaphoreType.DMA(()),
+            ],
         ),
         compiler_params=pltpu.CompilerParams(vmem_limit_bytes=VMEM_LIMIT),
         cost_estimate=pl.CostEstimate(
             flops=n * POS * CH * CH * 18, bytes_accessed=n * POS * CH * 22 + 5000000, transcendentals=0
         ),
         name="conv_forward",
-    )(frames, e, o, inp, emb, params, w)
+    )(frames, dest, e, o, inp, emb, params, *pieces)
 
 
 def attn_kernel(
@@ -310,10 +368,10 @@
     c = pl.program_id(0)
     rows = frames_s[c] * BINS
     R = 256
-    query_w = mat(w, 0, 4, 4)
-    out_w = mat(w, SQ, 4, 4)
-    key_w = mat(w, 2 * SQ, CTX // BS, 4)
-    value_w = mat(w, 2 * SQ + KV, CTX // BS, 4)
+    query_w = mat(w, SQ, 4, 4)
+    out_w = mat(w, 2 * SQ, 4, 4)
+    key_w = mat(w, 3 * SQ, CTX // BS, 4)
+    value_w = mat(w, 3 * SQ + KV, CTX // BS, 4)
 
     def project(i, carry):
         r = pl.multiple_of(i * R, R)
@@ -390,7 +448,7 @@
 def attention(frames, normed, tokens, tok_t, kmask, outlow, res, params, w):
     n = normed.shape[0]
     ctx_len = tokens.shape[1]
-    amount = 2 * SQ + 2 * KV
+    amount = SQ + SQ + SQ + KV + KV
     return pl.pallas_call(
         attn_kernel,
         out_shape=(
@@ -409,7 +467,11 @@
                 per_clip((POS, CH)),
                 per_clip((POS, CH)),
                 whole((8, CH)),
-                whole((amount, BS, BS)),
+                pl.BlockSpec(
+                    (pl.Element(amount), pl.Element(BS), pl.Element(BS)),
+                    lambda *_: (TEMB0, 0, 0),
+                    pipeline_mode=pl.Buffered(1),
+                ),
             ],
             out_specs=[
                 per_clip((POS, CH)),
@@ -502,7 +564,7 @@
                 per_clip((8, CH)),
                 per_clip((POS, CH)),
                 whole((8, CH)),
-                whole((SQ, BS, BS)),
+                pl.BlockSpec((SQ, BS, BS), lambda *_: (QUERY0 // SQ, 0, 0), pipeline_mode=pl.Buffered(1)),
             ],
             out_specs=[
                 per_clip((POS, CH)),
@@ -520,45 +582,88 @@
     )(frames, dq, res, stats, cot, params, w)
 
 
-def tap_kernel(at, e_ref, o_ref, out):
+def tap_kernel(parts, table_s, at, emb, sums, dw_att, e_ref, o_ref, *refs):
+    outs, (blocks, sem) = refs[: 2 * parts], refs[2 * parts :]
     n = e_ref.shape[0]
+    d = pl.program_id(0)
+    entries = table_s.shape[1]
+
+    def cut(value, first, stride):
+        low = value.astype(BF16)
+        for a in range(value.shape[0] // BS):
+            for b in range(4):
+                blocks[first + a * 4 + b] = low[a * BS : (a + 1) * BS, b * BS : (b + 1) * BS]
+
+    def send(lo, hi):
+        def one(i, carry):
+            for q in range(2 * parts):
+                @pl.when(table_s[0, i] == q)
+                def _():
+                    src = blocks.at[jnp.minimum(i, NBLK)]
+                    pltpu.make_async_copy(src, outs[q].at[table_s[1, i]], sem).start()
+
+            return carry
+
+        lax.fori_loop(lo, hi, one, 0)
+
     for df in range(3):
         acc = None
         for c in range(n):
             g = window(e_ref, o_ref, 2 - df, 0, 0, POS, (c,))
             part = nn(at[:, c * POS : (c + 1) * POS], g)
             acc = part if acc is None else acc + part
-        acc = (acc * CONV_SCALE).astype(BF16)
-        for a in range(4):
-            for b in range(4):
-                out[df, 0, a * 4 + b] = acc[a * BS : (a + 1) * BS, b * BS : (b + 1) * BS]
-
-
-def tap_gradients(at, e, o):
+        cut(acc * CONV_SCALE, (3 * df + d) * SQ, 4)
+        send((3 * df + d) * SQ, (3 * df + d + 1) * SQ)
+
+    @pl.when(d == 0)
+    def _():
+        rows = [jnp.sum(sums[c, 0:8], axis=0, keepdims=True) for c in range(n)]
+        grad = jnp.concatenate(rows + [jnp.zeros((16 - n, CH), F32)], axis=0).astype(BF16)
+        outer = lax.dot_general(emb[...], grad, (((0,), (0,)), ((), ())), preferred_element_type=F32)
+        cut(outer * INV_WIDTH, TEMB0, 4)
+        blocks[NBLK] = jnp.zeros((BS, BS), BF16)
+        cut(dw_att[0:CH] * INV_WIDTH, QUERY0, 4)
+        cut(dw_att[CH : 2 * CH] * OUT_SCALE, OUT0, 4)
+        cut(dw_att[2 * CH :] * INV_CTX, KEY0, 4)
+        send(TEMB0, entries)
+
+    @pl.when(d == pl.num_programs(0) - 1)
+    def _():
+        for out in outs:
+            pltpu.make_async_copy(out, out, sem).wait()
+
+
+def tap_gradients(table, at, emb, sums, dw_att, e, o, sizes):
     n = e.shape[0]
+    parts = len(sizes) // 2
     return pl.pallas_call(
-        tap_kernel,
-        out_shape=jax.ShapeDtypeStruct((3, 3, SQ, BS, BS), BF16),
+        functools.partial(tap_kernel, parts),
+        out_shape=tuple(jax.ShapeDtypeStruct((s, BS, BS), BF16) for s in sizes),
         grid_spec=pltpu.PrefetchScalarGridSpec(
-            num_scalar_prefetch=0,
+            num_scalar_prefetch=1,
             grid=(3,),
             in_specs=[
                 whole((CH, n * POS)),
-                pl.BlockSpec((n, 1, POS, CH), lambda d: (0, d, 0, 0)),
-                pl.BlockSpec((n, 1, POS + 16, CH), lambda d: (0, d, 0, 0)),
+                whole((16, CH)),
+                whole(sums.shape),
+                whole(dw_att.shape),
+                pl.BlockSpec((n, 1, POS, CH), lambda d, *_: (0, d, 0, 0)),
+                pl.BlockSpec((n, 1, POS + 16, CH), lambda d, *_: (0, d, 0, 0)),
             ],
-            out_specs=pl.BlockSpec((3, 1, SQ, BS, BS), lambda d: (0, d, 0, 0, 0)),
+            out_specs=[pl.BlockSpec(memory_space=pl.ANY)] * len(sizes),
+            scratch_shapes=[pltpu.VMEM((NBLK + 1, BS, BS), BF16), pltpu.SemaphoreType.DMA(())],
         ),
         compiler_params=pltpu.CompilerParams(vmem_limit_bytes=VMEM_LIMIT),
         cost_estimate=pl.CostEstimate(
-            flops=n * POS * CH * CH * 18, bytes_accessed=n * POS * CH * 14 + 5000000, transcendentals=0
+            flops=n * POS * CH * CH * 18, bytes_accessed=n * POS * CH * 14 + 20000000, transcendentals=0
         ),
         name="tap_gradients",
-    )(at, e, o)
-
-
-def input_kernel(frames_s, e_ref, o_ref, inp, stats, rgrad, params, w, out, sums, ag_s):
-    c = pl.program_id(0)
+    )(table, at, emb, sums, dw_att, e, o)
+
+
+def input_kernel(clip, frames_s, e_ref, o_ref, inp, stats, rgrad, params, w, *refs):
+    out, sums, ag_s = refs[-3:]
+    c = clip
     rows = frames_s[c] * BINS
     R = 256
     T = 64
@@ -607,40 +712,100 @@
     sums[0, 8:16] = s0
 
 
-def input_backward(frames, e, o, inp, stats, rgrad, params, w):
+def input_backward(clip, frames, e, o, inp, stats, rgrad, params, w, before=None):
     n = inp.shape[0]
+
+    def of_clip(shape):
+        return pl.BlockSpec((1,) + shape, lambda i, *_: (clip,) + (0,) * len(shape))
+
+    before = () if before is None else (before,)
     return pl.pallas_call(
-        input_kernel,
+        functools.partial(input_kernel, clip),
         out_shape=(
             jax.ShapeDtypeStruct((n, POS, CH), F32),
-            jax.ShapeDtypeStruct((n, 16, CH), F32),
+            jax.ShapeDtypeStruct((1, 16, CH), F32),
         ),
         grid_spec=pltpu.PrefetchScalarGridSpec(
             num_scalar_prefetch=1,
-            grid=(n,),
+            grid=(1,),
             in_specs=[
-                per_clip((3, POS, CH)),
-                per_clip((3, POS + 16, CH)),
-                per_clip((POS, CH)),
-                per_clip((8, CH)),
-                per_clip((POS, CH)),
+                of_clip((3, POS, CH)),
+                of_clip((3, POS + 16, CH)),
+                of_clip((POS, CH)),
+                of_clip((8, CH)),
+                of_clip((POS, CH)),
                 whole((8, CH)),
                 pl.BlockSpec((TEMB0, BS, BS), lambda *_: (0, 0, 0), pipeline_mode=pl.Buffered(1)),
-            ],
-            out_specs=[per_clip((POS, CH)), per_clip((16, CH))],
+            ]
+            + [pl.BlockSpec(memory_space=pl.ANY)] * len(before),
+            out_specs=[of_clip((POS, CH)), pl.BlockSpec((1, 16, CH), lambda *_: (0, 0, 0))],
             scratch_shapes=[pltpu.VMEM((POS, CH), F32)],
         ),
+        input_output_aliases={8: 0} if before else {},
         compiler_params=pltpu.CompilerParams(vmem_limit_bytes=VMEM_LIMIT),
         cost_estimate=pl.CostEstimate(
-            flops=n * POS * CH * CH * 18, bytes_accessed=n * POS * CH * 24, transcendentals=n * POS * CH
+            flops=POS * CH * CH * 18, bytes_accessed=POS * CH * 24, transcendentals=POS * CH
         ),
         name="input_backward",
-    )(frames, e, o, inp, stats, rgrad, params, w)
-
-
-def to_blocks(matrix):
-    r, k = matrix.shape
-    return matrix.reshape(r // BS, BS, k // BS, BS).transpose(0, 2, 1, 3).reshape(-1, BS, BS)
+    )(frames, e, o, inp, stats, rgrad, params, w, *before)
+
+
+def pad_kernel(n_data, table_s, obias, sums2, *refs):
+    sums1, (_, _, keep, send, blocks, sem) = refs[:-6], refs[-6:]
+    n_model = table_s.shape[1]
+    row_share = BS // n_data
+    width = CH // (n_data * n_model)
+    total = lambda v: jnp.sum(v, axis=0, keepdims=True)
+    first = sums1[0][0]
+    for v in sums1[1:]:
+        first = first + v[0]
+    second, bias = sums2[0], obias[0]
+    for i in range(1, sums2.shape[0]):
+        second, bias = second + sums2[i], bias + obias[i]
+    grads = jnp.concatenate(
+        [
+            total(first[0:8]), total(first[8:16]), total(second[0:8]), total(second[8:16]),
+            total(second[16:24]), total(bias), jnp.zeros((2, CH), F32),
+        ],
+        axis=0,
+    )
+    lane = lax.broadcasted_iota(jnp.int32, (8, BS), 1)
+    copies = []
+    for m in range(n_model):
+        tiles = []
+        for d in range(n_data):
+            at = (d * n_model + m) * width
+            tile = grads[:, at // BS * BS : (at // BS + 1) * BS]
+            tile = pltpu.roll(tile, (BS - at % BS) % BS, 1)
+            tiles.append(jnp.where(lane < width, tile, 0.0))
+            if row_share > 8:
+                tiles.append(jnp.zeros((row_share - 8, BS), F32))
+        blocks[m] = jnp.concatenate(tiles, axis=0).astype(BF16)
+    for m in range(n_model):
+        for q, out in enumerate((keep, send)):
+            @pl.when(table_s[0, m] == q)
+            def _():
+                pltpu.make_async_copy(blocks.at[m], out.at[table_s[1, m]], sem).start()
+
+    pltpu.make_async_copy(blocks, blocks, sem).wait()
+
+
+def add_norm_grads(table, n_data, obias, sums2, sums1, keep, send):
+    vm = pl.BlockSpec(memory_space=pltpu.VMEM)
+    any_space = pl.BlockSpec(memory_space=pl.ANY)
+    n = 3 + len(sums1)
+    return pl.pallas_call(
+        functools.partial(pad_kernel, n_data),
+        out_shape=(
+            jax.ShapeDtypeStruct(keep.shape, BF16),
+            jax.ShapeDtypeStruct(send.shape, BF16),
+        ),
+        in_specs=[pl.BlockSpec(memory_space=pltpu.SMEM)] + [vm] * (n - 1) + [any_space] * 2,
+        out_specs=[any_space] * 2,
+        scratch_shapes=[pltpu.VMEM((table.shape[1], BS, BS), BF16), pltpu.SemaphoreType.DMA(())],
+        input_output_aliases={n: 0, n + 1: 1},
+        name="norm_grads",
+    )(table, obias, sums2, *sums1, keep, send)
 
 
 def sinusoid(timesteps):
@@ -648,6 +813,168 @@
     freqs = jnp.exp(-math.log(10000.0) * jnp.arange(half_width, dtype=F32) / half_width)
     angles = timesteps.astype(F32)[:, None] * freqs[None, :]
     return jnp.concatenate([jnp.sin(angles), jnp.cos(angles)], axis=-1)
+
+
+def step_kernel(dp_s, grad, left_root, right_root, step, stats):
+    g = grad[0]
+    low = g.astype(BF16)
+    n_data, row_share = step.shape[0], step.shape[2]
+    left = nt(low, low)
+    right = lax.dot_general(low, low, (((0,), (0,)), ((), ())), preferred_element_type=F32)
+    side = nn(left_root[0].astype(BF16), low)
+    update = nn(side.astype(BF16), right_root[0].astype(BF16))
+    rate = learn_rate * lax.rsqrt(jnp.sum(update * update, keepdims=True) * (1.0 / (BS * BS)) + 1e-06)
+    step[:, 0] = (update * rate).reshape(n_data, row_share, BS).astype(BF16)
+    stats[:, 0, 0] = g.reshape(n_data, row_share, BS).astype(BF16)
+    stats[:, 0, 1] = left.reshape(n_data, row_share, BS).astype(BF16)
+    stats[:, 0, 2] = right.reshape(n_data, row_share, BS).astype(BF16)
+
+
+def owner_step(dp, grad, left_root, right_root, n_data, row_share):
+    k = grad.shape[0]
+    last = left_root.shape[0] - 1
+    root = pl.BlockSpec((1, BS, BS), lambda i, dp: (jnp.minimum(dp[0] * k + i, last), 0, 0))
+    return pl.pallas_call(
+        step_kernel,
+        out_shape=(
+            jax.ShapeDtypeStruct((n_data, k, row_share, BS), BF16),
+            jax.ShapeDtypeStruct((n_data, k, 3, row_share, BS), BF16),
+        ),
+        grid_spec=pltpu.PrefetchScalarGridSpec(
+            num_scalar_prefetch=1,
+            grid=(k,),
+            in_specs=[pl.BlockSpec((1, BS, BS), lambda i, dp: (i, 0, 0)), root, root],
+            out_specs=[
+                pl.BlockSpec((n_data, 1, row_share, BS), lambda i, dp: (0, i, 0, 0)),
+                pl.BlockSpec((n_data, 1, 3, row_share, BS), lambda i, dp: (0, i, 0, 0, 0)),
+            ],
+        ),
+        cost_estimate=pl.CostEstimate(flops=k * 8 * BS**3, bytes_accessed=k * BS * BS * 20, transcendentals=0),
+        name="owner_step",
+    )(dp, grad, left_root, right_root)
+
+
+def master_kernel(where_s, master, near, far, new, low, steps):
+    half = near.shape[0]
+    steps[0:half] = near[...].astype(F32)
+    steps[half:] = far[...].astype(F32)
+
+    def one(j, carry):
+        value = master[j] - steps[where_s[j]]
+        new[j] = value
+        low[j] = value.astype(BF16)
+        return carry
+
+    lax.fori_loop(0, master.shape[0], one, 0)
+
+
+def update_master(where, master, near, far):
+    vm = pl.BlockSpec(memory_space=pltpu.VMEM)
+    return pl.pallas_call(
+        master_kernel,
+        out_shape=(
+            jax.ShapeDtypeStruct(master.shape, F32),
+            jax.ShapeDtypeStruct(master.shape, BF16),
+        ),
+        in_specs=[pl.BlockSpec(memory_space=pltpu.SMEM), vm, vm, vm],
+        out_specs=[vm, vm],
+        scratch_shapes=[pltpu.VMEM((2 * near.shape[0],) + near.shape[1:], F32)],
+        name="update_master",
+    )(where, master, near, far)
+
+
+class Grid:
+    def __init__(self, n_data, n_model):
+        self.nd, self.nm = n_data, n_model
+        self.nx = n_model // 2
+        self.ny = 1
+        while self.ny * self.ny * 4 <= n_data:
+            self.ny *= 2
+        self.nz = n_data // self.ny
+        self.split = self.nx == self.ny
+        self.sizes = (self.ny, self.ny) if self.split else (self.ny, self.nx)
+        dp, mp = lax.axis_index("dp"), lax.axis_index("mp")
+        self.z, self.y, self.x, self.c = dp // self.ny, dp % self.ny, mp // 2, mp % 2
+
+    def permute(self, value, fn):
+        pairs = []
+        for src in range(self.nd * self.nm):
+            dp, mp = divmod(src, self.nm)
+            z, y, x, c = fn(dp // self.ny, dp % self.ny, mp // 2, mp % 2)
+            dst = ((z % self.nz) * self.ny + y % self.ny) * self.nm + (x % self.nx) * 2 + c % 2
+            pairs.append((src, dst))
+        return lax.ppermute(value, ("dp", "mp"), pairs)
+
+    def along_z(self, value, d):
+        return self.permute(value, lambda z, y, x, c: (z + d, y, x, c))
+
+    def along_plane(self, value, stage, d):
+        def fn(z, y, x, c):
+            on_y = (stage == 0) != (self.split and c == 1)
+            return (z, y + d, x, c) if on_y else (z, y, x + d, c)
+
+        return self.permute(value, fn)
+
+    def along_core(self, value):
+        return self.permute(value, lambda z, y, x, c: (z, y, x, c + 1))
+
+    def place(self, core, d0, d1, dz):
+        swap = (core == 1) if self.split else jnp.zeros_like(core == 1)
+        dy, dx = jnp.where(swap, d1, d0), jnp.where(swap, d0, d1)
+        zz, yy, xx = (self.z + dz) % self.nz, (self.y + dy) % self.ny, (self.x + dx) % self.nx
+        return zz * self.ny + yy, xx * 2 + core
+
+
+def after(value, *others):
+    return lax.optimization_barrier((value,) + others)[0]
+
+
+def gather_z(grid, shard):
+    return [shard] + [grid.along_z(shard, -d) for d in range(1, grid.nz)]
+
+
+def gather_plane(grid, stack):
+    got = [stack] + [grid.along_plane(stack, 0, -d) for d in range(1, grid.sizes[0])]
+    stack = jnp.concatenate(got)
+    got = [stack] + [grid.along_plane(stack, 1, -d) for d in range(1, grid.sizes[1])]
+    return got + [grid.along_core(v) for v in got]
+
+
+def gather_places(grid):
+    dps, mps = [], []
+    for rel in range(2):
+        core = (grid.c + rel) % 2
+        for d1 in range(grid.sizes[1]):
+            for d0 in range(grid.sizes[0]):
+                for dz in range(grid.nz):
+                    dp, mp = grid.place(core, d0, d1, dz)
+                    dps.append(dp)
+                    mps.append(mp)
+    return jnp.stack(dps), jnp.stack(mps)
+
+
+def add_low(*parts):
+    total = parts[0].astype(F32)
+    for p in parts[1:]:
+        total = total + p.astype(F32)
+    return total
+
+
+def scatter_core(grid, keep, send):
+    return add_low(keep, grid.along_core(send)).astype(BF16)
+
+
+def scatter_plane(grid, value, stage):
+    size = grid.sizes[stage]
+    value = value.reshape(size, -1, BS, BS)
+    got = [grid.along_plane(value[d], stage, d) for d in range(1, size)]
+    return add_low(value[0], *got).astype(BF16)
+
+
+def scatter_z(grid, value):
+    value = value.reshape(grid.nz, -1, BS, BS)
+    got = [grid.along_z(value[d], d) for d in range(1, grid.nz)]
+    return add_low(value[0], *got)
 
 
 def body(
@@ -660,96 +987,123 @@
     clip_count = clean_latent.shape[0]
     ctx_len = codec_tokens.shape[1]
     slot_count, row_share = (master_blocks.shape[0], master_blocks.shape[1])
-    master_low = master_blocks.astype(BF16)[None]
-    params_low = norm_params.astype(BF16)[None]
-    gathered = lax.all_gather(master_low, ("dp", "mp"), axis=0, tiled=True)
-    gathered_params = lax.all_gather(params_low, ("dp", "mp"), axis=0, tiled=True)
-    params = gathered_params.transpose(1, 0, 2).reshape(gathered_params.shape[1], -1).astype(F32)
-    params = jnp.pad(params, ((0, 2), (0, 0)))
-    blocks = (
-        gathered.reshape(n_data, n_model, slot_count, row_share, BS)
-        .transpose(1, 2, 0, 3, 4)
-        .reshape(n_model * slot_count, BS, BS)
+    param_rows, width = norm_params.shape
+    grid = Grid(n_data, n_model)
+    dp, mp = lax.axis_index("dp"), lax.axis_index("mp")
+    me = dp * n_model + mp
+
+    own_params = lax.dynamic_update_slice(
+        jnp.zeros((8, CH), BF16), norm_params.astype(BF16), (0, me * width)
     )
+    param_tiles = own_params.reshape(8, CH // BS, BS).transpose(1, 0, 2).reshape(-1, row_share, BS)
+    skip = param_tiles.shape[0]
+    master_low = master_blocks.astype(BF16)
+    cut = slot_count // 2
+    chunks = ((skip, 0, cut), (0, cut, slot_count - cut))
+    ring0 = gather_z(grid, jnp.concatenate([param_tiles, master_low[:cut]]))
+    ring1 = gather_z(grid, master_low[cut:])
+    place_dp, place_mp = gather_places(grid)
+    dest = jnp.stack([place_mp * slot_count, place_dp * row_share])
 
     phases = timesteps.astype(F32) * (0.5 * math.pi / TSTEPS)
     trig = jnp.stack([jnp.cos(phases), jnp.sin(phases)])
     embedding = jax.nn.silu(sinusoid(timesteps)).astype(BF16)
     emb_rows = jnp.broadcast_to(embedding[:, None, :], (clip_count, 16, CH))
+    emb_pad = jnp.pad(embedding, ((0, 16 - clip_count), (0, 0)))
     kmask = jnp.broadcast_to(codec_mask.astype(F32)[:, None, :], (clip_count, 8, ctx_len))
     tok_t = codec_tokens.transpose(0, 2, 1)
 
+    k = slot_count // n_data + 1
+    padded = n_data * k
+    k0 = k // 2
+
+    def route(to_mp, to_slot):
+        to_dp, to_k = to_slot // k, to_slot % k
+        to_core = to_mp % 2
+        rel_core = (to_core + grid.c) % 2
+        dz = (to_dp // grid.ny - grid.z) % grid.nz
+        dy = (to_dp % grid.ny - grid.y) % grid.ny
+        dx = (to_mp // 2 - grid.x) % grid.nx
+        swap = (to_core == 1) if grid.split else jnp.zeros_like(to_core == 1)
+        d0, d1 = jnp.where(swap, dx, dy), jnp.where(swap, dy, dx)
+        part = (to_k >= k0).astype(jnp.int32)
+        k_part = jnp.where(part == 1, k - k0, k0)
+        index = ((d1 * grid.sizes[0] + d0) * grid.nz + dz) * k_part + to_k - part * k0
+        return rel_core * 2 + part, index
+
+    block_ids = jnp.arange(NBLK, dtype=jnp.int32)
+    slot_of_block = jnp.sum(
+        jnp.where(owned_block[None, :] == block_ids[:, None], block_ids[None, :], 0), axis=1
+    )
+    pad_ids = jnp.arange(n_model * (padded - slot_count), dtype=jnp.int32)
+    per = padded - slot_count
+    block_mp = jnp.concatenate([slot_of_block // slot_count, pad_ids // per])
+    block_slot = jnp.concatenate([slot_of_block % slot_count, pad_ids % per + slot_count])
+    table = jnp.stack(route(block_mp, block_slot))
+    model_ids = jnp.arange(n_model, dtype=jnp.int32)
+    pad_quarter, pad_index = route(model_ids, jnp.full((n_model,), padded - 1, jnp.int32))
+    pad_table = jnp.stack([pad_quarter // 2, pad_index])
+    half = n_model * padded // 2
+    sizes = tuple(half // k * kk for _ in range(2) for kk in (k0, k - k0))
+    my_slots = lax.dynamic_slice_in_dim(slot_of_block, mp * slot_count, slot_count)
+    from_mp = my_slots // slot_count
+    where = (
+        ((from_mp + grid.c) % 2 * grid.nx + (from_mp // 2 - grid.x) % grid.nx) * padded + my_slots % slot_count
+    )
+
     inp, outlow, stats1, obias = pre(frames, trig, clean_latent, noise_latent, out_cotangent)
-    e1, o1 = acts_windows(frames, inp, stats1, params)
+    stack0 = after(jnp.stack(ring0), stats1)
+    pieces = gather_plane(grid, stack0)
+    stack1 = after(jnp.stack(ring1), table, pad_table, where, dest, kmask, emb_rows, emb_pad, tok_t)
+    later = gather_plane(grid, stack1)
+    e1, o1, params = acts_windows(frames, inp, stats1, pieces)
     at = e1[:, 1].reshape(-1, CH).T
-    res, normed, stats2 = conv_forward(frames, e1, o1, inp, emb_rows, params, blocks)
+    e1 = after(e1, at)
+    res, normed, stats2, blocks = conv_forward(
+        frames, dest, e1, o1, inp, emb_rows, params, pieces + later, chunks
+    )
     block_output, dq, dw_att = attention(
-        frames, normed, codec_tokens, tok_t, kmask, outlow, res, params, blocks[QUERY0:]
+        frames, normed, codec_tokens, tok_t, kmask, outlow, res, params, blocks
     )
-    rgrad, e2, o2, sums2 = norm2_backward(frames, dq, res, stats2, out_cotangent, params, blocks[QUERY0:OUT0])
-    dtaps = tap_gradients(at, e2, o2)
-    input_grad, sums1 = input_backward(frames, e2, o2, inp, stats1, rgrad, params, blocks)
-
-    clip_sums = jnp.sum(sums2[:, 0:8], axis=1)
-    temb_grad = clip_sums.astype(BF16)
-    dtemb = jnp.einsum("nc,nd->cd", embedding, temb_grad, preferred_element_type=F32) * INV_WIDTH
-    att_scales = jnp.concatenate(
-        [jnp.full((CH, 1), INV_WIDTH), jnp.full((CH, 1), OUT_SCALE), jnp.full((2 * CTX, 1), INV_CTX)]
-    ).astype(F32)
-    dw_att = (dw_att * att_scales).astype(BF16)
-    local_blocks = jnp.concatenate(
-        [
-            dtaps.reshape(TEMB0, BS, BS),
-            to_blocks(dtemb.astype(BF16)),
-            to_blocks(dw_att),
-        ],
-        axis=0,
+    rgrad, e2, o2, sums2 = norm2_backward(frames, dq, res, stats2, out_cotangent, params, blocks)
+    keep0, keep1, send0, send1 = tap_gradients(table, at, emb_pad, sums2, dw_att, e2, o2, sizes)
+
+    sums1, input_grad = [], None
+    value0 = keep0
+    for clip in range(clip_count):
+        if clip == 1:
+            value0 = scatter_core(grid, keep0, send0)
+        input_grad, part = input_backward(
+            clip, frames, after(e2, value0), o2, inp, stats1, rgrad, params, blocks, input_grad
+        )
+        sums1.append(part)
+    value0 = scatter_plane(grid, value0, 1)
+    keep1, send1 = add_norm_grads(pad_table, n_data, obias, sums2, sums1, keep1, send1)
+    value1 = scatter_core(grid, keep1, send1)
+    value0 = scatter_plane(grid, value0, 0)
+    value1 = scatter_plane(grid, value1, 1)
+    grad0 = scatter_z(grid, value0)
+    value1 = scatter_plane(grid, value1, 0)
+    grad1 = scatter_z(grid, value1)
+    full_grad = jnp.concatenate([grad0, grad1])
+
+    step, stats = owner_step(dp[None], full_grad, left_root, right_root, n_data, row_share)
+    step = lax.all_to_all(step, "dp", 0, 0, tiled=True).reshape(padded, row_share, BS)
+    near = jnp.concatenate(
+        [step] + [grid.permute(step, lambda z, y, x, c, d=d: (z, y, x - d, c)) for d in range(1, grid.nx)]
     )
-    param_grads = jnp.stack(
-        [
-            jnp.sum(sums1[:, 0:8], axis=(0, 1)),
-            jnp.sum(sums1[:, 8:16], axis=(0, 1)),
-            jnp.sum(clip_sums, axis=0),
-            jnp.sum(sums2[:, 8:16], axis=(0, 1)),
-            jnp.sum(sums2[:, 16:24], axis=(0, 1)),
-            jnp.sum(obias, axis=(0, 1)),
-        ]
-    )
-    permuted = jnp.take(local_blocks, owned_block, axis=0)
-    arranged = (
-        permuted.reshape(n_model, slot_count, n_data, row_share, BS)
-        .transpose(2, 0, 1, 3, 4)
-        .reshape(-1, row_share, BS)
-    )
-    param_rows = param_grads.shape[0]
-    param_arranged = (
-        param_grads.reshape(param_rows, total_devices, -1)
-        .transpose(1, 0, 2)
-        .reshape(total_devices * param_rows, -1)
-    )
-    owned_low = lax.psum_scatter(arranged, ("dp", "mp"), scatter_dimension=0, tiled=True)
-    norm_grads = lax.psum_scatter(param_arranged, ("dp", "mp"), scatter_dimension=0, tiled=True)
-    owned_rows = owned_low.astype(F32)
-    full_grad = lax.all_gather(owned_low, "dp", axis=1, tiled=True).astype(F32)
-    row_start = lax.axis_index("dp") * row_share
-    my_columns = lax.dynamic_slice_in_dim(full_grad, row_start, row_share, 2)
-    new_left = 0.5 * left_stats + 0.5 * jnp.einsum("srk,stk->srt", owned_rows, full_grad)
-    new_right = 0.5 * right_stats + 0.5 * jnp.einsum("skr,skt->srt", my_columns, full_grad)
-    left_side = jnp.einsum("srk,skt->srt", left_root, full_grad)
-    update = jnp.einsum("srk,skt->srt", left_side, right_root)
-    update_step = (
-        learn_rate * update * lax.rsqrt(jnp.mean(update * update, axis=(1, 2), keepdims=True) + 1e-06)
-    )
-    step_rows = lax.dynamic_slice_in_dim(update_step, row_start, row_share, 1)
-    all_steps = lax.all_gather(step_rows, "mp", axis=0, tiled=True)
-    natural = jnp.zeros_like(all_steps).at[owned_block].set(all_steps)
-    my_steps = lax.dynamic_slice_in_dim(natural, lax.axis_index("mp") * slot_count, slot_count, 0)
-    new_master = master_blocks - my_steps
+    far = grid.along_core(near)
+    stats = lax.all_to_all(stats, "dp", 0, 0, tiled=True).reshape(padded, 3, row_share, BS)
+    new_master, master_copy = update_master(where, master_blocks, near, far)
+    owned_rows = stats[:slot_count, 0].astype(F32)
+    new_left = 0.5 * left_stats + 0.5 * stats[:slot_count, 1].astype(F32)
+    new_right = 0.5 * right_stats + 0.5 * stats[:slot_count, 2].astype(F32)
+    norm_grads = stats[padded - 1, 0, :param_rows, :width].astype(F32)
     small_rate = 0.5 / math.sqrt(clip_count * total_devices * POS)
     new_norm = norm_params - small_rate * norm_grads
     return (
-        block_output, input_grad, owned_rows, new_left, new_right, new_master,
-        new_master.astype(BF16), norm_grads, new_norm,
+        block_output, input_grad, owned_rows, new_left, new_right, new_master, master_copy,
+        norm_grads, new_norm,
     )
 
 

time: 542 us -> 352 us (0.65)
  waiting for transfers between devices: 179 us -> 72.4 us
  blocking collectives: 82.8 us -> 12.1 us
  starting transfers between devices: 0.16 us -> 44.2 us
  local copies, waits for them, and re-layouts: 56.4 us -> 12.5 us
  Pallas kernels: 167 us -> 195 us
  other arithmetic: 28 us -> 13.9 us
  between operations: 14.1 us -> 1.1 us
  matrix products: 12.8 us -> 0 us
    reduce_scatter x1 -> x0, waiting for transfers between devices: 121 us -> none  [body(): lax.psum_scatter(arranged, ('dp', 'mp'), scatter_dimension=0, tiled=True)]
    ppermute x0 -> x28, waiting for transfers between devices: none -> 66.4 us  [permute(): return lax.ppermute(value, ('dp', 'mp'), pairs)]
    all_gather x3 -> x0, waiting for transfers between devices: 57.7 us -> none  [the longest x1 50.9 us: body(): full_grad = lax.all_gather(owned_low, 'dp', axis=1, tiled=True).astype(F32)]
    all_gather x1 -> x0, blocking collectives: 43.8 us -> none  [body(): lax.all_gather(params_low, ('dp', 'mp'), axis=0, tiled=True)]
    ppermute x0 -> x28, starting transfers between devices: none -> 40.5 us  [permute(): return lax.ppermute(value, ('dp', 'mp'), pairs)]
    unnamed x1 -> x0, blocking collectives: 39 us -> none
    pallas_call x3 -> x7, Pallas kernels: 64.5 us -> 93 us  [the longest x2 31.9 us: input_backward(): pl.pallas_call(functools.partial(input_kernel, clip), out_shape=(jax.Shap...]
    scatter x1 -> x0, local copies, waits for them, and re-layouts: 17.7 us -> none  [body(): natural = jnp.zeros_like(all_steps).at[owned_block].set(all_steps)]
  transfers between devices with their start and end apart: 4 -> 29, of which waited for: 3 -> 13; matrix products, arithmetic and copies ran while one was open for 4% -> 5% of each run, Pallas kernels for 8% -> 10%
where the time goes in v2:
time: 352 us; the launch traced here: 351 us
  Pallas kernels  195 us (55%)
  waiting for transfers between devices  72.4 us (21%)
  starting transfers between devices  44.2 us (13%)
  other arithmetic  13.9 us (4%)
  local copies, waits for them, and re-layouts  12.5 us (4%)
  blocking collectives  12.1 us (3%)
    pallas_call x1, Pallas kernels, attention(): pl.pallas_call(attn_kernel, out_shape=(jax.ShapeDtypeStruct((n, POS, CH),...  68.8 us
    ppermute x28, waiting for transfers between devices, permute(): return lax.ppermute(value, ('dp', 'mp'), pairs)  66.4 us
    ppermute x28, starting transfers between devices, permute(): return lax.ppermute(value, ('dp', 'mp'), pairs)  40.5 us
    pallas_call x2, Pallas kernels, input_backward(): pl.pallas_call(functools.partial(input_kernel, clip), out_shape=(jax.Shap...  31.9 us
    pallas_call x1, Pallas kernels, conv_forward(): pl.pallas_call(functools.partial(conv_kernel, chunks), out_shape=(jax.Sha...  26.6 us
    pallas_call x1, Pallas kernels, tap_gradients(): pl.pallas_call(functools.partial(tap_kernel, parts), out_shape=tuple((jax...  23 us
    pallas_call x1, Pallas kernels, norm2_backward(): pl.pallas_call(norm2_kernel, out_shape=(jax.ShapeDtypeStruct((n, POS, CH)...  15.5 us
    all_to_all x1, blocking collectives, body(): lax.all_to_all(step, 'dp', 0, 0, tiled=True).reshape(padded, row_share, BS)  12.1 us
  transfers between devices with their start and end apart: 29, of which 13 were waited for; matrix products, arithmetic and copies ran while one was open for 5% of the time, Pallas kernels for 10%

profile of v2, /device:TPU:0, one launch (start us, length us, event | category | flops | bytes accessed | tf_op | source)
XLA Modules:
  0.0 351.1 jit_solution(8427048001798684662)
XLA Ops:
  1.8 4.1 %collective-permute-start.8 = (bf16[30,16,128]{2,1,0:T(8,128)(2,1)S(1)}, bf16[30,16,128]{2,1,0:T(8,128)(2,1)S(1)}, u32[]{:S(2)}, u32[]{:S(2)}) collective-permute-start(bf16[30,16,128]{2,1,0:T(8,128)(2,1)S(1)} %get-tuple-element.94), channel_id=1, source_target_pairs={{0,16},{1,17},{2,18},{3,19},{4,20},{5,21},{6,22},{7,23},{8,24},{9,... | collective-permute-start | bytes 368648 | tf_op jit(solution)/shard_map/ppermute | solution.py:906
  14.5 9.3 %inputs_stats.1 = (f32[2,1024,512]{2,1,0:T(8,128)}, bf16[2,1024,512]{2,1,0:T(8,128)(2,1)}, f32[2,8,512]{2,1,0:T(8,128)}, f32[2,8,512]{2,1,0:T(8,128)}) custom-call(s32[2]{0:T(128)} %frames_s.13, f32[2,2]{1,0:T(2,128)} %pad_maximum_fusion.6.trig_s, f32[2,1024,512]{2,1,0:T(8,128)} %clean.1, f32[2,1024,512]{2,1,0:T(8,128)} %noise.1, f32[2,1024,512]{2,1,0:T(8,128)} %cot.3), custom_call_target="tpu_custom_call" | custom-call | flops 20971520 | bytes 18874368 | tf_op jit(solution)/shard_map/inputs_stats/pallas_call | solution.py:155
  36.3 9.8 %collective-permute-done.10 = bf16[4,30,16,128]{3,2,1,0:T(8,128)(2,1)S(1)} collective-permute-done((bf16[4,30,16,128]{3,2,1,0:T(8,128)(2,1)S(1)}, bf16[4,30,16,128]{3,2,1,0:T(8,128)(2,1)S(1)}, u32[]{:S(2)}, u32[]{:S(2)}) %collective-permute-start.10) | collective-permute-done | bytes 491552 | tf_op jit(solution)/shard_map/ppermute | solution.py:906
  51.3 10.0 %collective-permute-done.11.refs_5_ = bf16[8,30,16,128]{3,2,1,0:T(8,128)(2,1)} collective-permute-done((bf16[8,30,16,128]{3,2,1,0:T(8,128)(2,1)}, bf16[8,30,16,128]{3,2,1,0:T(8,128)(2,1)}, u32[]{:S(2)}, u32[]{:S(2)}) %collective-permute-start.11) | collective-permute-done | bytes 983072 | tf_op jit(solution)/shard_map/ppermute | solution.py:906
  62.9 8.4 %acts.1 = (bf16[2,3,1024,512]{3,2,1,0:T(8,128)(2,1)}, bf16[2,3,1040,512]{3,2,1,0:T(8,128)(2,1)}, f32[8,512]{1,0:T(8,128)}) custom-call(s32[2]{0:T(128)} %frames_s.13, f32[2,1024,512]{2,1,0:T(8,128)} %get-tuple-element.46.inp, f32[2,8,512]{2,1,0:T(8,128)} %get-tuple-element.47.stats, bf16[8,32,16,128]{3,2,1,0:T(8,128)(2,1)} %copy-done.1, ...), custom_call_target="tpu_custom_call" | custom-call | flops 31457280 | bytes 16777216 | tf_op jit(solution)/shard_map/acts/pallas_call | solution.py:206
  75.5 26.6 %conv_forward.1 = (f32[2,1024,512]{2,1,0:T(8,128)}, bf16[2,1024,512]{2,1,0:T(8,128)(2,1)}, f32[2,8,512]{2,1,0:T(8,128)}, bf16[240,128,128]{2,1,0:T(8,128)(2,1)}) custom-call(s32[2]{0:T(128)} %frames_s.13, s32[2,32]{1,0:T(2,128)} %pad_add_fusion.1.dest_s, bf16[2,3,1024,512]{3,2,1,0:T(8,128)(2,1)} %get-tuple-element.50.e_ref, ...), custom_call_target="tpu_custom_call" | custom-call | flops 9663676416 | bytes 28068672 | tf_op jit(solution)/shard_map/conv_forward/pallas_call | solution.py:324
  102.2 68.8 %attention.1 = (f32[2,1024,512]{2,1,0:T(8,128)}, bf16[2,1024,512]{2,1,0:T(8,128)(2,1)}, f32[2560,512]{1,0:T(8,128)}) custom-call(s32[2]{0:T(128)} %frames_s.13, bf16[2,1024,512]{2,1,0:T(8,128)(2,1)} %get-tuple-element.54.normed, bf16[2,512,768]{2,1,0:T(8,128)(2,1)} %tokens.1, bf16[2,768,512]{2,1,0:T(8,128)(2,1)} %bitcast.91, ...), custom_call_target="tpu_custom_call" | custom-call | flops 19327352832 | bytes 16777216 | tf_op jit(solution)/shard_map/attention/pallas_call | solution.py:452
  170.9 15.5 %norm2_backward.1 = (f32[2,1024,512]{2,1,0:T(8,128)}, bf16[2,3,1024,512]{3,2,1,0:T(8,128)(2,1)}, bf16[2,3,1040,512]{3,2,1,0:T(8,128)(2,1)}, f32[2,24,512]{2,1,0:T(8,128)}) custom-call(s32[2]{0:T(128)} %frames_s.13, bf16[2,1024,512]{2,1,0:T(8,128)(2,1)} %get-tuple-element.59.dq_ref, f32[2,1024,512]{2,1,0:T(8,128)} %get-tuple-element.56.res, ...), custom_call_target="tpu_custom_call" | custom-call | flops 1073741824 | bytes 27262976 | tf_op jit(solution)/shard_map/norm2_backward/pallas_call | solution.py:550
  186.5 23.0 %tap_gradients.1 = (bf16[64,128,128]{2,1,0:T(8,128)(2,1)}, bf16[64,128,128]{2,1,0:T(8,128)(2,1)}, bf16[64,128,128]{2,1,0:T(8,128)(2,1)}, bf16[64,128,128]{2,1,0:T(8,128)(2,1)}) custom-call(s32[2,256]{1,0:T(2,128)} %pad_add_fusion.table_s, bf16[512,2048]{1,0:T(8,128)(2,1)} %bitcast.90, bf16[16,512]{1,0:T(8,128)(2,1)} %pad.4.emb, ...), custom_call_target="tpu_custom_call" | custom-call | flops 9663676416 | bytes 34680064 | tf_op jit(solution)/shard_map/tap_gradients/pallas_call | solution.py:639
  209.8 15.9 %input_backward.2 = (f32[2,1024,512]{2,1,0:T(8,128)}, f32[1,16,512]{2,1,0:T(8,128)}) custom-call(s32[2]{0:T(128)} %frames_s.13, bf16[2,3,1024,512]{3,2,1,0:T(8,128)(2,1)} %get-tuple-element.69.e_ref, bf16[2,3,1040,512]{3,2,1,0:T(8,128)(2,1)} %get-tuple-element.64.o_ref, f32[2,1024,512]{2,1,0:T(8,128)} %get-tuple-element.46.inp, ...), custom_call_target="tpu_custom_call" | custom-call | flops 4831838208 | bytes 12582912 | tf_op jit(solution)/shard_map/input_backward/pallas_call | solution.py:722
  225.7 3.0 add_convert_fusion.1
  228.7 15.9 %input_backward.3 = (f32[2,1024,512]{2,1,0:T(8,128)}, f32[1,16,512]{2,1,0:T(8,128)}) custom-call(s32[2]{0:T(128)} %frames_s.13, bf16[2,3,1024,512]{3,2,1,0:T(8,128)(2,1)} %get-tuple-element.69.e_ref, bf16[2,3,1040,512]{3,2,1,0:T(8,128)(2,1)} %get-tuple-element.64.o_ref, f32[2,1024,512]{2,1,0:T(8,128)} %get-tuple-element.46.inp, ...), custom_call_target="tpu_custom_call", output_to_operand_aliasing={{0}: (8, {})} | custom-call | flops 4831838208 | bytes 12582912 | tf_op jit(solution)/shard_map/input_backward/pallas_call | solution.py:722
  253.8 7.8 %collective-permute-done.15 = bf16[32,128,128]{2,1,0:T(8,128)(2,1)S(1)} collective-permute-done((bf16[32,128,128]{2,1,0:T(8,128)(2,1)S(1)}, bf16[32,128,128]{2,1,0:T(8,128)(2,1)S(1)}, u32[]{:S(2)}, u32[]{:S(2)}) %collective-permute-start.15) | collective-permute-done | bytes 1048608 | tf_op jit(solution)/shard_map/ppermute | solution.py:906
  263.8 14.7 %collective-permute-done.21 = bf16[32,128,128]{2,1,0:T(8,128)(2,1)S(1)} collective-permute-done((bf16[32,128,128]{2,1,0:T(8,128)(2,1)S(1)}, bf16[32,128,128]{2,1,0:T(8,128)(2,1)S(1)}, u32[]{:S(2)}, u32[]{:S(2)}) %collective-permute-start.21) | collective-permute-done | bytes 1048608 | tf_op jit(solution)/shard_map/ppermute | solution.py:906
  282.0 2.6 collective-permute-start.19
  292.2 4.3 %collective-permute-start.24 = (bf16[4,128,128]{2,1,0:T(8,128)(2,1)S(1)}, bf16[4,128,128]{2,1,0:T(8,128)(2,1)S(1)}, u32[]{:S(2)}, u32[]{:S(2)}) collective-permute-start(bf16[4,128,128]{2,1,0:T(8,128)(2,1)S(1)} %get-tuple-element.92), channel_id=1, source_target_pairs={{0,16},{1,17},{2,18},{3,19},{4,20},{5,21},{6,22},{7,23},{8,24},{9,... | collective-permute-start | bytes 393224 | tf_op jit(solution)/shard_map/ppermute | solution.py:906
  296.6 5.9 %collective-permute-done.18 = bf16[4,128,128]{2,1,0:T(8,128)(2,1)S(1)} collective-permute-done((bf16[4,128,128]{2,1,0:T(8,128)(2,1)S(1)}, bf16[4,128,128]{2,1,0:T(8,128)(2,1)S(1)}, u32[]{:S(2)}, u32[]{:S(2)}) %collective-permute-start.18) | collective-permute-done | bytes 131104 | tf_op jit(solution)/shard_map/ppermute | solution.py:906
  302.5 4.5 %collective-permute-done.24 = bf16[4,128,128]{2,1,0:T(8,128)(2,1)S(1)} collective-permute-done((bf16[4,128,128]{2,1,0:T(8,128)(2,1)S(1)}, bf16[4,128,128]{2,1,0:T(8,128)(2,1)S(1)}, u32[]{:S(2)}, u32[]{:S(2)}) %collective-permute-start.24) | collective-permute-done | bytes 131104 | tf_op jit(solution)/shard_map/ppermute | solution.py:906
  307.9 7.0 %owner_step.1 = (bf16[8,8,16,128]{3,2,1,0:T(8,128)(2,1)}, bf16[8,8,3,16,128]{4,3,2,1,0:T(8,128)(2,1)}) custom-call(s32[1]{0:T(128)} %bitcast.52.dp_s, f32[8,128,128]{2,1,0:T(8,128)} %pad_maximum_fusion.1.grad, f32[60,128,128]{2,1,0:T(8,128)} %left_root.1, f32[60,128,128]{2,1,0:T(8,128)} %right_root.1), custom_call_target="tpu_custom_call" | custom-call | flops 134217728 | bytes 2621440 | tf_op jit(solution)/shard_map/owner_step/pallas_call | solution.py:837
  314.8 12.1 %all_to_all.10 = bf16[8,8,16,128]{3,2,1,0:T(8,128)(2,1)S(1)} all-to-all(bf16[8,8,16,128]{3,2,1,0:T(8,128)(2,1)} %get-tuple-element.80), channel_id=1, replica_groups=mesh['dp'=8,'mp'=4] {'dp'}, dimensions={0} | all-to-all | bytes 524288 | tf_op jit(solution)/shard_map/all_to_all | solution.py:1091
  326.9 3.7 %all-to-all-start = ((bf16[8,8,3,16,128]{4,3,2,1,0:T(8,128)(2,1)}), bf16[8,8,3,16,128]{4,3,2,1,0:T(8,128)(2,1)S(1)}, u32[]{:S(2)}, u32[]{:S(2)}) async-start(bf16[8,8,3,16,128]{4,3,2,1,0:T(8,128)(2,1)} %get-tuple-element.79), calls=%async_computation | async-start | bytes 1572864 | tf_op jit(solution)/shard_map/all_to_all | solution.py:1096
  331.3 5.8 %collective-permute-done.26 = bf16[64,16,128]{2,1,0:T(8,128)(2,1)S(1)} collective-permute-done((bf16[64,16,128]{2,1,0:T(8,128)(2,1)S(1)}, bf16[64,16,128]{2,1,0:T(8,128)(2,1)S(1)}, u32[]{:S(2)}, u32[]{:S(2)}) %collective-permute-start.26) | collective-permute-done | bytes 262176 | tf_op jit(solution)/shard_map/ppermute | solution.py:906
  339.9 2.8 update_master.1
  342.7 6.0 %all-to-all-done = bf16[8,8,3,16,128]{4,3,2,1,0:T(8,128)(2,1)S(1)} async-done(((bf16[8,8,3,16,128]{4,3,2,1,0:T(8,128)(2,1)}), bf16[8,8,3,16,128]{4,3,2,1,0:T(8,128)(2,1)S(1)}, u32[]{:S(2)}, u32[]{:S(2)}) %all-to-all-start) | async-done | bytes 786464 | tf_op jit(solution)/shard_map/all_to_all | solution.py:1096
  (130 shorter events, 62.6 us)
Async XLA Ops:
  1.8 27.5 %collective-permute-start.8 = (bf16[30,16,128]{2,1,0:T(8,128)(2,1)S(1)}, bf16[30,16,128]{2,1,0:T(8,128)(2,1)S(1)}, u32[]{:S(2)}, u32[]{:S(2)}) collective-permute-start(bf16[30,16,128]{2,1,0:T(8,128)(2,1)S(1)} %get-tuple-element.94), channel_id=1, source_target_pairs={{0,16},{1,17},{2,18},{3,19},{4,20},{5,21},{6,22},{7,23},{8,24},{9,... | collective-permute-start | bytes 368648 | tf_op jit(solution)/shard_map/ppermute | solution.py:906
  5.9 23.4 %collective-permute-start.7 = (bf16[30,16,128]{2,1,0:T(8,128)(2,1)S(1)}, bf16[30,16,128]{2,1,0:T(8,128)(2,1)S(1)}, u32[]{:S(2)}, u32[]{:S(2)}) collective-permute-start(bf16[30,16,128]{2,1,0:T(8,128)(2,1)S(1)} %get-tuple-element.94), channel_id=1, source_target_pairs={{0,24},{1,25},{2,26},{3,27},{4,28},{5,29},{6,30},{7,31},{8,0},{9,1... | collective-permute-start | bytes 368648 | tf_op jit(solution)/shard_map/ppermute | solution.py:906
  8.2 15.7 %collective-permute-start.1 = (bf16[32,16,128]{2,1,0:T(8,128)(2,1)S(1)}, bf16[32,16,128]{2,1,0:T(8,128)(2,1)S(1)}, u32[]{:S(2)}, u32[]{:S(2)}) collective-permute-start(bf16[32,16,128]{2,1,0:T(8,128)(2,1)S(1)} %get-tuple-element.97), channel_id=1, source_target_pairs={{0,16},{1,17},{2,18},{3,19},{4,20},{5,21},{6,22},{7,23},{8,24},{9,... | collective-permute-start | bytes 393224 | tf_op jit(solution)/shard_map/ppermute | solution.py:906
  9.9 14.1 %collective-permute-start = (bf16[32,16,128]{2,1,0:T(8,128)(2,1)S(1)}, bf16[32,16,128]{2,1,0:T(8,128)(2,1)S(1)}, u32[]{:S(2)}, u32[]{:S(2)}) collective-permute-start(bf16[32,16,128]{2,1,0:T(8,128)(2,1)S(1)} %get-tuple-element.97), channel_id=1, source_target_pairs={{0,24},{1,25},{2,26},{3,27},{4,28},{5,29},{6,30},{7,31},{8,0},{9,1... | collective-permute-start | bytes 393224 | tf_op jit(solution)/shard_map/ppermute | solution.py:906
  11.3 12.7 %collective-permute-start.2 = (bf16[32,16,128]{2,1,0:T(8,128)(2,1)S(1)}, bf16[32,16,128]{2,1,0:T(8,128)(2,1)S(1)}, u32[]{:S(2)}, u32[]{:S(2)}) collective-permute-start(bf16[32,16,128]{2,1,0:T(8,128)(2,1)S(1)} %get-tuple-element.97), channel_id=1, source_target_pairs={{0,8},{1,9},{2,10},{3,11},{4,12},{5,13},{6,14},{7,15},{8,16},{9,17... | collective-permute-start | bytes 393224 | tf_op jit(solution)/shard_map/ppermute | solution.py:906
  24.1 9.7 %collective-permute-start.3 = (bf16[4,32,16,128]{3,2,1,0:T(8,128)(2,1)S(1)}, bf16[4,32,16,128]{3,2,1,0:T(8,128)(2,1)S(1)}, u32[]{:S(2)}, u32[]{:S(2)}) collective-permute-start(bf16[4,32,16,128]{3,2,1,0:T(8,128)(2,1)S(1)} %pad_maximum_fusion), channel_id=1, source_target_pairs={{0,4},{1,3},{2,6},{3,1},{4,0},{5,7},{6,2},{7,5},{8,12},{9,11},{10,... | collective-permute-start | bytes 1572872 | tf_op jit(solution)/shard_map/ppermute | solution.py:906
  32.0 14.1 %collective-permute-start.10 = (bf16[4,30,16,128]{3,2,1,0:T(8,128)(2,1)S(1)}, bf16[4,30,16,128]{3,2,1,0:T(8,128)(2,1)S(1)}, u32[]{:S(2)}, u32[]{:S(2)}) collective-permute-start(bf16[4,30,16,128]{3,2,1,0:T(8,128)(2,1)S(1)} %pad_maximum_fusion.3), channel_id=1, source_target_pairs={{0,4},{1,3},{2,6},{3,1},{4,0},{5,7},{6,2},{7,5},{8,12},{9,11},{10,... | collective-permute-start | bytes 1474568 | tf_op jit(solution)/shard_map/ppermute | solution.py:906
  33.8 15.0 %collective-permute-start.4 = (bf16[8,32,16,128]{3,2,1,0:T(8,128)(2,1)S(1)}, bf16[8,32,16,128]{3,2,1,0:T(8,128)(2,1)S(1)}, u32[]{:S(2)}, u32[]{:S(2)}) collective-permute-start(bf16[8,32,16,128]{3,2,1,0:T(8,128)(2,1)S(1)} %constant_dynamic-update-slice_fusion.refs_0_), channel_id=1, source_target_pairs={{0,2},{1,5},{2,0},{3,7},{4,6},{5,1},{6,4},{7,3},{8,10},{9,13},{10,... | collective-permute-start | bytes 3145736 | tf_op jit(solution)/shard_map/ppermute | solution.py:906
  46.9 14.4 %collective-permute-start.11 = (bf16[8,30,16,128]{3,2,1,0:T(8,128)(2,1)}, bf16[8,30,16,128]{3,2,1,0:T(8,128)(2,1)}, u32[]{:S(2)}, u32[]{:S(2)}) collective-permute-start(bf16[8,30,16,128]{3,2,1,0:T(8,128)(2,1)} %constant_dynamic-update-slice_fusion.2.refs_4_), channel_id=1, source_target_pairs={{0,2},{1,5},{2,0},{3,7},{4,6},{5,1},{6,4},{7,3},{8,10},{9,13},{10,... | collective-permute-start | bytes 2949128 | tf_op jit(solution)/shard_map/ppermute | solution.py:906
  48.6 12.9 %collective-permute-start.5 = (bf16[8,32,16,128]{3,2,1,0:T(8,128)(2,1)S(1)}, bf16[8,32,16,128]{3,2,1,0:T(8,128)(2,1)S(1)}, u32[]{:S(2)}, u32[]{:S(2)}) collective-permute-start(bf16[8,32,16,128]{3,2,1,0:T(8,128)(2,1)S(1)} %constant_dynamic-update-slice_fusion.refs_0_), channel_id=1, source_target_pairs={{0,1},{1,0},{2,3},{3,2},{4,5},{5,4},{6,7},{7,6},{8,9},{9,8},{10,11... | collective-permute-start | bytes 3145736 | tf_op jit(solution)/shard_map/ppermute | solution.py:906
  48.9 12.7 %collective-permute-start.6 = (bf16[8,32,16,128]{3,2,1,0:T(8,128)(2,1)S(1)}, bf16[8,32,16,128]{3,2,1,0:T(8,128)(2,1)S(1)}, u32[]{:S(2)}, u32[]{:S(2)}) collective-permute-start(bf16[8,32,16,128]{3,2,1,0:T(8,128)(2,1)S(1)} %collective-permute-done.4.refs_1_), channel_id=1, source_target_pairs={{0,1},{1,0},{2,3},{3,2},{4,5},{5,4},{6,7},{7,6},{8,9},{9,8},{10,11... | collective-permute-start | bytes 3145736 | tf_op jit(solution)/shard_map/ppermute | solution.py:906
  51.3 24.2 %collective-permute-start.12 = (bf16[8,30,16,128]{3,2,1,0:T(8,128)(2,1)}, bf16[8,30,16,128]{3,2,1,0:T(8,128)(2,1)}, u32[]{:S(2)}, u32[]{:S(2)}) collective-permute-start(bf16[8,30,16,128]{3,2,1,0:T(8,128)(2,1)} %constant_dynamic-update-slice_fusion.2.refs_4_), channel_id=1, source_target_pairs={{0,1},{1,0},{2,3},{3,2},{4,5},{5,4},{6,7},{7,6},{8,9},{9,8},{10,11... | collective-permute-start | bytes 2949128 | tf_op jit(solution)/shard_map/ppermute | solution.py:906
  61.3 14.2 %collective-permute-start.13 = (bf16[8,30,16,128]{3,2,1,0:T(8,128)(2,1)}, bf16[8,30,16,128]{3,2,1,0:T(8,128)(2,1)}, u32[]{:S(2)}, u32[]{:S(2)}) collective-permute-start(bf16[8,30,16,128]{3,2,1,0:T(8,128)(2,1)} %collective-permute-done.11.refs_5_), channel_id=1, source_target_pairs={{0,1},{1,0},{2,3},{3,2},{4,5},{5,4},{6,7},{7,6},{8,9},{9,8},{10,11... | collective-permute-start | bytes 2949128 | tf_op jit(solution)/shard_map/ppermute | solution.py:906
  209.5 16.2 %collective-permute-start.14 = (bf16[64,128,128]{2,1,0:T(8,128)(2,1)}, bf16[64,128,128]{2,1,0:T(8,128)(2,1)}, u32[]{:S(2)}, u32[]{:S(2)}) collective-permute-start(bf16[64,128,128]{2,1,0:T(8,128)(2,1)} %get-tuple-element.66), channel_id=1, source_target_pairs={{0,1},{1,0},{2,3},{3,2},{4,5},{5,4},{6,7},{7,6},{8,9},{9,8},{10,11... | collective-permute-start | bytes 6291464 | tf_op jit(solution)/shard_map/ppermute | solution.py:906
  246.8 14.9 %collective-permute-start.15 = (bf16[32,128,128]{2,1,0:T(8,128)(2,1)S(1)}, bf16[32,128,128]{2,1,0:T(8,128)(2,1)S(1)}, u32[]{:S(2)}, u32[]{:S(2)}) collective-permute-start(bf16[32,128,128]{2,1,0:T(8,128)(2,1)S(1)} %slice.111), channel_id=1, source_target_pairs={{0,2},{1,5},{2,0},{3,7},{4,6},{5,1},{6,4},{7,3},{8,10},{9,13},{10,... | collective-permute-start | bytes 3145736 | tf_op jit(solution)/shard_map/ppermute | solution.py:906
  252.0 26.5 %collective-permute-start.21 = (bf16[32,128,128]{2,1,0:T(8,128)(2,1)S(1)}, bf16[32,128,128]{2,1,0:T(8,128)(2,1)S(1)}, u32[]{:S(2)}, u32[]{:S(2)}) collective-permute-start(bf16[32,128,128]{2,1,0:T(8,128)(2,1)S(1)} %slice.119), channel_id=1, source_target_pairs={{0,2},{1,5},{2,0},{3,7},{4,6},{5,1},{6,4},{7,3},{8,10},{9,13},{10,... | collective-permute-start | bytes 3145736 | tf_op jit(solution)/shard_map/ppermute | solution.py:906
  262.1 18.5 %collective-permute-start.16 = (bf16[16,128,128]{2,1,0:T(8,128)(2,1)S(1)}, bf16[16,128,128]{2,1,0:T(8,128)(2,1)S(1)}, u32[]{:S(2)}, u32[]{:S(2)}) collective-permute-start(bf16[16,128,128]{2,1,0:T(8,128)(2,1)S(1)} %slice.113), channel_id=1, source_target_pairs={{0,4},{1,3},{2,6},{3,1},{4,0},{5,7},{6,2},{7,5},{8,12},{9,11},{10,... | collective-permute-start | bytes 1572872 | tf_op jit(solution)/shard_map/ppermute | solution.py:906
  280.8 11.4 %collective-permute-start.17 = (bf16[4,128,128]{2,1,0:T(8,128)(2,1)S(1)}, bf16[4,128,128]{2,1,0:T(8,128)(2,1)S(1)}, u32[]{:S(2)}, u32[]{:S(2)}) collective-permute-start(bf16[4,128,128]{2,1,0:T(8,128)(2,1)S(1)} %get-tuple-element.87), channel_id=1, source_target_pairs={{0,8},{1,9},{2,10},{3,11},{4,12},{5,13},{6,14},{7,15},{8,16},{9,17... | collective-permute-start | bytes 393224 | tf_op jit(solution)/shard_map/ppermute | solution.py:906
  282.0 14.5 %collective-permute-start.19 = (bf16[4,128,128]{2,1,0:T(8,128)(2,1)S(1)}, bf16[4,128,128]{2,1,0:T(8,128)(2,1)S(1)}, u32[]{:S(2)}, u32[]{:S(2)}) collective-permute-start(bf16[4,128,128]{2,1,0:T(8,128)(2,1)S(1)} %get-tuple-element.88), channel_id=1, source_target_pairs={{0,24},{1,25},{2,26},{3,27},{4,28},{5,29},{6,30},{7,31},{8,0},{9,1... | collective-permute-start | bytes 393224 | tf_op jit(solution)/shard_map/ppermute | solution.py:906
  284.7 17.7 %collective-permute-start.18 = (bf16[4,128,128]{2,1,0:T(8,128)(2,1)S(1)}, bf16[4,128,128]{2,1,0:T(8,128)(2,1)S(1)}, u32[]{:S(2)}, u32[]{:S(2)}) collective-permute-start(bf16[4,128,128]{2,1,0:T(8,128)(2,1)S(1)} %get-tuple-element.89), channel_id=1, source_target_pairs={{0,16},{1,17},{2,18},{3,19},{4,20},{5,21},{6,22},{7,23},{8,24},{9,... | collective-permute-start | bytes 393224 | tf_op jit(solution)/shard_map/ppermute | solution.py:906
  288.4 14.1 %collective-permute-start.23 = (bf16[4,128,128]{2,1,0:T(8,128)(2,1)S(1)}, bf16[4,128,128]{2,1,0:T(8,128)(2,1)S(1)}, u32[]{:S(2)}, u32[]{:S(2)}) collective-permute-start(bf16[4,128,128]{2,1,0:T(8,128)(2,1)S(1)} %get-tuple-element.90), channel_id=1, source_target_pairs={{0,8},{1,9},{2,10},{3,11},{4,12},{5,13},{6,14},{7,15},{8,16},{9,17... | collective-permute-start | bytes 393224 | tf_op jit(solution)/shard_map/ppermute | solution.py:906
  290.3 12.2 %collective-permute-start.25 = (bf16[4,128,128]{2,1,0:T(8,128)(2,1)S(1)}, bf16[4,128,128]{2,1,0:T(8,128)(2,1)S(1)}, u32[]{:S(2)}, u32[]{:S(2)}) collective-permute-start(bf16[4,128,128]{2,1,0:T(8,128)(2,1)S(1)} %get-tuple-element.91), channel_id=1, source_target_pairs={{0,24},{1,25},{2,26},{3,27},{4,28},{5,29},{6,30},{7,31},{8,0},{9,1... | collective-permute-start | bytes 393224 | tf_op jit(solution)/shard_map/ppermute | solution.py:906
  292.2 14.7 %collective-permute-start.24 = (bf16[4,128,128]{2,1,0:T(8,128)(2,1)S(1)}, bf16[4,128,128]{2,1,0:T(8,128)(2,1)S(1)}, u32[]{:S(2)}, u32[]{:S(2)}) collective-permute-start(bf16[4,128,128]{2,1,0:T(8,128)(2,1)S(1)} %get-tuple-element.92), channel_id=1, source_target_pairs={{0,16},{1,17},{2,18},{3,19},{4,20},{5,21},{6,22},{7,23},{8,24},{9,... | collective-permute-start | bytes 393224 | tf_op jit(solution)/shard_map/ppermute | solution.py:906
  326.9 21.8 %all-to-all-start = ((bf16[8,8,3,16,128]{4,3,2,1,0:T(8,128)(2,1)}), bf16[8,8,3,16,128]{4,3,2,1,0:T(8,128)(2,1)S(1)}, u32[]{:S(2)}, u32[]{:S(2)}) async-start(bf16[8,8,3,16,128]{4,3,2,1,0:T(8,128)(2,1)} %get-tuple-element.79), calls=%async_computation | async-start | bytes 1572864 | tf_op jit(solution)/shard_map/all_to_all | solution.py:1096
  (19 other events, 196.6 us)

commit v3 on v2

--- a/solution.py
+++ b/solution.py
@@ -65,17 +65,21 @@
     return jnp.sum(x.reshape(-1, 8, x.shape[-1]), axis=0)
 
 
-def group_sums(rows8, gmat):
-    total = jnp.broadcast_to(jnp.sum(rows8, axis=0, keepdims=True), (8, CH))
-    return lax.dot_general(
-        total, gmat, (((1,), (0,)), ((), ())), preferred_element_type=F32, precision=highest
-    )[0:1]
-
-
-def group_matrix():
+def group_sums(*partials):
     i = lax.broadcasted_iota(jnp.int32, (CH, CH), 0) // (CH // GROUPS)
     j = lax.broadcasted_iota(jnp.int32, (CH, CH), 1) // (CH // GROUPS)
-    return (i == j).astype(F32)
+    gmat = jnp.where(i == j, 1.0, 0.0).astype(BF16)
+    row = lax.broadcasted_iota(jnp.int32, (16, CH), 0)
+    stack = jnp.zeros((16, CH), F32)
+    for k, rows8 in enumerate(partials):
+        rest = jnp.sum(rows8, axis=0, keepdims=True)
+        for t in range(3):
+            term = rest.astype(BF16).astype(F32)
+            stack = jnp.where(row == 3 * k + t, term, stack)
+            rest = rest - term
+    out = nn(stack.astype(BF16), gmat)
+    sums = [out[3 * k : 3 * k + 1] + out[3 * k + 1 : 3 * k + 2] + out[3 * k + 2 : 3 * k + 3] for k in range(len(partials))]
+    return sums[0] if len(sums) == 1 else sums
 
 
 def shift_bins(tile, step):
@@ -88,7 +92,7 @@
     return jnp.where(keep, rolled, 0.0).reshape(tile.shape)
 
 
-def write_windows(pad, e_ref, o_ref, sign):
+def write_windows(pad, e_ref, o_ref, sign, lead=0):
     T = 64
 
     def body(i, carry):
@@ -97,14 +101,14 @@
         low = pad[pl.ds(r, T), :]
         for d in range(3):
             step = sign * (d - 1)
-            e_ref[0, d, pl.ds(r, T), :] = shift_bins(mid, step).astype(BF16)
-            o_ref[0, d, pl.ds(r, T), :] = shift_bins(low, step).astype(BF16)
+            e_ref[lead, d, pl.ds(r, T), :] = shift_bins(mid, step).astype(BF16)
+            o_ref[lead, d, pl.ds(r, T), :] = shift_bins(low, step).astype(BF16)
         return carry
 
     lax.fori_loop(0, POS // T, body, 0)
     last = pad[POS : POS + 16, :]
     for d in range(3):
-        o_ref[0, d, POS : POS + 16, :] = shift_bins(last, sign * (d - 1)).astype(BF16)
+        o_ref[lead, d, POS : POS + 16, :] = shift_bins(last, sign * (d - 1)).astype(BF16)
 
 
 def window(e_ref, o_ref, df, db, r, n, lead=(0,)):
@@ -120,7 +124,6 @@
     cs, sn = trig_s[0, c], trig_s[1, c]
     T = 64
     zero = jnp.zeros((8, CH), F32)
-    gmat = group_matrix()
     inv_n = 1.0 / (rows * (CH // GROUPS)).astype(F32)
 
     def first(i, carry):
@@ -134,7 +137,7 @@
         return (s0 + fold8(x), s1 + fold8(g))
 
     s0, s1 = lax.fori_loop(0, POS // T, first, (zero, zero))
-    mean = group_sums(s0, gmat) * inv_n
+    mean = group_sums(s0) * inv_n
 
     def second(i, s):
         r = pl.multiple_of(i * T, T)
@@ -143,7 +146,7 @@
         return s + fold8(d * d)
 
     s2 = lax.fori_loop(0, POS // T, second, zero)
-    rstd = lax.rsqrt(group_sums(s2, gmat) * inv_n + eps)
+    rstd = lax.rsqrt(group_sums(s2) * inv_n + eps)
     stats[0] = jnp.concatenate([mean, rstd, jnp.zeros((6, CH), F32)], axis=0)
     obias[0] = s1
 
@@ -269,7 +272,6 @@
     R = 256
     T = 64
     zero = jnp.zeros((8, CH), F32)
-    gmat = group_matrix()
     inv_n = 1.0 / (rows * (CH // GROUPS)).astype(F32)
     temb = nn(emb[0], mat(w, TEMB0, 4, 4))[0:1] * INV_WIDTH
     add = temb + params[2:3]
@@ -285,7 +287,7 @@
         return s + fold8(jnp.where(row_iota(r, R) < rows, v, 0.0))
 
     s = lax.fori_loop(0, POS // R, tile, zero)
-    mean = group_sums(s, gmat) * inv_n
+    mean = group_sums(s) * inv_n
 
     def second(i, s):
         r = pl.multiple_of(i * T, T)
@@ -293,7 +295,7 @@
         return s + fold8(d * d)
 
     s2 = lax.fori_loop(0, POS // T, second, zero)
-    rstd = lax.rsqrt(group_sums(s2, gmat) * inv_n + eps)
+    rstd = lax.rsqrt(group_sums(s2) * inv_n + eps)
     scale = rstd * params[3:4]
     shift = params[4:5]
 
@@ -363,72 +365,98 @@
 def attn_kernel(
     frames_s, normed, tokens, tok_t, kmask, outlow, res, params, w,
     block_out, dq_ref, dw_ref,
-    q_s, do_s, kv_s, qt_s, dot_s, mixed_s, dkt_s, dvt_s, dkv_acc,
+    q_s, do_s, qt_s, dot_s, mixed_s, dkt_s, dvt_s, dkv_acc, km_s, s_s, dp_s, pb_s, ds_s, odq_s, dw_s,
 ):
     c = pl.program_id(0)
     rows = frames_s[c] * BINS
     R = 256
-    query_w = mat(w, SQ, 4, 4)
-    out_w = mat(w, 2 * SQ, 4, 4)
-    key_w = mat(w, 3 * SQ, CTX // BS, 4)
-    value_w = mat(w, 3 * SQ + KV, CTX // BS, 4)
-
+    C = 32
     def project(i, carry):
         r = pl.multiple_of(i * R, R)
-        q = (nn(normed[0, pl.ds(r, R), :], query_w) * INV_WIDTH).astype(BF16)
+        q = (nn(normed[0, pl.ds(r, R), :], mat(w, SQ, 4, 4)) * INV_WIDTH).astype(BF16)
         q_s[pl.ds(r, R), :] = q
         qt_s[:, pl.ds(r, R)] = q.T
-        d = (nt(outlow[0, pl.ds(r, R), :], out_w) * OUT_SCALE).astype(BF16)
+        d = (nt(outlow[0, pl.ds(r, R), :], mat(w, 2 * SQ, 4, 4)) * OUT_SCALE).astype(BF16)
         do_s[pl.ds(r, R), :] = d
         dot_s[:, pl.ds(r, R)] = d.T
         return carry
 
     lax.fori_loop(0, POS // R, project, 0)
-    kv_s[0] = ((nn(tokens[0], key_w) * INV_CTX).astype(BF16).astype(F32) * ATT_SCALE).astype(BF16)
-    kv_s[1] = (nn(tokens[0], value_w) * INV_CTX).astype(BF16)
-    valid = kmask[0, 0:1, :] > 0.0
     lane = lax.broadcasted_iota(jnp.int32, (1, BS), 1)
     first = lane < HEADDIM
-
+    keys = ((nn(tokens[0], mat(w, 3 * SQ, CTX // BS, 4)) * INV_CTX).astype(BF16).astype(F32) * ATT_SCALE).astype(BF16)
+    values = (nn(tokens[0], mat(w, 3 * SQ + KV, CTX // BS, 4)) * INV_CTX).astype(BF16)
+    for slab in range(HEADS // 2):
+        for j, side in enumerate((keys, values)):
+            two = side[:, slab * BS : (slab + 1) * BS]
+            none = jnp.zeros_like(two)
+            km_s[slab, 2 * j] = jnp.where(first, two, none)
+            km_s[slab, 2 * j + 1] = jnp.where(first, none, two)
+    dkv_acc[...] = jnp.zeros_like(dkv_acc)
+    pb_s[1] = jnp.zeros(pb_s.shape[1:], BF16)
+    ds_s[1] = jnp.zeros(ds_s.shape[1:], BF16)
+    valid = kmask[0, 0:1, :] > 0.0
+    RA = s_s.shape[1]
+    tiles = POS // RA
+    steps = HEADS // 2 * tiles
+
+    def place(i):
+        slab = i // tiles
+        return slab, pl.ds(pl.multiple_of(slab * BS, BS), BS), pl.ds(pl.multiple_of(i % tiles * RA, RA), RA)
+
+    def scores(i, h):
+        slab, cols, at = place(i)
+        s_s[h] = nt(q_s[at, cols], km_s[slab, h])
+        dp_s[h] = nt(do_s[at, cols], km_s[slab, 2 + h])
+
+    def soften(h):
+        for j in range(RA // C):
+            part = slice(j * C, (j + 1) * C)
+            s = jnp.where(valid, s_s[h, part, :], -1000000000.0)
+            e = jnp.exp(s - jnp.max(s, axis=-1, keepdims=True))
+            p = e * (1.0 / jnp.sum(e, axis=-1, keepdims=True))
+            pb_s[h, part, :] = p.astype(BF16)
+            dp = dp_s[h, part, :]
+            delta = jnp.sum(p * dp, axis=-1, keepdims=True)
+            ds_s[h, part, :] = (p * (dp - delta)).astype(BF16)
+
+    def back(i, h):
+        slab, cols, at = place(i)
+        half = pl.ds(pl.multiple_of(slab * BS + h * HEADDIM, HEADDIM), HEADDIM)
+        mine = slice(h * HEADDIM, (h + 1) * HEADDIM)
+        pb, ds = pb_s[h], ds_s[h]
+        dkv_acc[slab, 0, mine, :] += nn(qt_s[half, at], ds)
+        dkv_acc[slab, 1, mine, :] += nn(dot_s[half, at], pb)
+        o, dq = nn(pb, km_s[slab, 2 + h]), nn(ds, km_s[slab, h])
+        if h == 0:
+            odq_s[0] = o
+            odq_s[1] = dq
+        else:
+            mixed_s[at, cols] = (odq_s[0] + o).astype(BF16)
+            dq_ref[0, at, cols] = (odq_s[1] + dq).astype(BF16)
+
+    scores(0, 0)
+
+    def step(i, carry):
+        back(jnp.maximum(i - 1, 0), 1)
+        scores(i, 1)
+        soften(0)
+        back(i, 0)
+        scores(jnp.minimum(i + 1, steps - 1), 0)
+        soften(1)
+        return carry
+
+    odq_s[...] = jnp.zeros_like(odq_s)
+    lax.fori_loop(0, steps, step, 0)
+    back(steps - 1, 1)
     for slab in range(HEADS // 2):
         cols = slice(slab * BS, (slab + 1) * BS)
-        k2, v2 = kv_s[0, :, cols], kv_s[1, :, cols]
-        none = jnp.zeros_like(k2)
-        ks = (jnp.where(first, k2, none), jnp.where(first, none, k2))
-        vs = (jnp.where(first, v2, none), jnp.where(first, none, v2))
-        dkv_acc[...] = jnp.zeros_like(dkv_acc)
-
-        def tile(i, carry):
-            r = pl.multiple_of(i * R, R)
-            q = q_s[pl.ds(r, R), cols]
-            d = do_s[pl.ds(r, R), cols]
-            o = jnp.zeros((R, BS), F32)
-            dq = jnp.zeros((R, BS), F32)
-            for h in range(2):
-                s = jnp.where(valid, nt(q, ks[h]), -1000000000.0)
-                e = jnp.exp(s - jnp.max(s, axis=-1, keepdims=True))
-                p = e * (1.0 / jnp.sum(e, axis=-1, keepdims=True))
-                pb = p.astype(BF16)
-                dp = nt(d, vs[h])
-                delta = jnp.sum(p * dp, axis=-1, keepdims=True)
-                ds = (p * (dp - delta)).astype(BF16)
-                o = o + nn(pb, vs[h])
-                dq = dq + nn(ds, ks[h])
-                half = slice(slab * BS + h * HEADDIM, slab * BS + (h + 1) * HEADDIM)
-                mine = slice(h * HEADDIM, (h + 1) * HEADDIM)
-                dkv_acc[0, mine, :] += nn(qt_s[half, pl.ds(r, R)], ds)
-                dkv_acc[1, mine, :] += nn(dot_s[half, pl.ds(r, R)], pb)
-            mixed_s[pl.ds(r, R), cols] = o.astype(BF16)
-            dq_ref[0, pl.ds(r, R), cols] = dq.astype(BF16)
-            return carry
-
-        lax.fori_loop(0, POS // R, tile, 0)
-        dkt_s[cols, :] = (dkv_acc[0] * ATT_SCALE).astype(BF16)
-        dvt_s[cols, :] = dkv_acc[1].astype(BF16)
+        dkt_s[cols, :] = (dkv_acc[slab, 0] * ATT_SCALE).astype(BF16)
+        dvt_s[cols, :] = dkv_acc[slab, 1].astype(BF16)
 
     def project_out(i, carry):
         r = pl.multiple_of(i * R, R)
-        proj = nn(mixed_s[pl.ds(r, R), :], out_w) * OUT_SCALE + params[5:6]
+        proj = nn(mixed_s[pl.ds(r, R), :], mat(w, 2 * SQ, 4, 4)) * OUT_SCALE + params[5:6]
         m = row_iota(r, R) < rows
         block_out[0, pl.ds(r, R), :] = jnp.where(m, res[0, pl.ds(r, R), :] + proj, 0.0)
         return carry
@@ -437,12 +465,24 @@
 
     @pl.when(c == 0)
     def _():
-        dw_ref[...] = jnp.zeros_like(dw_ref)
-
-    dw_ref[0:CH, :] += nn(normed[0].T, dq_ref[0])
-    dw_ref[CH : 2 * CH, :] += nn(mixed_s[...].T, outlow[0])
-    dw_ref[2 * CH : 2 * CH + CTX, :] += nt(tok_t[0], dkt_s[...])
-    dw_ref[2 * CH + CTX :, :] += nt(tok_t[0], dvt_s[...])
+        dw_s[...] = jnp.zeros_like(dw_s)
+
+    dw_s[0:CH, :] += nn(normed[0].T, dq_ref[0])
+    dw_s[CH : 2 * CH, :] += nn(mixed_s[...].T, outlow[0])
+    dw_s[2 * CH : 2 * CH + CTX, :] += nt(tok_t[0], dkt_s[...])
+    dw_s[2 * CH + CTX :, :] += nt(tok_t[0], dvt_s[...])
+
+    @pl.when(c == pl.num_programs(0) - 1)
+    def _():
+        def cut(i, carry):
+            r = pl.multiple_of(i * BS, BS)
+            scale = jnp.where(i < CH // BS, INV_WIDTH, jnp.where(i < 2 * CH // BS, OUT_SCALE, INV_CTX))
+            low = (dw_s[pl.ds(r, BS), :] * scale).astype(BF16)
+            for b in range(CH // BS):
+                dw_ref[i * (CH // BS) + b] = low[:, b * BS : (b + 1) * BS]
+            return carry
+
+        lax.fori_loop(0, dw_s.shape[0] // BS, cut, 0)
 
 
 def attention(frames, normed, tokens, tok_t, kmask, outlow, res, params, w):
@@ -454,7 +494,7 @@
         out_shape=(
             jax.ShapeDtypeStruct((n, POS, CH), F32),
             jax.ShapeDtypeStruct((n, POS, CH), BF16),
-            jax.ShapeDtypeStruct((2 * CH + 2 * CTX, CH), F32),
+            jax.ShapeDtypeStruct((NBLK - QUERY0, BS, BS), BF16),
         ),
         grid_spec=pltpu.PrefetchScalarGridSpec(
             num_scalar_prefetch=1,
@@ -476,18 +516,24 @@
             out_specs=[
                 per_clip((POS, CH)),
                 per_clip((POS, CH)),
-                pl.BlockSpec((2 * CH + 2 * CTX, CH), lambda *_: (0, 0)),
+                pl.BlockSpec((NBLK - QUERY0, BS, BS), lambda *_: (0, 0, 0)),
             ],
             scratch_shapes=[
                 pltpu.VMEM((POS, CH), BF16),
                 pltpu.VMEM((POS, CH), BF16),
-                pltpu.VMEM((2, ctx_len, CH), BF16),
                 pltpu.VMEM((CH, POS), BF16),
                 pltpu.VMEM((CH, POS), BF16),
                 pltpu.VMEM((POS, CH), BF16),
                 pltpu.VMEM((CH, ctx_len), BF16),
                 pltpu.VMEM((CH, ctx_len), BF16),
-                pltpu.VMEM((2, BS, ctx_len), F32),
+                pltpu.VMEM((HEADS // 2, 2, BS, ctx_len), F32),
+                pltpu.VMEM((HEADS // 2, 4, ctx_len, BS), BF16),
+                pltpu.VMEM((2, 256, ctx_len), F32),
+                pltpu.VMEM((2, 256, ctx_len), F32),
+                pltpu.VMEM((2, 256, ctx_len), BF16),
+                pltpu.VMEM((2, 256, ctx_len), BF16),
+                pltpu.VMEM((2, 256, BS), F32),
+                pltpu.VMEM((2 * CH + 2 * CTX, CH), F32),
             ],
         ),
         compiler_params=pltpu.CompilerParams(vmem_limit_bytes=VMEM_LIMIT),
@@ -500,165 +546,153 @@
     )(frames, normed, tokens, tok_t, kmask, outlow, res, params, w)
 
 
-def norm2_kernel(frames_s, dq_ref, res, stats, cot, params, w, rgrad, e_ref, o_ref, sums, ng_s, pad):
-    c = pl.program_id(0)
-    rows = frames_s[c] * BINS
-    R = 256
+def taps_kernel(
+    counts, frames_s, slots_s, owned_s, dq_ref, res, stats, cot, params, w, at, emb, dw_att,
+    rgrad, sums, e_out, o_out, *refs,
+):
+    outs, refs = refs[: len(counts)], refs[len(counts) :]
+    ng_s, pad, e_ref, o_ref, blocks, sem, sem_w = refs
+    n = e_ref.shape[0]
+    step = pl.program_id(0)
     T = 64
-    zero = jnp.zeros((8, CH), F32)
-    gmat = group_matrix()
-    inv_n = 1.0 / (rows * (CH // GROUPS)).astype(F32)
-    mean, rstd = stats[0, 0:1], stats[0, 1:2]
-    gain = params[3:4]
-    query_w = mat(w, 0, 4, 4)
-
-    def first(i, carry):
-        s0, s1 = carry
-        r = pl.multiple_of(i * R, R)
-        ng = nt(dq_ref[0, pl.ds(r, R), :], query_w) * INV_WIDTH
-        m = row_iota(r, R) < rows
-        ng = jnp.where(m, ng, 0.0)
-        ng_s[pl.ds(r, R), :] = ng
-        x = jnp.where(m, (res[0, pl.ds(r, R), :] - mean) * rstd, 0.0)
-        return (s0 + fold8(ng), s1 + fold8(ng * x))
-
-    s0, s1 = lax.fori_loop(0, POS // R, first, (zero, zero))
-    mh = group_sums(s0 * gain, gmat) * inv_n
-    mhx = group_sums(s1 * gain, gmat) * inv_n
-    pad[0:8, :] = zero
-    pad[8 + POS :, :] = zero
-
-    def second(i, s):
-        r = pl.multiple_of(i * T, T)
-        m = row_iota(r, T) < rows
-        x = (res[0, pl.ds(r, T), :] - mean) * rstd
-        d = rstd * (gain * ng_s[pl.ds(r, T), :] - mh - x * mhx)
-        g = jnp.where(m, cot[0, pl.ds(r, T), :] + d, 0.0)
-        rgrad[0, pl.ds(r, T), :] = g
-        pad[pl.ds(r + 8, T), :] = g
-        return s + fold8(g)
-
-    s2 = lax.fori_loop(0, POS // T, second, zero)
-    sums[0, 0:8] = s2
-    sums[0, 8:16] = s1
-    sums[0, 16:24] = s0
-    write_windows(pad, e_ref, o_ref, -1)
-
-
-def norm2_backward(frames, dq, res, stats, cot, params, w):
-    n = dq.shape[0]
-    return pl.pallas_call(
-        norm2_kernel,
-        out_shape=(
-            jax.ShapeDtypeStruct((n, POS, CH), F32),
-            jax.ShapeDtypeStruct((n, 3, POS, CH), BF16),
-            jax.ShapeDtypeStruct((n, 3, POS + 16, CH), BF16),
-            jax.ShapeDtypeStruct((n, 24, CH), F32),
-        ),
-        grid_spec=pltpu.PrefetchScalarGridSpec(
-            num_scalar_prefetch=1,
-            grid=(n,),
-            in_specs=[
-                per_clip((POS, CH)),
-                per_clip((POS, CH)),
-                per_clip((8, CH)),
-                per_clip((POS, CH)),
-                whole((8, CH)),
-                pl.BlockSpec((SQ, BS, BS), lambda *_: (QUERY0 // SQ, 0, 0), pipeline_mode=pl.Buffered(1)),
-            ],
-            out_specs=[
-                per_clip((POS, CH)),
-                per_clip((3, POS, CH)),
-                per_clip((3, POS + 16, CH)),
-                per_clip((24, CH)),
-            ],
-            scratch_shapes=[pltpu.VMEM((POS, CH), F32), pltpu.VMEM((POS + 16, CH), F32)],
-        ),
-        compiler_params=pltpu.CompilerParams(vmem_limit_bytes=VMEM_LIMIT),
-        cost_estimate=pl.CostEstimate(
-            flops=n * POS * CH * CH * 2, bytes_accessed=n * POS * CH * 26, transcendentals=0
-        ),
-        name="norm2_backward",
-    )(frames, dq, res, stats, cot, params, w)
-
-
-def tap_kernel(parts, table_s, at, emb, sums, dw_att, e_ref, o_ref, *refs):
-    outs, (blocks, sem) = refs[: 2 * parts], refs[2 * parts :]
-    n = e_ref.shape[0]
-    d = pl.program_id(0)
-    entries = table_s.shape[1]
-
-    def cut(value, first, stride):
+
+    @pl.when(step == 0)
+    def _():
+        blocks[NBLK] = jnp.zeros((BS, BS), BF16)
+        pltpu.make_async_copy(dw_att, blocks.at[pl.ds(QUERY0, NBLK - QUERY0)], sem.at[0]).start()
+
+    @pl.when(step < n)
+    def _():
+        rows = frames_s[step] * BINS
+        R = 256
+        zero = jnp.zeros((8, CH), F32)
+        inv_n = 1.0 / (rows * (CH // GROUPS)).astype(F32)
+        mean, rstd = stats[0, 0:1], stats[0, 1:2]
+        gain = params[3:4]
+
+        def first(i, carry):
+            s0, s1 = carry
+            r = pl.multiple_of(i * R, R)
+            ng = nt(dq_ref[0, pl.ds(r, R), :], mat(w, 0, 4, 4)) * INV_WIDTH
+            m = row_iota(r, R) < rows
+            ng = jnp.where(m, ng, 0.0)
+            ng_s[pl.ds(r, R), :] = ng
+            x = jnp.where(m, (res[0, pl.ds(r, R), :] - mean) * rstd, 0.0)
+            return (s0 + fold8(ng), s1 + fold8(ng * x))
+
+        s0, s1 = lax.fori_loop(0, POS // R, first, (zero, zero))
+        mh, mhx = group_sums(s0 * gain, s1 * gain)
+        scale, mh, mhx = rstd * gain, rstd * mh * inv_n, rstd * mhx * inv_n
+        pad[0:8, :] = zero
+        pad[8 + POS :, :] = zero
+
+        def second(i, s):
+            r = pl.multiple_of(i * T, T)
+            m = row_iota(r, T) < rows
+            x = (res[0, pl.ds(r, T), :] - mean) * rstd
+            d = scale * ng_s[pl.ds(r, T), :] - mh - x * mhx
+            g = jnp.where(m, cot[0, pl.ds(r, T), :] + d, 0.0)
+            rgrad[0, pl.ds(r, T), :] = g
+            pad[pl.ds(r + 8, T), :] = g
+            return s + fold8(g)
+
+        s2 = lax.fori_loop(0, POS // T, second, zero)
+        sums[pl.ds(step, 1)] = jnp.concatenate([s2, s1, s0], axis=0)[None]
+        write_windows(pad, e_ref, o_ref, -1, step)
+        pltpu.make_async_copy(e_ref.at[step], e_out.at[step], sem_w.at[2 * step]).start()
+        pltpu.make_async_copy(o_ref.at[step], o_out.at[step], sem_w.at[2 * step + 1]).start()
+
+    def cut(value, first):
         low = value.astype(BF16)
-        for a in range(value.shape[0] // BS):
+        for a in range(4):
             for b in range(4):
                 blocks[first + a * 4 + b] = low[a * BS : (a + 1) * BS, b * BS : (b + 1) * BS]
 
-    def send(lo, hi):
-        def one(i, carry):
-            for q in range(2 * parts):
-                @pl.when(table_s[0, i] == q)
-                def _():
-                    src = blocks.at[jnp.minimum(i, NBLK)]
-                    pltpu.make_async_copy(src, outs[q].at[table_s[1, i]], sem).start()
-
-            return carry
-
-        lax.fori_loop(lo, hi, one, 0)
-
-    for df in range(3):
-        acc = None
-        for c in range(n):
-            g = window(e_ref, o_ref, 2 - df, 0, 0, POS, (c,))
-            part = nn(at[:, c * POS : (c + 1) * POS], g)
-            acc = part if acc is None else acc + part
-        cut(acc * CONV_SCALE, (3 * df + d) * SQ, 4)
-        send((3 * df + d) * SQ, (3 * df + d + 1) * SQ)
-
-    @pl.when(d == 0)
+    @pl.when(step >= n)
+    def _():
+        d = step - n
+        for df in range(3):
+            acc = None
+            for c in range(n):
+                g = window(e_ref, o_ref, 2 - df, d, 0, POS, (c,))
+                part = nn(at[:, c * POS : (c + 1) * POS], g)
+                acc = part if acc is None else acc + part
+            cut(acc * CONV_SCALE, (3 * df + d) * SQ)
+
+    @pl.when(step == pl.num_programs(0) - 1)
     def _():
         rows = [jnp.sum(sums[c, 0:8], axis=0, keepdims=True) for c in range(n)]
         grad = jnp.concatenate(rows + [jnp.zeros((16 - n, CH), F32)], axis=0).astype(BF16)
         outer = lax.dot_general(emb[...], grad, (((0,), (0,)), ((), ())), preferred_element_type=F32)
-        cut(outer * INV_WIDTH, TEMB0, 4)
-        blocks[NBLK] = jnp.zeros((BS, BS), BF16)
-        cut(dw_att[0:CH] * INV_WIDTH, QUERY0, 4)
-        cut(dw_att[CH : 2 * CH] * OUT_SCALE, OUT0, 4)
-        cut(dw_att[2 * CH :] * INV_CTX, KEY0, 4)
-        send(TEMB0, entries)
-
-    @pl.when(d == pl.num_programs(0) - 1)
-    def _():
-        for out in outs:
-            pltpu.make_async_copy(out, out, sem).wait()
-
-
-def tap_gradients(table, at, emb, sums, dw_att, e, o, sizes):
-    n = e.shape[0]
-    parts = len(sizes) // 2
+        cut(outer * INV_WIDTH, TEMB0)
+        pltpu.make_async_copy(dw_att, blocks.at[pl.ds(QUERY0, NBLK - QUERY0)], sem.at[0]).wait()
+        start = sum(counts)
+        for q in reversed(range(len(counts))):
+            start -= counts[q]
+
+            def send(i, carry, q=q, start=start):
+                for u in range(8):
+                    t = i * 8 + u
+                    src = owned_s[slots_s[start + t]]
+                    pltpu.make_async_copy(blocks.at[src], outs[q].at[t], sem.at[1 + q]).start()
+                return carry
+
+            lax.fori_loop(0, counts[q] // 8, send, 0)
+        for c in range(n):
+            pltpu.make_async_copy(e_ref.at[c], e_out.at[c], sem_w.at[2 * c]).wait()
+            pltpu.make_async_copy(o_ref.at[c], o_out.at[c], sem_w.at[2 * c + 1]).wait()
+        for q, out in enumerate(outs):
+            pltpu.make_async_copy(out, out, sem.at[1 + q]).wait()
+
+
+def tap_gradients(frames, slots, owned, dq, res, stats, cot, params, w, at, emb, dw_att, counts):
+    n = dq.shape[0]
+
+    def of_clip(shape):
+        return pl.BlockSpec((1,) + shape, lambda i, *_: (jnp.minimum(i, n - 1),) + (0,) * len(shape))
+
+    any_space = pl.BlockSpec(memory_space=pl.ANY)
     return pl.pallas_call(
-        functools.partial(tap_kernel, parts),
-        out_shape=tuple(jax.ShapeDtypeStruct((s, BS, BS), BF16) for s in sizes),
+        functools.partial(taps_kernel, counts),
+        out_shape=(
+            jax.ShapeDtypeStruct((n, POS, CH), F32),
+            jax.ShapeDtypeStruct((n, 24, CH), F32),
+            jax.ShapeDtypeStruct((n, 3, POS, CH), BF16),
+            jax.ShapeDtypeStruct((n, 3, POS + 16, CH), BF16),
+        )
+        + tuple(jax.ShapeDtypeStruct((s, BS, BS), BF16) for s in counts),
         grid_spec=pltpu.PrefetchScalarGridSpec(
-            num_scalar_prefetch=1,
-            grid=(3,),
+            num_scalar_prefetch=3,
+            grid=(n + 3,),
             in_specs=[
+                of_clip((POS, CH)),
+                of_clip((POS, CH)),
+                of_clip((8, CH)),
+                of_clip((POS, CH)),
+                whole((8, CH)),
+                pl.BlockSpec((SQ, BS, BS), lambda *_: (QUERY0 // SQ, 0, 0), pipeline_mode=pl.Buffered(1)),
                 whole((CH, n * POS)),
                 whole((16, CH)),
-                whole(sums.shape),
-                whole(dw_att.shape),
-                pl.BlockSpec((n, 1, POS, CH), lambda d, *_: (0, d, 0, 0)),
-                pl.BlockSpec((n, 1, POS + 16, CH), lambda d, *_: (0, d, 0, 0)),
+                any_space,
             ],
-            out_specs=[pl.BlockSpec(memory_space=pl.ANY)] * len(sizes),
-            scratch_shapes=[pltpu.VMEM((NBLK + 1, BS, BS), BF16), pltpu.SemaphoreType.DMA(())],
+            out_specs=[of_clip((POS, CH)), pl.BlockSpec((n, 24, CH), lambda *_: (0, 0, 0)), any_space, any_space]
+            + [any_space] * len(counts),
+            scratch_shapes=[
+                pltpu.VMEM((POS, CH), F32),
+                pltpu.VMEM((POS + 16, CH), F32),
+                pltpu.VMEM((n, 3, POS, CH), BF16),
+                pltpu.VMEM((n, 3, POS + 16, CH), BF16),
+                pltpu.VMEM((NBLK + 1, BS, BS), BF16),
+                pltpu.SemaphoreType.DMA((1 + len(counts),)),
+                pltpu.SemaphoreType.DMA((2 * n,)),
+            ],
         ),
         compiler_params=pltpu.CompilerParams(vmem_limit_bytes=VMEM_LIMIT),
         cost_estimate=pl.CostEstimate(
-            flops=n * POS * CH * CH * 18, bytes_accessed=n * POS * CH * 14 + 20000000, transcendentals=0
+            flops=n * POS * CH * CH * 20, bytes_accessed=n * POS * CH * 30 + 20000000, transcendentals=0
         ),
         name="tap_gradients",
-    )(table, at, emb, sums, dw_att, e, o)
+    )(frames, slots, owned, dq, res, stats, cot, params, w, at, emb, dw_att)
 
 
 def input_kernel(clip, frames_s, e_ref, o_ref, inp, stats, rgrad, params, w, *refs):
@@ -668,7 +702,6 @@
     R = 256
     T = 64
     zero = jnp.zeros((8, CH), F32)
-    gmat = group_matrix()
     inv_n = 1.0 / (rows * (CH // GROUPS)).astype(F32)
     mean, rstd = stats[0, 0:1], stats[0, 1:2]
     gain, shift = params[0:1], params[1:2]
@@ -696,8 +729,8 @@
         return (s0 + fold8(dy), s1 + fold8(dy * x))
 
     s0, s1 = lax.fori_loop(0, POS // T, first, (zero, zero))
-    mh = group_sums(s0 * gain, gmat) * inv_n
-    mhx = group_sums(s1 * gain, gmat) * inv_n
+    mh, mhx = group_sums(s0 * gain, s1 * gain)
+    mh, mhx = mh * inv_n, mhx * inv_n
 
     def second(i, carry):
         r = pl.multiple_of(i * T, T)
@@ -750,11 +783,10 @@
     )(frames, e, o, inp, stats, rgrad, params, w, *before)
 
 
-def pad_kernel(n_data, table_s, obias, sums2, *refs):
-    sums1, (_, _, keep, send, blocks, sem) = refs[:-6], refs[-6:]
-    n_model = table_s.shape[1]
-    row_share = BS // n_data
-    width = CH // (n_data * n_model)
+def norm_grads_kernel(obias, sums2, *refs):
+    sums1, tiles = refs[:-1], refs[-1]
+    count = tiles.shape[0]
+    width = CH // count
     total = lambda v: jnp.sum(v, axis=0, keepdims=True)
     first = sums1[0][0]
     for v in sums1[1:]:
@@ -770,42 +802,23 @@
         axis=0,
     )
     lane = lax.broadcasted_iota(jnp.int32, (8, BS), 1)
-    copies = []
-    for m in range(n_model):
-        tiles = []
-        for d in range(n_data):
-            at = (d * n_model + m) * width
-            tile = grads[:, at // BS * BS : (at // BS + 1) * BS]
-            tile = pltpu.roll(tile, (BS - at % BS) % BS, 1)
-            tiles.append(jnp.where(lane < width, tile, 0.0))
-            if row_share > 8:
-                tiles.append(jnp.zeros((row_share - 8, BS), F32))
-        blocks[m] = jnp.concatenate(tiles, axis=0).astype(BF16)
-    for m in range(n_model):
-        for q, out in enumerate((keep, send)):
-            @pl.when(table_s[0, m] == q)
-            def _():
-                pltpu.make_async_copy(blocks.at[m], out.at[table_s[1, m]], sem).start()
-
-    pltpu.make_async_copy(blocks, blocks, sem).wait()
-
-
-def add_norm_grads(table, n_data, obias, sums2, sums1, keep, send):
+    for d in range(count):
+        at = d * width
+        tile = grads[:, at // BS * BS : (at // BS + 1) * BS]
+        tile = pltpu.roll(tile, (BS - at % BS) % BS, 1)
+        tiles[d] = jnp.where(lane < width, tile, 0.0)
+
+
+def norm_grad_tiles(count, obias, sums2, sums1):
     vm = pl.BlockSpec(memory_space=pltpu.VMEM)
-    any_space = pl.BlockSpec(memory_space=pl.ANY)
-    n = 3 + len(sums1)
     return pl.pallas_call(
-        functools.partial(pad_kernel, n_data),
-        out_shape=(
-            jax.ShapeDtypeStruct(keep.shape, BF16),
-            jax.ShapeDtypeStruct(send.shape, BF16),
-        ),
-        in_specs=[pl.BlockSpec(memory_space=pltpu.SMEM)] + [vm] * (n - 1) + [any_space] * 2,
-        out_specs=[any_space] * 2,
-        scratch_shapes=[pltpu.VMEM((table.shape[1], BS, BS), BF16), pltpu.SemaphoreType.DMA(())],
-        input_output_aliases={n: 0, n + 1: 1},
+        norm_grads_kernel,
+        out_shape=jax.ShapeDtypeStruct((count, 8, BS), F32),
+        in_specs=[vm] * (2 + len(sums1)),
+        out_specs=vm,
+        cost_estimate=pl.CostEstimate(flops=100000, bytes_accessed=400000, transcendentals=0),
         name="norm_grads",
-    )(table, obias, sums2, *sums1, keep, send)
+    )(obias, sums2, *sums1)
 
 
 def sinusoid(timesteps):
@@ -879,6 +892,7 @@
         in_specs=[pl.BlockSpec(memory_space=pltpu.SMEM), vm, vm, vm],
         out_specs=[vm, vm],
         scratch_shapes=[pltpu.VMEM((2 * near.shape[0],) + near.shape[1:], F32)],
+        cost_estimate=pl.CostEstimate(flops=300000, bytes_accessed=3000000, transcendentals=0),
         name="update_master",
     )(where, master, near, far)
 
@@ -929,14 +943,19 @@
     return lax.optimization_barrier((value,) + others)[0]
 
 
+def after_all(values, *others):
+    return list(lax.optimization_barrier(tuple(values) + others)[: len(values)])
+
+
 def gather_z(grid, shard):
     return [shard] + [grid.along_z(shard, -d) for d in range(1, grid.nz)]
 
 
-def gather_plane(grid, stack):
-    got = [stack] + [grid.along_plane(stack, 0, -d) for d in range(1, grid.sizes[0])]
-    stack = jnp.concatenate(got)
-    got = [stack] + [grid.along_plane(stack, 1, -d) for d in range(1, grid.sizes[1])]
+def gather_plane(grid, stack, stage):
+    return [stack] + [grid.along_plane(stack, stage, -d) for d in range(1, grid.sizes[stage])]
+
+
+def gather_core(grid, got):
     return got + [grid.along_core(v) for v in got]
 
 
@@ -964,17 +983,14 @@
     return add_low(keep, grid.along_core(send)).astype(BF16)
 
 
-def scatter_plane(grid, value, stage):
-    size = grid.sizes[stage]
-    value = value.reshape(size, -1, BS, BS)
-    got = [grid.along_plane(value[d], stage, d) for d in range(1, size)]
-    return add_low(value[0], *got).astype(BF16)
-
-
-def scatter_z(grid, value):
+def send_plane(grid, value, stage):
+    value = value.reshape(grid.sizes[stage], -1, BS, BS)
+    return [value[0]] + [grid.along_plane(value[d], stage, d) for d in range(1, value.shape[0])]
+
+
+def send_z(grid, value):
     value = value.reshape(grid.nz, -1, BS, BS)
-    got = [grid.along_z(value[d], d) for d in range(1, grid.nz)]
-    return add_low(value[0], *got)
+    return [value[0]] + [grid.along_z(value[d], d) for d in range(1, value.shape[0])]
 
 
 def body(
@@ -998,7 +1014,7 @@
     param_tiles = own_params.reshape(8, CH // BS, BS).transpose(1, 0, 2).reshape(-1, row_share, BS)
     skip = param_tiles.shape[0]
     master_low = master_blocks.astype(BF16)
-    cut = slot_count // 2
+    cut = slot_count * 3 // 10
     chunks = ((skip, 0, cut), (0, cut, slot_count - cut))
     ring0 = gather_z(grid, jnp.concatenate([param_tiles, master_low[:cut]]))
     ring1 = gather_z(grid, master_low[cut:])
@@ -1015,49 +1031,51 @@
 
     k = slot_count // n_data + 1
     padded = n_data * k
-    k0 = k // 2
-
-    def route(to_mp, to_slot):
-        to_dp, to_k = to_slot // k, to_slot % k
-        to_core = to_mp % 2
-        rel_core = (to_core + grid.c) % 2
-        dz = (to_dp // grid.ny - grid.z) % grid.nz
-        dy = (to_dp % grid.ny - grid.y) % grid.ny
-        dx = (to_mp // 2 - grid.x) % grid.nx
-        swap = (to_core == 1) if grid.split else jnp.zeros_like(to_core == 1)
-        d0, d1 = jnp.where(swap, dx, dy), jnp.where(swap, dy, dx)
-        part = (to_k >= k0).astype(jnp.int32)
-        k_part = jnp.where(part == 1, k - k0, k0)
-        index = ((d1 * grid.sizes[0] + d0) * grid.nz + dz) * k_part + to_k - part * k0
-        return rel_core * 2 + part, index
-
+    k0 = max(1, k // 4)
+
+    planes = grid.sizes[0] * grid.sizes[1]
+    half = n_model * padded // 2
+    counts, slot_list = [], []
+    for rel in range(2):
+        core = (grid.c + rel) % 2
+        for part, kk in ((0, k0), (1, k - k0)):
+            t = jnp.arange(half // k * kk, dtype=jnp.int32)
+            group, k_id = t // kk, t % kk + part * k0
+            if part == 1:
+                plane, dz = group // grid.nz, group % grid.nz
+            else:
+                plane, dz = group % planes, group // planes
+            to_dp, to_mp = grid.place(core, plane % grid.sizes[0], plane // grid.sizes[0], dz)
+            to_slot = to_dp * k + k_id
+            slot_list.append(jnp.where(to_slot < slot_count, to_mp * slot_count + to_slot, NBLK))
+            counts.append(half // k * kk)
+    slots = jnp.concatenate(slot_list)
+    owned = jnp.concatenate([owned_block, jnp.full((1,), NBLK, jnp.int32)])
+    counts = tuple(counts)
     block_ids = jnp.arange(NBLK, dtype=jnp.int32)
     slot_of_block = jnp.sum(
         jnp.where(owned_block[None, :] == block_ids[:, None], block_ids[None, :], 0), axis=1
     )
-    pad_ids = jnp.arange(n_model * (padded - slot_count), dtype=jnp.int32)
-    per = padded - slot_count
-    block_mp = jnp.concatenate([slot_of_block // slot_count, pad_ids // per])
-    block_slot = jnp.concatenate([slot_of_block % slot_count, pad_ids % per + slot_count])
-    table = jnp.stack(route(block_mp, block_slot))
-    model_ids = jnp.arange(n_model, dtype=jnp.int32)
-    pad_quarter, pad_index = route(model_ids, jnp.full((n_model,), padded - 1, jnp.int32))
-    pad_table = jnp.stack([pad_quarter // 2, pad_index])
-    half = n_model * padded // 2
-    sizes = tuple(half // k * kk for _ in range(2) for kk in (k0, k - k0))
     my_slots = lax.dynamic_slice_in_dim(slot_of_block, mp * slot_count, slot_count)
     from_mp = my_slots // slot_count
     where = (
         ((from_mp + grid.c) % 2 * grid.nx + (from_mp // 2 - grid.x) % grid.nx) * padded + my_slots % slot_count
     )
 
-    inp, outlow, stats1, obias = pre(frames, trig, clean_latent, noise_latent, out_cotangent)
-    stack0 = after(jnp.stack(ring0), stats1)
-    pieces = gather_plane(grid, stack0)
-    stack1 = after(jnp.stack(ring1), table, pad_table, where, dest, kmask, emb_rows, emb_pad, tok_t)
-    later = gather_plane(grid, stack1)
-    e1, o1, params = acts_windows(frames, inp, stats1, pieces)
+    stack0 = jnp.stack(ring0)
+    inp, outlow, stats1, obias = pre(after(frames, stack0), trig, clean_latent, noise_latent, out_cotangent)
+    got0 = jnp.concatenate(gather_plane(grid, stack0, 0))
+    stack1 = after(jnp.stack(ring1), stats1, got0)
+    got0 = gather_plane(grid, got0, 1)
+    pieces = gather_core(grid, got0)
+    got1 = jnp.concatenate(gather_plane(grid, stack1, 0))
+    got1 = after(got1, *got0[1:])
+    ready = after(frames, slots, owned, where, dest, kmask, emb_rows, emb_pad, tok_t)
+    e1, o1, params = acts_windows(ready, inp, stats1, pieces)
     at = e1[:, 1].reshape(-1, CH).T
+    got1 = gather_plane(grid, got1, 1)
+    got1 = [got1[0]] + [after(v, e1) for v in got1[1:]]
+    later = gather_core(grid, got1)
     e1 = after(e1, at)
     res, normed, stats2, blocks = conv_forward(
         frames, dest, e1, o1, inp, emb_rows, params, pieces + later, chunks
@@ -1065,27 +1083,37 @@
     block_output, dq, dw_att = attention(
         frames, normed, codec_tokens, tok_t, kmask, outlow, res, params, blocks
     )
-    rgrad, e2, o2, sums2 = norm2_backward(frames, dq, res, stats2, out_cotangent, params, blocks)
-    keep0, keep1, send0, send1 = tap_gradients(table, at, emb_pad, sums2, dw_att, e2, o2, sizes)
-
-    sums1, input_grad = [], None
-    value0 = keep0
-    for clip in range(clip_count):
-        if clip == 1:
-            value0 = scatter_core(grid, keep0, send0)
+    rgrad, sums2, e2, o2, keep0, keep1, send0, send1 = tap_gradients(
+        frames, slots, owned, dq, res, stats2, out_cotangent, params, blocks, at, emb_pad, dw_att, counts
+    )
+
+    value0 = scatter_core(grid, keep0, send0)
+    value1 = scatter_core(grid, keep1, send1)
+    ready = after(e2, value0, value1)
+    moved0 = send_z(grid, value0)
+    moved1 = send_plane(grid, value1, 1)
+    input_grad, part = input_backward(0, frames, ready, o2, inp, stats1, rgrad, params, blocks)
+    sums1 = [part]
+    moved = after_all(moved1 + moved0, part)
+    moved1, moved0 = moved[: len(moved1)], moved[len(moved1) :]
+    value1 = add_low(*moved1).astype(BF16)
+    value1 = add_low(*send_plane(grid, value1, 0)).astype(BF16)
+    moved1 = send_z(grid, value1)
+    value0 = add_low(*after_all(moved0, value1)).astype(BF16)
+    moved0 = send_plane(grid, value0, 1)
+    ready = after(e2, value0)
+    for clip in range(1, clip_count):
         input_grad, part = input_backward(
-            clip, frames, after(e2, value0), o2, inp, stats1, rgrad, params, blocks, input_grad
+            clip, frames, ready, o2, inp, stats1, rgrad, params, blocks, input_grad
         )
         sums1.append(part)
-    value0 = scatter_plane(grid, value0, 1)
-    keep1, send1 = add_norm_grads(pad_table, n_data, obias, sums2, sums1, keep1, send1)
-    value1 = scatter_core(grid, keep1, send1)
-    value0 = scatter_plane(grid, value0, 0)
-    value1 = scatter_plane(grid, value1, 1)
-    grad0 = scatter_z(grid, value0)
-    value1 = scatter_plane(grid, value1, 0)
-    grad1 = scatter_z(grid, value1)
-    full_grad = jnp.concatenate([grad0, grad1])
+    value0 = add_low(*after_all(moved0, part)).astype(BF16)
+    grad0 = add_low(*send_plane(grid, value0, 0))
+    grad1 = add_low(*after_all(moved1, part))
+    full_grad = jnp.concatenate([grad0.reshape(k0, BS, BS), grad1.reshape(k - k0, BS, BS)])
+    tiles = norm_grad_tiles(total_devices, obias, after(sums2, full_grad), sums1)
+    tiles = lax.all_to_all(tiles, ("dp", "mp"), 0, 0, tiled=True)
+    norm_grads = jnp.sum(tiles, axis=0)[:param_rows, :width]
 
     step, stats = owner_step(dp[None], full_grad, left_root, right_root, n_data, row_share)
     step = lax.all_to_all(step, "dp", 0, 0, tiled=True).reshape(padded, row_share, BS)
@@ -1098,7 +1126,6 @@
     owned_rows = stats[:slot_count, 0].astype(F32)
     new_left = 0.5 * left_stats + 0.5 * stats[:slot_count, 1].astype(F32)
     new_right = 0.5 * right_stats + 0.5 * stats[:slot_count, 2].astype(F32)
-    norm_grads = stats[padded - 1, 0, :param_rows, :width].astype(F32)
     small_rate = 0.5 / math.sqrt(clip_count * total_devices * POS)
     new_norm = norm_params - small_rate * norm_grads
     return (

time: 352 us -> 311 us (0.88)
  Pallas kernels: 195 us -> 164 us
  waiting for transfers between devices: 72.4 us -> 57.8 us
    ppermute x28, waiting for transfers between devices: 66.4 us -> 49.7 us  [permute(): return lax.ppermute(value, ('dp', 'mp'), pairs)]
    pallas_call x1, Pallas kernels: 68.8 us -> 52.1 us  [attention(): pl.pallas_call(attn_kernel, out_shape=(jax.ShapeDtypeStruct((n, POS, CH),...]
    pallas_call x3 -> x2, Pallas kernels: 40.2 us -> 29 us  [the longest x1 27.4 us: tap_gradients(): pl.pallas_call(functools.partial(taps_kernel, counts), out_shape=(jax.Sha...]
    ppermute x28, starting transfers between devices: 40.5 us -> 35.3 us  [permute(): return lax.ppermute(value, ('dp', 'mp'), pairs)]
    all_to_all x0 -> x1, starting transfers between devices: none -> 3.73 us  [body(): tiles = lax.all_to_all(tiles, ('dp', 'mp'), 0, 0, tiled=True)]
  transfers between devices with their start and end apart: 29 -> 30, of which waited for: 13 -> 11; matrix products, arithmetic and copies ran while one was open for 5% -> 7% of each run, Pallas kernels for 10% -> 19%
where the time goes in v3:
time: 311 us; the launch traced here: 310 us
  Pallas kernels  164 us (53%)
  waiting for transfers between devices  57.8 us (19%)
  starting transfers between devices  42.8 us (14%)
  other arithmetic  15.8 us (5%)
  local copies, waits for them, and re-layouts  15.3 us (5%)
  blocking collectives  13.7 us (4%)
    pallas_call x1, Pallas kernels, attention(): pl.pallas_call(attn_kernel, out_shape=(jax.ShapeDtypeStruct((n, POS, CH),...  52.1 us
    ppermute x28, waiting for transfers between devices, permute(): return lax.ppermute(value, ('dp', 'mp'), pairs)  49.7 us
    ppermute x28, starting transfers between devices, permute(): return lax.ppermute(value, ('dp', 'mp'), pairs)  35.3 us
    pallas_call x2, Pallas kernels, input_backward(): pl.pallas_call(functools.partial(input_kernel, clip), out_shape=(jax.Shap...  30.9 us
    pallas_call x1, Pallas kernels, tap_gradients(): pl.pallas_call(functools.partial(taps_kernel, counts), out_shape=(jax.Sha...  27.4 us
    pallas_call x1, Pallas kernels, conv_forward(): pl.pallas_call(functools.partial(conv_kernel, chunks), out_shape=(jax.Sha...  25.2 us
    all_to_all x1, blocking collectives, body(): lax.all_to_all(step, 'dp', 0, 0, tiled=True).reshape(padded, row_share, BS)  13.7 us
    pallas_call x1, Pallas kernels, acts_windows(): pl.pallas_call(acts_kernel, out_shape=(jax.ShapeDtypeStruct((n, 3, POS, C...  8.38 us
  transfers between devices with their start and end apart: 30, of which 11 were waited for; matrix products, arithmetic and copies ran while one was open for 7% of the time, Pallas kernels for 19%

profile of v3, /device:TPU:0, one launch (start us, length us, event | category | flops | bytes accessed | tf_op | source)
XLA Modules:
  0.0 310.2 jit_solution(5493235930045662258)
XLA Ops:
  2.8 4.1 %collective-permute-start.1 = (bf16[20,16,128]{2,1,0:T(8,128)(2,1)S(1)}, bf16[20,16,128]{2,1,0:T(8,128)(2,1)S(1)}, u32[]{:S(2)}, u32[]{:S(2)}) collective-permute-start(bf16[20,16,128]{2,1,0:T(8,128)(2,1)S(1)} %get-tuple-element.138), channel_id=1, source_target_pairs={{0,16},{1,17},{2,18},{3,19},{4,20},{5,21},{6,22},{7,23},{8,24},{9,... | collective-permute-start | bytes 245768 | tf_op jit(solution)/shard_map/ppermute | solution.py:920
  10.0 2.9 collective-permute-start.7
  17.3 8.4 %inputs_stats.1 = (f32[2,1024,512]{2,1,0:T(8,128)}, bf16[2,1024,512]{2,1,0:T(8,128)(2,1)}, f32[2,8,512]{2,1,0:T(8,128)}, f32[2,8,512]{2,1,0:T(8,128)}) custom-call(s32[2]{0:T(128)} %frames_s.11, f32[2,2]{1,0:T(2,128)} %pad_maximum_fusion.7.trig_s, f32[2,1024,512]{2,1,0:T(8,128)} %clean.1, f32[2,1024,512]{2,1,0:T(8,128)} %noise.1, f32[2,1024,512]{2,1,0:T(8,128)} %cot.3), custom_call_target="tpu_custom_call" | custom-call | flops 20971520 | bytes 18874368 | tf_op jit(solution)/shard_map/inputs_stats/pallas_call | solution.py:158
  30.5 14.5 %collective-permute-done.10 = bf16[4,42,16,128]{3,2,1,0:T(8,128)(2,1)S(1)} collective-permute-done((bf16[4,42,16,128]{3,2,1,0:T(8,128)(2,1)S(1)}, bf16[4,42,16,128]{3,2,1,0:T(8,128)(2,1)S(1)}, u32[]{:S(2)}, u32[]{:S(2)}) %collective-permute-start.10) | collective-permute-done | bytes 688160 | tf_op jit(solution)/shard_map/ppermute | solution.py:920
  54.0 8.4 %acts.1 = (bf16[2,3,1024,512]{3,2,1,0:T(8,128)(2,1)}, bf16[2,3,1040,512]{3,2,1,0:T(8,128)(2,1)}, f32[8,512]{1,0:T(8,128)}) custom-call(s32[2]{0:T(128)} %frames_s.11, f32[2,1024,512]{2,1,0:T(8,128)} %get-tuple-element.66.inp, f32[2,8,512]{2,1,0:T(8,128)} %get-tuple-element.67.stats, bf16[8,20,16,128]{3,2,1,0:T(8,128)(2,1)} %constant_dynamic-update-slice_fusion.refs_0_, ...), custom_call_target="tpu_custom_call" | custom-call | flops 31457280 | bytes 16777216 | tf_op jit(solution)/shard_map/acts/pallas_call | solution.py:209
  67.9 25.2 %conv_forward.1 = (f32[2,1024,512]{2,1,0:T(8,128)}, bf16[2,1024,512]{2,1,0:T(8,128)(2,1)}, f32[2,8,512]{2,1,0:T(8,128)}, bf16[240,128,128]{2,1,0:T(8,128)(2,1)}) custom-call(s32[2]{0:T(128)} %frames_s.11, s32[2,32]{1,0:T(2,128)} %pad_add_fusion.dest_s, bf16[2,3,1024,512]{3,2,1,0:T(8,128)(2,1)} %get-tuple-element.69.e_ref, ...), custom_call_target="tpu_custom_call" | custom-call | flops 9663676416 | bytes 28068672 | tf_op jit(solution)/shard_map/conv_forward/pallas_call | solution.py:326
  93.1 52.1 %attention.1 = (f32[2,1024,512]{2,1,0:T(8,128)}, bf16[2,1024,512]{2,1,0:T(8,128)(2,1)}, bf16[80,128,128]{2,1,0:T(8,128)(2,1)}) custom-call(s32[2]{0:T(128)} %frames_s.11, bf16[2,1024,512]{2,1,0:T(8,128)(2,1)} %get-tuple-element.75.normed, bf16[2,512,768]{2,1,0:T(8,128)(2,1)} %tokens.1, bf16[2,768,512]{2,1,0:T(8,128)(2,1)} %bitcast.86, ...), custom_call_target="tpu_custom_call" | custom-call | flops 19327352832 | bytes 16777216 | tf_op jit(solution)/shard_map/attention/pallas_call | solution.py:492
  145.2 27.4 %tap_gradients.1 = (f32[2,1024,512]{2,1,0:T(8,128)}, f32[2,24,512]{2,1,0:T(8,128)}, bf16[2,3,1024,512]{3,2,1,0:T(8,128)(2,1)}, bf16[2,3,1040,512]{3,2,1,0:T(8,12...) custom-call(s32[2]{0:T(128)} %frames_s.11, ...), custom_call_target="tpu_custom_call" | custom-call | flops 10737418240 | bytes 51457280 | tf_op jit(solution)/shard_map/tap_gradients/pallas_call | solution.py:655
  173.3 5.4 %collective-permute-done.14 = bf16[96,128,128]{2,1,0:T(8,128)(2,1)S(1)} collective-permute-done((bf16[96,128,128]{2,1,0:T(8,128)(2,1)}, bf16[96,128,128]{2,1,0:T(8,128)(2,1)S(1)}, u32[]{:S(2)}, u32[]{:S(2)}) %collective-permute-start.14) | collective-permute-done | bytes 3145760 | tf_op jit(solution)/shard_map/ppermute | solution.py:920
  178.7 3.2 %add_convert_fusion = bf16[96,128,128]{2,1,0:T(8,128)(2,1)S(1)} fusion(bf16[96,128,128]{2,1,0:T(8,128)(2,1)S(1)} %collective-permute-done.14, bf16[96,128,128]{2,1,0:T(8,128)(2,1)} %get-tuple-element.84), kind=kLoop, calls=%fused_computation | loop fusion | flops 6291456 | bytes 9437184 | tf_op jit(solution)/shard_map/convert_element_type | solution.py:983
  185.3 5.4 %collective-permute-start.19 = (bf16[8,128,128]{2,1,0:T(8,128)(2,1)}, bf16[8,128,128]{2,1,0:T(8,128)(2,1)S(1)}, u32[]{:S(2)}, u32[]{:S(2)}) collective-permute-start(bf16[8,128,128]{2,1,0:T(8,128)(2,1)} %get-tuple-element.123), channel_id=1, source_target_pairs={{0,24},{1,25},{2,26},{3,27},{4,28},{5,29},{6,30},{7,31},{8,0},{9,1... | collective-permute-start | bytes 786440 | tf_op jit(solution)/shard_map/ppermute | solution.py:920
  190.7 5.0 %collective-permute-start.18 = (bf16[8,128,128]{2,1,0:T(8,128)(2,1)}, bf16[8,128,128]{2,1,0:T(8,128)(2,1)S(1)}, u32[]{:S(2)}, u32[]{:S(2)}) collective-permute-start(bf16[8,128,128]{2,1,0:T(8,128)(2,1)} %get-tuple-element.124), channel_id=1, source_target_pairs={{0,16},{1,17},{2,18},{3,19},{4,20},{5,21},{6,22},{7,23},{8,24},{9,... | collective-permute-start | bytes 786440 | tf_op jit(solution)/shard_map/ppermute | solution.py:920
  197.8 15.5 %input_backward.2 = (f32[2,1024,512]{2,1,0:T(8,128)}, f32[1,16,512]{2,1,0:T(8,128)}) custom-call(s32[2]{0:T(128)} %frames_s.11, bf16[2,3,1024,512]{3,2,1,0:T(8,128)(2,1)} %get-tuple-element.102.e_ref, bf16[2,3,1040,512]{3,2,1,0:T(8,128)(2,1)} %get-tuple-element.89.o_ref, f32[2,1024,512]{2,1,0:T(8,128)} %get-tuple-element.66.inp, ...), custom_call_target="tpu_custom_call" | custom-call | flops 4831838208 | bytes 12582912 | tf_op jit(solution)/shard_map/input_backward/pallas_call | solution.py:755
  213.2 6.2 %collective-permute-done.18 = bf16[8,128,128]{2,1,0:T(8,128)(2,1)S(1)} collective-permute-done((bf16[8,128,128]{2,1,0:T(8,128)(2,1)}, bf16[8,128,128]{2,1,0:T(8,128)(2,1)S(1)}, u32[]{:S(2)}, u32[]{:S(2)}) %collective-permute-start.18) | collective-permute-done | bytes 262176 | tf_op jit(solution)/shard_map/ppermute | solution.py:920
  220.8 11.3 %collective-permute-done.20 = bf16[24,128,128]{2,1,0:T(8,128)(2,1)S(1)} collective-permute-done((bf16[24,128,128]{2,1,0:T(8,128)(2,1)S(1)}, bf16[24,128,128]{2,1,0:T(8,128)(2,1)S(1)}, u32[]{:S(2)}, u32[]{:S(2)}) %collective-permute-start.20) | collective-permute-done | bytes 786464 | tf_op jit(solution)/shard_map/ppermute | solution.py:920
  236.8 15.4 %input_backward.3 = (f32[2,1024,512]{2,1,0:T(8,128)}, f32[1,16,512]{2,1,0:T(8,128)}) custom-call(s32[2]{0:T(128)} %frames_s.11, bf16[2,3,1024,512]{3,2,1,0:T(8,128)(2,1)} %get-tuple-element.102.e_ref, bf16[2,3,1040,512]{3,2,1,0:T(8,128)(2,1)} %get-tuple-element.89.o_ref, f32[2,1024,512]{2,1,0:T(8,128)} %get-tuple-element.66.inp, ...), custom_call_target="tpu_custom_call", output_to_operand_aliasing={{0}: (8, {})} | custom-call | flops 4831838208 | bytes 12582912 | tf_op jit(solution)/shard_map/input_backward/pallas_call | solution.py:755
  253.3 3.3 %collective-permute-done.22 = bf16[2,128,128]{2,1,0:T(8,128)(2,1)S(1)} collective-permute-done((bf16[2,128,128]{2,1,0:T(8,128)(2,1)S(1)}, bf16[2,128,128]{2,1,0:T(8,128)(2,1)S(1)}, u32[]{:S(2)}, u32[]{:S(2)}) %collective-permute-start.22) | collective-permute-done | bytes 65568 | tf_op jit(solution)/shard_map/ppermute | solution.py:920
  259.1 3.7 %all-to-all-start.2 = ((f32[32,8,128]{2,1,0:T(8,128)}), f32[32,8,128]{2,1,0:T(8,128)S(1)}, u32[]{:S(2)}, u32[]{:S(2)}) async-start(f32[32,8,128]{2,1,0:T(8,128)} %norm_grads.1), calls=%async_computation.2 | async-start | bytes 262144 | tf_op jit(solution)/shard_map/all_to_all | solution.py:1115
  262.8 7.0 %owner_step.1 = (bf16[8,8,16,128]{3,2,1,0:T(8,128)(2,1)}, bf16[8,8,3,16,128]{4,3,2,1,0:T(8,128)(2,1)}) custom-call(s32[1]{0:T(128)} %bitcast.48.dp_s, f32[8,128,128]{2,1,0:T(8,128)} %pad_maximum_fusion.2.grad, f32[60,128,128]{2,1,0:T(8,128)} %left_root.1, f32[60,128,128]{2,1,0:T(8,128)} %right_root.1), custom_call_target="tpu_custom_call" | custom-call | flops 134217728 | bytes 2621440 | tf_op jit(solution)/shard_map/owner_step/pallas_call | solution.py:850
  271.1 13.7 %all_to_all.15 = bf16[8,8,16,128]{3,2,1,0:T(8,128)(2,1)S(1)} all-to-all(bf16[8,8,16,128]{3,2,1,0:T(8,128)(2,1)} %get-tuple-element.113), channel_id=1, replica_groups=mesh['dp'=8,'mp'=4] {'dp'}, dimensions={0} | all-to-all | bytes 524288 | tf_op jit(solution)/shard_map/all_to_all | solution.py:1119
  284.7 3.7 %all-to-all-start = ((bf16[8,8,3,16,128]{4,3,2,1,0:T(8,128)(2,1)}), bf16[8,8,3,16,128]{4,3,2,1,0:T(8,128)(2,1)S(1)}, u32[]{:S(2)}, u32[]{:S(2)}) async-start(bf16[8,8,3,16,128]{4,3,2,1,0:T(8,128)(2,1)} %get-tuple-element.112), calls=%async_computation | async-start | bytes 1572864 | tf_op jit(solution)/shard_map/all_to_all | solution.py:1124
  290.0 5.9 %collective-permute-done.26 = bf16[64,16,128]{2,1,0:T(8,128)(2,1)S(1)} collective-permute-done((bf16[64,16,128]{2,1,0:T(8,128)(2,1)S(1)}, bf16[64,16,128]{2,1,0:T(8,128)(2,1)S(1)}, u32[]{:S(2)}, u32[]{:S(2)}) %collective-permute-start.26) | collective-permute-done | bytes 262176 | tf_op jit(solution)/shard_map/ppermute | solution.py:920
  298.7 2.8 update_master.1
  301.5 6.8 %all-to-all-done = bf16[8,8,3,16,128]{4,3,2,1,0:T(8,128)(2,1)S(1)} async-done(((bf16[8,8,3,16,128]{4,3,2,1,0:T(8,128)(2,1)}), bf16[8,8,3,16,128]{4,3,2,1,0:T(8,128)(2,1)S(1)}, u32[]{:S(2)}, u32[]{:S(2)}) %all-to-all-start) | async-done | bytes 786464 | tf_op jit(solution)/shard_map/all_to_all | solution.py:1124
  (131 shorter events, 51.8 us)
Async XLA Ops:
  2.8 12.1 %collective-permute-start.1 = (bf16[20,16,128]{2,1,0:T(8,128)(2,1)S(1)}, bf16[20,16,128]{2,1,0:T(8,128)(2,1)S(1)}, u32[]{:S(2)}, u32[]{:S(2)}) collective-permute-start(bf16[20,16,128]{2,1,0:T(8,128)(2,1)S(1)} %get-tuple-element.138), channel_id=1, source_target_pairs={{0,16},{1,17},{2,18},{3,19},{4,20},{5,21},{6,22},{7,23},{8,24},{9,... | collective-permute-start | bytes 245768 | tf_op jit(solution)/shard_map/ppermute | solution.py:920
  6.9 8.0 %collective-permute-start = (bf16[20,16,128]{2,1,0:T(8,128)(2,1)S(1)}, bf16[20,16,128]{2,1,0:T(8,128)(2,1)S(1)}, u32[]{:S(2)}, u32[]{:S(2)}) collective-permute-start(bf16[20,16,128]{2,1,0:T(8,128)(2,1)S(1)} %get-tuple-element.138), channel_id=1, source_target_pairs={{0,24},{1,25},{2,26},{3,27},{4,28},{5,29},{6,30},{7,31},{8,0},{9,1... | collective-permute-start | bytes 245768 | tf_op jit(solution)/shard_map/ppermute | solution.py:920
  8.2 7.2 %collective-permute-start.2 = (bf16[20,16,128]{2,1,0:T(8,128)(2,1)S(1)}, bf16[20,16,128]{2,1,0:T(8,128)(2,1)S(1)}, u32[]{:S(2)}, u32[]{:S(2)}) collective-permute-start(bf16[20,16,128]{2,1,0:T(8,128)(2,1)S(1)} %get-tuple-element.138), channel_id=1, source_target_pairs={{0,8},{1,9},{2,10},{3,11},{4,12},{5,13},{6,14},{7,15},{8,16},{9,17... | collective-permute-start | bytes 245768 | tf_op jit(solution)/shard_map/ppermute | solution.py:920
  8.9 18.7 %collective-permute-start.8 = (bf16[42,16,128]{2,1,0:T(8,128)(2,1)S(1)}, bf16[42,16,128]{2,1,0:T(8,128)(2,1)S(1)}, u32[]{:S(2)}, u32[]{:S(2)}) collective-permute-start(bf16[42,16,128]{2,1,0:T(8,128)(2,1)S(1)} %get-tuple-element.136), channel_id=1, source_target_pairs={{0,16},{1,17},{2,18},{3,19},{4,20},{5,21},{6,22},{7,23},{8,24},{9,... | collective-permute-start | bytes 516104 | tf_op jit(solution)/shard_map/ppermute | solution.py:920
  10.0 17.6 %collective-permute-start.7 = (bf16[42,16,128]{2,1,0:T(8,128)(2,1)S(1)}, bf16[42,16,128]{2,1,0:T(8,128)(2,1)S(1)}, u32[]{:S(2)}, u32[]{:S(2)}) collective-permute-start(bf16[42,16,128]{2,1,0:T(8,128)(2,1)S(1)} %get-tuple-element.136), channel_id=1, source_target_pairs={{0,24},{1,25},{2,26},{3,27},{4,28},{5,29},{6,30},{7,31},{8,0},{9,1... | collective-permute-start | bytes 516104 | tf_op jit(solution)/shard_map/ppermute | solution.py:920
  14.9 12.8 %collective-permute-start.9 = (bf16[42,16,128]{2,1,0:T(8,128)(2,1)S(1)}, bf16[42,16,128]{2,1,0:T(8,128)(2,1)S(1)}, u32[]{:S(2)}, u32[]{:S(2)}) collective-permute-start(bf16[42,16,128]{2,1,0:T(8,128)(2,1)S(1)} %get-tuple-element.136), channel_id=1, source_target_pairs={{0,8},{1,9},{2,10},{3,11},{4,12},{5,13},{6,14},{7,15},{8,16},{9,17... | collective-permute-start | bytes 516104 | tf_op jit(solution)/shard_map/ppermute | solution.py:920
  15.5 12.2 %collective-permute-start.3 = (bf16[4,20,16,128]{3,2,1,0:T(8,128)(2,1)S(1)}, bf16[4,20,16,128]{3,2,1,0:T(8,128)(2,1)S(1)}, u32[]{:S(2)}, u32[]{:S(2)}) collective-permute-start(bf16[4,20,16,128]{3,2,1,0:T(8,128)(2,1)S(1)} %pad_maximum_fusion.4), channel_id=1, source_target_pairs={{0,4},{1,3},{2,6},{3,1},{4,0},{5,7},{6,2},{7,5},{8,12},{9,11},{10,... | collective-permute-start | bytes 983048 | tf_op jit(solution)/shard_map/ppermute | solution.py:920
  28.5 16.5 %collective-permute-start.10 = (bf16[4,42,16,128]{3,2,1,0:T(8,128)(2,1)S(1)}, bf16[4,42,16,128]{3,2,1,0:T(8,128)(2,1)S(1)}, u32[]{:S(2)}, u32[]{:S(2)}) collective-permute-start(bf16[4,42,16,128]{3,2,1,0:T(8,128)(2,1)S(1)} %pad_maximum_fusion.1), channel_id=1, source_target_pairs={{0,4},{1,3},{2,6},{3,1},{4,0},{5,7},{6,2},{7,5},{8,12},{9,11},{10,... | collective-permute-start | bytes 2064392 | tf_op jit(solution)/shard_map/ppermute | solution.py:920
  28.9 16.3 %collective-permute-start.4 = (bf16[8,20,16,128]{3,2,1,0:T(8,128)(2,1)}, bf16[8,20,16,128]{3,2,1,0:T(8,128)(2,1)}, u32[]{:S(2)}, u32[]{:S(2)}) collective-permute-start(bf16[8,20,16,128]{3,2,1,0:T(8,128)(2,1)} %constant_dynamic-update-slice_fusion.refs_0_), channel_id=1, source_target_pairs={{0,2},{1,5},{2,0},{3,7},{4,6},{5,1},{6,4},{7,3},{8,10},{9,13},{10,... | collective-permute-start | bytes 1966088 | tf_op jit(solution)/shard_map/ppermute | solution.py:920
  45.2 18.5 %collective-permute-start.11 = (bf16[8,42,16,128]{3,2,1,0:T(8,128)(2,1)S(1)}, bf16[8,42,16,128]{3,2,1,0:T(8,128)(2,1)}, u32[]{:S(2)}, u32[]{:S(2)}) collective-permute-start(bf16[8,42,16,128]{3,2,1,0:T(8,128)(2,1)S(1)} %pad_maximum_fusion.refs_4_), channel_id=1, source_target_pairs={{0,2},{1,5},{2,0},{3,7},{4,6},{5,1},{6,4},{7,3},{8,10},{9,13},{10,... | collective-permute-start | bytes 4128776 | tf_op jit(solution)/shard_map/ppermute | solution.py:920
  52.9 15.1 %collective-permute-start.12 = (bf16[8,42,16,128]{3,2,1,0:T(8,128)(2,1)S(1)}, bf16[8,42,16,128]{3,2,1,0:T(8,128)(2,1)}, u32[]{:S(2)}, u32[]{:S(2)}) collective-permute-start(bf16[8,42,16,128]{3,2,1,0:T(8,128)(2,1)S(1)} %pad_maximum_fusion.refs_4_), channel_id=1, source_target_pairs={{0,1},{1,0},{2,3},{3,2},{4,5},{5,4},{6,7},{7,6},{8,9},{9,8},{10,11... | collective-permute-start | bytes 4128776 | tf_op jit(solution)/shard_map/ppermute | solution.py:920
  173.2 10.9 %collective-permute-start.16 = (bf16[32,128,128]{2,1,0:T(8,128)(2,1)}, bf16[32,128,128]{2,1,0:T(8,128)(2,1)S(1)}, u32[]{:S(2)}, u32[]{:S(2)}) collective-permute-start(bf16[32,128,128]{2,1,0:T(8,128)(2,1)} %get-tuple-element.87), channel_id=1, source_target_pairs={{0,1},{1,0},{2,3},{3,2},{4,5},{5,4},{6,7},{7,6},{8,9},{9,8},{10,11... | collective-permute-start | bytes 3145736 | tf_op jit(solution)/shard_map/ppermute | solution.py:920
  183.3 36.1 %collective-permute-start.15 = (bf16[48,128,128]{2,1,0:T(8,128)(2,1)}, bf16[48,128,128]{2,1,0:T(8,128)(2,1)S(1)}, u32[]{:S(2)}, u32[]{:S(2)}) collective-permute-start(bf16[48,128,128]{2,1,0:T(8,128)(2,1)} %get-tuple-element.121), channel_id=1, source_target_pairs={{0,2},{1,5},{2,0},{3,7},{4,6},{5,1},{6,4},{7,3},{8,10},{9,13},{10,... | collective-permute-start | bytes 4718600 | tf_op jit(solution)/shard_map/ppermute | solution.py:920
  185.3 27.9 %collective-permute-start.19 = (bf16[8,128,128]{2,1,0:T(8,128)(2,1)}, bf16[8,128,128]{2,1,0:T(8,128)(2,1)S(1)}, u32[]{:S(2)}, u32[]{:S(2)}) collective-permute-start(bf16[8,128,128]{2,1,0:T(8,128)(2,1)} %get-tuple-element.123), channel_id=1, source_target_pairs={{0,24},{1,25},{2,26},{3,27},{4,28},{5,29},{6,30},{7,31},{8,0},{9,1... | collective-permute-start | bytes 786440 | tf_op jit(solution)/shard_map/ppermute | solution.py:920
  190.7 28.7 %collective-permute-start.18 = (bf16[8,128,128]{2,1,0:T(8,128)(2,1)}, bf16[8,128,128]{2,1,0:T(8,128)(2,1)S(1)}, u32[]{:S(2)}, u32[]{:S(2)}) collective-permute-start(bf16[8,128,128]{2,1,0:T(8,128)(2,1)} %get-tuple-element.124), channel_id=1, source_target_pairs={{0,16},{1,17},{2,18},{3,19},{4,20},{5,21},{6,22},{7,23},{8,24},{9,... | collective-permute-start | bytes 786440 | tf_op jit(solution)/shard_map/ppermute | solution.py:920
  195.8 23.7 %collective-permute-start.17 = (bf16[8,128,128]{2,1,0:T(8,128)(2,1)}, bf16[8,128,128]{2,1,0:T(8,128)(2,1)}, u32[]{:S(2)}, u32[]{:S(2)}) collective-permute-start(bf16[8,128,128]{2,1,0:T(8,128)(2,1)} %get-tuple-element.125), channel_id=1, source_target_pairs={{0,8},{1,9},{2,10},{3,11},{4,12},{5,13},{6,14},{7,15},{8,16},{9,17... | collective-permute-start | bytes 786440 | tf_op jit(solution)/shard_map/ppermute | solution.py:920
  220.0 12.1 %collective-permute-start.20 = (bf16[24,128,128]{2,1,0:T(8,128)(2,1)S(1)}, bf16[24,128,128]{2,1,0:T(8,128)(2,1)S(1)}, u32[]{:S(2)}, u32[]{:S(2)}) collective-permute-start(bf16[24,128,128]{2,1,0:T(8,128)(2,1)S(1)} %slice.117), channel_id=1, source_target_pairs={{0,4},{1,3},{2,6},{3,1},{4,0},{5,7},{6,2},{7,5},{8,12},{9,11},{10,... | collective-permute-start | bytes 2359304 | tf_op jit(solution)/shard_map/ppermute | solution.py:920
  233.5 18.7 %collective-permute-start.21 = (bf16[4,128,128]{2,1,0:T(8,128)(2,1)S(1)}, bf16[4,128,128]{2,1,0:T(8,128)(2,1)S(1)}, u32[]{:S(2)}, u32[]{:S(2)}) collective-permute-start(bf16[4,128,128]{2,1,0:T(8,128)(2,1)S(1)} %get-tuple-element.133), channel_id=1, source_target_pairs={{0,2},{1,5},{2,0},{3,7},{4,6},{5,1},{6,4},{7,3},{8,10},{9,13},{10,... | collective-permute-start | bytes 393224 | tf_op jit(solution)/shard_map/ppermute | solution.py:920
  234.7 18.4 %collective-permute-start.25 = (bf16[6,128,128]{2,1,0:T(8,128)(2,1)S(1)}, bf16[6,128,128]{2,1,0:T(8,128)(2,1)S(1)}, u32[]{:S(2)}, u32[]{:S(2)}) collective-permute-start(bf16[6,128,128]{2,1,0:T(8,128)(2,1)S(1)} %get-tuple-element.129), channel_id=1, source_target_pairs={{0,24},{1,25},{2,26},{3,27},{4,28},{5,29},{6,30},{7,31},{8,0},{9,1... | collective-permute-start | bytes 589832 | tf_op jit(solution)/shard_map/ppermute | solution.py:920
  234.7 18.4 %collective-permute-start.24 = (bf16[6,128,128]{2,1,0:T(8,128)(2,1)S(1)}, bf16[6,128,128]{2,1,0:T(8,128)(2,1)S(1)}, u32[]{:S(2)}, u32[]{:S(2)}) collective-permute-start(bf16[6,128,128]{2,1,0:T(8,128)(2,1)S(1)} %get-tuple-element.130), channel_id=1, source_target_pairs={{0,16},{1,17},{2,18},{3,19},{4,20},{5,21},{6,22},{7,23},{8,24},{9,... | collective-permute-start | bytes 589832 | tf_op jit(solution)/shard_map/ppermute | solution.py:920
  234.7 18.4 %collective-permute-start.23 = (bf16[6,128,128]{2,1,0:T(8,128)(2,1)S(1)}, bf16[6,128,128]{2,1,0:T(8,128)(2,1)S(1)}, u32[]{:S(2)}, u32[]{:S(2)}) collective-permute-start(bf16[6,128,128]{2,1,0:T(8,128)(2,1)S(1)} %get-tuple-element.131), channel_id=1, source_target_pairs={{0,8},{1,9},{2,10},{3,11},{4,12},{5,13},{6,14},{7,15},{8,16},{9,17... | collective-permute-start | bytes 589832 | tf_op jit(solution)/shard_map/ppermute | solution.py:920
  259.1 12.0 %all-to-all-start.2 = ((f32[32,8,128]{2,1,0:T(8,128)}), f32[32,8,128]{2,1,0:T(8,128)S(1)}, u32[]{:S(2)}, u32[]{:S(2)}) async-start(f32[32,8,128]{2,1,0:T(8,128)} %norm_grads.1), calls=%async_computation.2 | async-start | bytes 262144 | tf_op jit(solution)/shard_map/all_to_all | solution.py:1115
  284.7 23.6 %all-to-all-start = ((bf16[8,8,3,16,128]{4,3,2,1,0:T(8,128)(2,1)}), bf16[8,8,3,16,128]{4,3,2,1,0:T(8,128)(2,1)S(1)}, u32[]{:S(2)}, u32[]{:S(2)}) async-start(bf16[8,8,3,16,128]{4,3,2,1,0:T(8,128)(2,1)} %get-tuple-element.112), calls=%async_computation | async-start | bytes 1572864 | tf_op jit(solution)/shard_map/all_to_all | solution.py:1124
  288.4 7.4 %collective-permute-start.26 = (bf16[64,16,128]{2,1,0:T(8,128)(2,1)S(1)}, bf16[64,16,128]{2,1,0:T(8,128)(2,1)S(1)}, u32[]{:S(2)}, u32[]{:S(2)}) collective-permute-start(bf16[64,16,128]{2,1,0:T(8,128)(2,1)S(1)} %bitcast.87), channel_id=1, source_target_pairs={{0,2},{1,3},{2,0},{3,1},{4,6},{5,7},{6,4},{7,5},{8,10},{9,11},{10,... | collective-permute-start | bytes 786440 | tf_op jit(solution)/shard_map/ppermute | solution.py:920
  (19 other events, 182.8 us)

commit v4 on v3

--- a/solution.py
+++ b/solution.py
@@ -42,6 +42,7 @@
 F32 = jnp.float32
 BF16 = jnp.bfloat16
 VMEM_LIMIT = 60 * 1024 * 1024
+SMALL = pl.CostEstimate(flops=1000000, bytes_accessed=1000000, transcendentals=0)
 
 
 def nt(a, b):
@@ -167,7 +168,7 @@
             num_scalar_prefetch=2, grid=(n,), in_specs=[big, big, big], out_specs=[big, big, small, small]
         ),
         compiler_params=pltpu.CompilerParams(vmem_limit_bytes=VMEM_LIMIT),
-        cost_estimate=pl.CostEstimate(flops=n * POS * CH * 20, bytes_accessed=n * POS * CH * 18, transcendentals=0),
+        cost_estimate=SMALL,
         name="inputs_stats",
     )(frames, trig, clean, noise, cot)
 
@@ -232,9 +233,7 @@
             scratch_shapes=[pltpu.VMEM((POS + 16, CH), F32)],
         ),
         compiler_params=pltpu.CompilerParams(vmem_limit_bytes=VMEM_LIMIT),
-        cost_estimate=pl.CostEstimate(
-            flops=n * POS * CH * 30, bytes_accessed=n * POS * CH * 16, transcendentals=n * POS * CH
-        ),
+        cost_estimate=SMALL,
         name="acts",
     )(frames, inp, stats, *pieces)
 
@@ -695,16 +694,8 @@
     )(frames, slots, owned, dq, res, stats, cot, params, w, at, emb, dw_att)
 
 
-def input_kernel(clip, frames_s, e_ref, o_ref, inp, stats, rgrad, params, w, *refs):
-    out, sums, ag_s = refs[-3:]
-    c = clip
-    rows = frames_s[c] * BINS
+def transposed_conv(e_ref, o_ref, w, out):
     R = 256
-    T = 64
-    zero = jnp.zeros((8, CH), F32)
-    inv_n = 1.0 / (rows * (CH // GROUPS)).astype(F32)
-    mean, rstd = stats[0, 0:1], stats[0, 1:2]
-    gain, shift = params[0:1], params[1:2]
 
     def conv(i, carry):
         r = pl.multiple_of(i * R, R)
@@ -712,10 +703,56 @@
         for t in range(9):
             df, db = divmod(t, 3)
             acc = acc + nt(window(e_ref, o_ref, 2 - df, db, r, R), mat(w, t * SQ, 4, 4))
-        ag_s[pl.ds(r, R), :] = acc * CONV_SCALE
+        out[pl.ds(r, R), :] = acc * CONV_SCALE
         return carry
 
     lax.fori_loop(0, POS // R, conv, 0)
+
+
+def acts_grad_kernel(e_ref, o_ref, w, out):
+    transposed_conv(e_ref, o_ref, w, out)
+
+
+def acts_gradient(clip, e, o, w):
+    def of_clip(shape):
+        return pl.BlockSpec(
+            (1,) + shape, lambda *_: (clip,) + (0,) * len(shape), pipeline_mode=pl.Buffered(1)
+        )
+
+    return pl.pallas_call(
+        acts_grad_kernel,
+        out_shape=jax.ShapeDtypeStruct((POS, CH), F32),
+        grid=(1,),
+        in_specs=[
+            of_clip((3, POS, CH)),
+            of_clip((3, POS + 16, CH)),
+            pl.BlockSpec((TEMB0, BS, BS), lambda *_: (0, 0, 0), pipeline_mode=pl.Buffered(1)),
+        ],
+        out_specs=pl.BlockSpec((POS, CH), lambda *_: (0, 0)),
+        compiler_params=pltpu.CompilerParams(vmem_limit_bytes=VMEM_LIMIT),
+        cost_estimate=pl.CostEstimate(flops=POS * CH * CH * 18, bytes_accessed=POS * CH * 24, transcendentals=0),
+        name="acts_gradient",
+    )(e, o, w)
+
+
+def input_kernel(clip, frames_s, ag, inp, stats, rgrad, params, *refs):
+    out, sums, dy_s = refs[-3:]
+    norm1_backward(clip, frames_s, ag, inp, stats, rgrad, params, out, sums, dy_s)
+
+
+def clip_kernel(clip, frames_s, e_ref, o_ref, w, inp, stats, rgrad, params, *refs):
+    out, sums, dy_s = refs[-3:]
+    transposed_conv(e_ref, o_ref, w, dy_s)
+    norm1_backward(clip, frames_s, dy_s, inp, stats, rgrad, params, out, sums, dy_s)
+
+
+def norm1_backward(clip, frames_s, ag, inp, stats, rgrad, params, out, sums, dy_s):
+    rows = frames_s[clip] * BINS
+    T = 64
+    zero = jnp.zeros((8, CH), F32)
+    inv_n = 1.0 / (rows * (CH // GROUPS)).astype(F32)
+    mean, rstd = stats[0, 0:1], stats[0, 1:2]
+    gain, shift = params[0:1], params[1:2]
 
     def first(i, carry):
         s0, s1 = carry
@@ -724,19 +761,19 @@
         x = (inp[0, pl.ds(r, T), :] - mean) * rstd
         y = x * gain + shift
         sg = jax.nn.sigmoid(y)
-        dy = jnp.where(m, ag_s[pl.ds(r, T), :] * (sg * (1.0 + y * (1.0 - sg))), 0.0)
-        ag_s[pl.ds(r, T), :] = dy
+        dy = jnp.where(m, ag[pl.ds(r, T), :] * (sg * (1.0 + y * (1.0 - sg))), 0.0)
+        dy_s[pl.ds(r, T), :] = dy
         return (s0 + fold8(dy), s1 + fold8(dy * x))
 
     s0, s1 = lax.fori_loop(0, POS // T, first, (zero, zero))
     mh, mhx = group_sums(s0 * gain, s1 * gain)
-    mh, mhx = mh * inv_n, mhx * inv_n
+    scale, mh, mhx = rstd * gain, rstd * mh * inv_n, rstd * mhx * inv_n
 
     def second(i, carry):
         r = pl.multiple_of(i * T, T)
         m = row_iota(r, T) < rows
         x = (inp[0, pl.ds(r, T), :] - mean) * rstd
-        d = rstd * (gain * ag_s[pl.ds(r, T), :] - mh - x * mhx)
+        d = scale * dy_s[pl.ds(r, T), :] - mh - x * mhx
         out[0, pl.ds(r, T), :] = jnp.where(m, rgrad[0, pl.ds(r, T), :] + d, 0.0)
         return carry
 
@@ -745,11 +782,11 @@
     sums[0, 8:16] = s0
 
 
-def input_backward(clip, frames, e, o, inp, stats, rgrad, params, w, before=None):
+def input_backward(clip, frames, ag, inp, stats, rgrad, params, before=None):
     n = inp.shape[0]
 
     def of_clip(shape):
-        return pl.BlockSpec((1,) + shape, lambda i, *_: (clip,) + (0,) * len(shape))
+        return pl.BlockSpec((1,) + shape, lambda *_: (clip,) + (0,) * len(shape))
 
     before = () if before is None else (before,)
     return pl.pallas_call(
@@ -761,32 +798,60 @@
         grid_spec=pltpu.PrefetchScalarGridSpec(
             num_scalar_prefetch=1,
             grid=(1,),
+            in_specs=[whole((POS, CH)), of_clip((POS, CH)), of_clip((8, CH)), of_clip((POS, CH)), whole((8, CH))]
+            + [pl.BlockSpec(memory_space=pl.ANY)] * len(before),
+            out_specs=[of_clip((POS, CH)), pl.BlockSpec((1, 16, CH), lambda *_: (0, 0, 0))],
+            scratch_shapes=[pltpu.VMEM((POS, CH), F32)],
+        ),
+        input_output_aliases={6: 0} if before else {},
+        compiler_params=pltpu.CompilerParams(vmem_limit_bytes=VMEM_LIMIT),
+        cost_estimate=pl.CostEstimate(flops=POS * CH * 30, bytes_accessed=POS * CH * 20, transcendentals=POS * CH),
+        name="input_backward",
+    )(frames, ag, inp, stats, rgrad, params, *before)
+
+
+def whole_backward(clip, frames, e, o, w, inp, stats, rgrad, params, before):
+    n = inp.shape[0]
+
+    def of_clip(shape, **mode):
+        return pl.BlockSpec((1,) + shape, lambda *_: (clip,) + (0,) * len(shape), **mode)
+
+    once = {"pipeline_mode": pl.Buffered(1)}
+    return pl.pallas_call(
+        functools.partial(clip_kernel, clip),
+        out_shape=(
+            jax.ShapeDtypeStruct((n, POS, CH), F32),
+            jax.ShapeDtypeStruct((1, 16, CH), F32),
+        ),
+        grid_spec=pltpu.PrefetchScalarGridSpec(
+            num_scalar_prefetch=1,
+            grid=(1,),
             in_specs=[
-                of_clip((3, POS, CH)),
-                of_clip((3, POS + 16, CH)),
+                of_clip((3, POS, CH), **once),
+                of_clip((3, POS + 16, CH), **once),
+                pl.BlockSpec((TEMB0, BS, BS), lambda *_: (0, 0, 0), pipeline_mode=pl.Buffered(1)),
                 of_clip((POS, CH)),
                 of_clip((8, CH)),
                 of_clip((POS, CH)),
                 whole((8, CH)),
-                pl.BlockSpec((TEMB0, BS, BS), lambda *_: (0, 0, 0), pipeline_mode=pl.Buffered(1)),
-            ]
-            + [pl.BlockSpec(memory_space=pl.ANY)] * len(before),
+                pl.BlockSpec(memory_space=pl.ANY),
+            ],
             out_specs=[of_clip((POS, CH)), pl.BlockSpec((1, 16, CH), lambda *_: (0, 0, 0))],
             scratch_shapes=[pltpu.VMEM((POS, CH), F32)],
         ),
-        input_output_aliases={8: 0} if before else {},
+        input_output_aliases={8: 0},
         compiler_params=pltpu.CompilerParams(vmem_limit_bytes=VMEM_LIMIT),
         cost_estimate=pl.CostEstimate(
             flops=POS * CH * CH * 18, bytes_accessed=POS * CH * 24, transcendentals=POS * CH
         ),
-        name="input_backward",
-    )(frames, e, o, inp, stats, rgrad, params, w, *before)
-
-
-def norm_grads_kernel(obias, sums2, *refs):
-    sums1, tiles = refs[:-1], refs[-1]
-    count = tiles.shape[0]
-    width = CH // count
+        name="whole_backward",
+    )(frames, e, o, w, inp, stats, rgrad, params, before)
+
+
+def norm_grads_kernel(me_s, obias, sums2, *refs):
+    sums1, keep, send = refs[:-2], refs[-2], refs[-1]
+    nx, n_data = keep.shape[0], keep.shape[1]
+    width = CH // (2 * nx * n_data)
     total = lambda v: jnp.sum(v, axis=0, keepdims=True)
     first = sums1[0][0]
     for v in sums1[1:]:
@@ -802,23 +867,37 @@
         axis=0,
     )
     lane = lax.broadcasted_iota(jnp.int32, (8, BS), 1)
-    for d in range(count):
-        at = d * width
-        tile = grads[:, at // BS * BS : (at // BS + 1) * BS]
-        tile = pltpu.roll(tile, (BS - at % BS) % BS, 1)
-        tiles[d] = jnp.where(lane < width, tile, 0.0)
-
-
-def norm_grad_tiles(count, obias, sums2, sums1):
+    for x in range(nx):
+        far = lax.rem(x - me_s[0] + nx, nx)
+        for c in range(2):
+            tiles = []
+            for d in range(n_data):
+                at = (d * 2 * nx + x * 2 + c) * width
+                tile = grads[:, at // BS * BS : (at // BS + 1) * BS]
+                tile = pltpu.roll(tile, (BS - at % BS) % BS, 1)
+                tiles.append(jnp.where(lane < width, tile, 0.0)[None])
+            tiles = jnp.concatenate(tiles, axis=0)
+
+            @pl.when(me_s[1] == c)
+            def _():
+                keep[far] = tiles
+
+            @pl.when(me_s[1] != c)
+            def _():
+                send[far] = tiles
+
+
+def norm_grad_tiles(n_data, me, obias, sums2, sums1, n_model):
     vm = pl.BlockSpec(memory_space=pltpu.VMEM)
+    shape = jax.ShapeDtypeStruct((n_model // 2, n_data, 8, BS), F32)
     return pl.pallas_call(
         norm_grads_kernel,
-        out_shape=jax.ShapeDtypeStruct((count, 8, BS), F32),
-        in_specs=[vm] * (2 + len(sums1)),
-        out_specs=vm,
-        cost_estimate=pl.CostEstimate(flops=100000, bytes_accessed=400000, transcendentals=0),
+        out_shape=(shape, shape),
+        in_specs=[pl.BlockSpec(memory_space=pltpu.SMEM)] + [vm] * (2 + len(sums1)),
+        out_specs=[vm, vm],
+        cost_estimate=SMALL,
         name="norm_grads",
-    )(obias, sums2, *sums1)
+    )(me, obias, sums2, *sums1)
 
 
 def sinusoid(timesteps):
@@ -828,43 +907,83 @@
     return jnp.concatenate([jnp.sin(angles), jnp.cos(angles)], axis=-1)
 
 
-def step_kernel(dp_s, grad, left_root, right_root, step, stats):
-    g = grad[0]
-    low = g.astype(BF16)
+def step_kernel(split, dp_s, *refs):
+    first, second = refs[: split[0]], refs[split[0] : split[0] + split[1]]
+    left_root, right_root, step, stats = refs[sum(split) :]
+    k0, k1 = first[0].shape[0], second[0].shape[0]
     n_data, row_share = step.shape[0], step.shape[2]
-    left = nt(low, low)
-    right = lax.dot_general(low, low, (((0,), (0,)), ((), ())), preferred_element_type=F32)
-    side = nn(left_root[0].astype(BF16), low)
-    update = nn(side.astype(BF16), right_root[0].astype(BF16))
-    rate = learn_rate * lax.rsqrt(jnp.sum(update * update, keepdims=True) * (1.0 / (BS * BS)) + 1e-06)
-    step[:, 0] = (update * rate).reshape(n_data, row_share, BS).astype(BF16)
-    stats[:, 0, 0] = g.reshape(n_data, row_share, BS).astype(BF16)
-    stats[:, 0, 1] = left.reshape(n_data, row_share, BS).astype(BF16)
-    stats[:, 0, 2] = right.reshape(n_data, row_share, BS).astype(BF16)
-
-
-def owner_step(dp, grad, left_root, right_root, n_data, row_share):
-    k = grad.shape[0]
-    last = left_root.shape[0] - 1
-    root = pl.BlockSpec((1, BS, BS), lambda i, dp: (jnp.minimum(dp[0] * k + i, last), 0, 0))
+    offset = dp_s[1]
+    for i in range(k0 + k1):
+        parts = [r[i] for r in first] if i < k0 else [r[i - k0] for r in second]
+        g = add_low(*parts)
+        low = g.astype(BF16)
+        root = jnp.minimum(i + offset, left_root.shape[0] - 1)
+        left = nt(low, low)
+        right = lax.dot_general(low, low, (((0,), (0,)), ((), ())), preferred_element_type=F32)
+        side = nn(left_root[root].astype(BF16), low)
+        update = nn(side.astype(BF16), right_root[root].astype(BF16))
+        rate = learn_rate * lax.rsqrt(jnp.sum(update * update, keepdims=True) * (1.0 / (BS * BS)) + 1e-06)
+        step[:, i] = (update * rate).reshape(n_data, row_share, BS).astype(BF16)
+        for j, value in enumerate((g, left, right)):
+            stats[:, 3 * i + j] = value.reshape(n_data, row_share, BS).astype(BF16)
+    for j in range(16 // row_share):
+        stats[:, 3 * (k0 + k1) + j] = jnp.zeros((n_data, row_share, BS), BF16)
+
+
+def owner_step(dp, first, second, left_root, right_root, row_share):
+    first = [v.reshape(-1, BS, BS) for v in first]
+    second = [v.reshape(-1, BS, BS) for v in second]
+    k = first[0].shape[0] + second[0].shape[0]
+    n_data = BS // row_share
+    entries = 3 * k + 16 // row_share
+    start = jnp.minimum(dp * k, left_root.shape[0] - k)
+    where = jnp.concatenate([start, dp * k - start])
+    root = pl.BlockSpec((pl.Element(k), pl.Element(BS), pl.Element(BS)), lambda i, w: (w[0], 0, 0))
+    full = lambda shape: pl.BlockSpec(shape, lambda i, w: (0,) * len(shape))
     return pl.pallas_call(
-        step_kernel,
+        functools.partial(step_kernel, (len(first), len(second))),
         out_shape=(
             jax.ShapeDtypeStruct((n_data, k, row_share, BS), BF16),
-            jax.ShapeDtypeStruct((n_data, k, 3, row_share, BS), BF16),
+            jax.ShapeDtypeStruct((n_data, entries, row_share, BS), BF16),
         ),
         grid_spec=pltpu.PrefetchScalarGridSpec(
             num_scalar_prefetch=1,
-            grid=(k,),
-            in_specs=[pl.BlockSpec((1, BS, BS), lambda i, dp: (i, 0, 0)), root, root],
-            out_specs=[
-                pl.BlockSpec((n_data, 1, row_share, BS), lambda i, dp: (0, i, 0, 0)),
-                pl.BlockSpec((n_data, 1, 3, row_share, BS), lambda i, dp: (0, i, 0, 0, 0)),
-            ],
+            grid=(1,),
+            in_specs=[full(v.shape) for v in first + second] + [root, root],
+            out_specs=[full((n_data, k, row_share, BS)), full((n_data, entries, row_share, BS))],
         ),
         cost_estimate=pl.CostEstimate(flops=k * 8 * BS**3, bytes_accessed=k * BS * BS * 20, transcendentals=0),
         name="owner_step",
-    )(dp, grad, left_root, right_root)
+    )(where, *first, *second, left_root, right_root)
+
+
+def add_tiles_kernel(*refs):
+    tiles, (_, stats, pair, sem) = refs[:-4], refs[-4:]
+    tile = add_low(*[t[...] for t in tiles])
+    high = tile.astype(BF16)
+    both = jnp.concatenate([high, (tile - high.astype(F32)).astype(BF16)], axis=1)
+    count, row_share = pair.shape[1], pair.shape[2]
+    for j in range(count):
+        pair[:, j] = both[:, j * row_share : (j + 1) * row_share]
+    copy = pltpu.make_async_copy(pair, stats.at[:, pl.ds(stats.shape[1] - count, count)], sem)
+    copy.start()
+    copy.wait()
+
+
+def add_tiles(tiles, stats):
+    vm = pl.BlockSpec(memory_space=pltpu.VMEM)
+    any_space = pl.BlockSpec(memory_space=pl.ANY)
+    n_data, _, row_share, _ = stats.shape
+    return pl.pallas_call(
+        add_tiles_kernel,
+        out_shape=jax.ShapeDtypeStruct(stats.shape, BF16),
+        in_specs=[vm] * len(tiles) + [any_space],
+        out_specs=any_space,
+        scratch_shapes=[pltpu.VMEM((n_data, 16 // row_share, row_share, BS), BF16), pltpu.SemaphoreType.DMA(())],
+        input_output_aliases={len(tiles): 0},
+        cost_estimate=SMALL,
+        name="add_tiles",
+    )(*tiles, stats)
 
 
 def master_kernel(where_s, master, near, far, new, low, steps):
@@ -1031,7 +1150,7 @@
 
     k = slot_count // n_data + 1
     padded = n_data * k
-    k0 = max(1, k // 4)
+    k0 = max(1, k // 8)
 
     planes = grid.sizes[0] * grid.sizes[1]
     half = n_model * padded // 2
@@ -1063,13 +1182,13 @@
     )
 
     stack0 = jnp.stack(ring0)
-    inp, outlow, stats1, obias = pre(after(frames, stack0), trig, clean_latent, noise_latent, out_cotangent)
     got0 = jnp.concatenate(gather_plane(grid, stack0, 0))
-    stack1 = after(jnp.stack(ring1), stats1, got0)
+    stack1 = jnp.stack(after_all(ring1, got0))
     got0 = gather_plane(grid, got0, 1)
     pieces = gather_core(grid, got0)
     got1 = jnp.concatenate(gather_plane(grid, stack1, 0))
-    got1 = after(got1, *got0[1:])
+    inp, outlow, stats1, obias = pre(after(frames, stack1), trig, clean_latent, noise_latent, out_cotangent)
+    got1 = after(got1, stats1, *got0[1:])
     ready = after(frames, slots, owned, where, dest, kmask, emb_rows, emb_pad, tok_t)
     e1, o1, params = acts_windows(ready, inp, stats1, pieces)
     at = e1[:, 1].reshape(-1, CH).T
@@ -1092,36 +1211,47 @@
     ready = after(e2, value0, value1)
     moved0 = send_z(grid, value0)
     moved1 = send_plane(grid, value1, 1)
-    input_grad, part = input_backward(0, frames, ready, o2, inp, stats1, rgrad, params, blocks)
+    ag = acts_gradient(0, ready, o2, blocks)
+    moved = after_all(moved1 + moved0, ag)
+    moved1, moved0 = moved[: len(moved1)], moved[len(moved1) :]
+    value1 = add_low(*moved1).astype(BF16)
+    moved1 = send_plane(grid, value1, 0)
+    value0 = add_low(*moved0).astype(BF16)
+    moved0 = send_plane(grid, value0, 1)
+    input_grad, part = input_backward(0, after(frames, value1, value0), ag, inp, stats1, rgrad, params)
     sums1 = [part]
     moved = after_all(moved1 + moved0, part)
     moved1, moved0 = moved[: len(moved1)], moved[len(moved1) :]
     value1 = add_low(*moved1).astype(BF16)
-    value1 = add_low(*send_plane(grid, value1, 0)).astype(BF16)
     moved1 = send_z(grid, value1)
-    value0 = add_low(*after_all(moved0, value1)).astype(BF16)
-    moved0 = send_plane(grid, value0, 1)
-    ready = after(e2, value0)
+    value0 = add_low(*moved0).astype(BF16)
+    moved0 = send_plane(grid, value0, 0)
+    ready = after(e2, value1, value0)
     for clip in range(1, clip_count):
-        input_grad, part = input_backward(
-            clip, frames, ready, o2, inp, stats1, rgrad, params, blocks, input_grad
+        input_grad, part = whole_backward(
+            clip, frames, ready, o2, blocks, inp, stats1, rgrad, params, input_grad
         )
         sums1.append(part)
-    value0 = add_low(*after_all(moved0, part)).astype(BF16)
-    grad0 = add_low(*send_plane(grid, value0, 0))
-    grad1 = add_low(*after_all(moved1, part))
-    full_grad = jnp.concatenate([grad0.reshape(k0, BS, BS), grad1.reshape(k - k0, BS, BS)])
-    tiles = norm_grad_tiles(total_devices, obias, after(sums2, full_grad), sums1)
-    tiles = lax.all_to_all(tiles, ("dp", "mp"), 0, 0, tiled=True)
-    norm_grads = jnp.sum(tiles, axis=0)[:param_rows, :width]
-
-    step, stats = owner_step(dp[None], full_grad, left_root, right_root, n_data, row_share)
+    moved = after_all(moved1 + moved0, part)
+    moved1, moved0 = moved[: len(moved1)], moved[len(moved1) :]
+    tiles, tiles_sent = norm_grad_tiles(
+        n_data, jnp.stack([grid.x, grid.c]), after(obias, *moved1), sums2, sums1, n_model
+    )
+    step, stats = owner_step(dp[None], moved0, moved1, left_root, right_root, row_share)
+    tiles = tiles + after(grid.along_core(tiles_sent), step)
+    tiles = [tiles[0]] + [
+        grid.permute(tiles[d], lambda z, y, x, c, d=d: (z, y, x + d, c)) for d in range(1, grid.nx)
+    ]
     step = lax.all_to_all(step, "dp", 0, 0, tiled=True).reshape(padded, row_share, BS)
+    stats = add_tiles(after_all(tiles, step), stats)
     near = jnp.concatenate(
         [step] + [grid.permute(step, lambda z, y, x, c, d=d: (z, y, x - d, c)) for d in range(1, grid.nx)]
     )
     far = grid.along_core(near)
-    stats = lax.all_to_all(stats, "dp", 0, 0, tiled=True).reshape(padded, 3, row_share, BS)
+    stats = lax.all_to_all(stats, "dp", 0, 0, tiled=True)
+    tiles = jnp.sum(stats[:, 3 * k :].astype(F32), axis=0).reshape(16, BS)
+    norm_grads = (tiles[0:8] + tiles[8:16])[:param_rows, :width]
+    stats = stats[:, : 3 * k].reshape(padded, 3, row_share, BS)
     new_master, master_copy = update_master(where, master_blocks, near, far)
     owned_rows = stats[:slot_count, 0].astype(F32)
     new_left = 0.5 * left_stats + 0.5 * stats[:slot_count, 1].astype(F32)

time: 311 us -> 301 us (0.968)
  waiting for transfers between devices: 57.8 us -> 43.4 us
  blocking collectives: 13.7 us -> 0 us
  starting transfers between devices: 42.8 us -> 52.2 us
  local copies, waits for them, and re-layouts: 15.3 us -> 18.8 us
    pallas_call x2 -> x5, Pallas kernels: 8.62 us -> 34.4 us  [the longest x1 15.3 us: whole_backward(): pl.pallas_call(functools.partial(clip_kernel, clip), out_shape=(jax.Shape...]
    pallas_call x2 -> x1, Pallas kernels: 30.9 us -> 7.11 us  [input_backward(): pl.pallas_call(functools.partial(input_kernel, clip), out_shape=(jax.Shap...]
    ppermute x28 -> x30, waiting for transfers between devices: 49.7 us -> 35.9 us  [permute(): return lax.ppermute(value, ('dp', 'mp'), pairs)]
    all_to_all x1 -> x0, blocking collectives: 13.7 us -> none  [body(): lax.all_to_all(step, 'dp', 0, 0, tiled=True).reshape(padded, row_share, BS)]
    ppermute x28 -> x30, starting transfers between devices: 35.3 us -> 42.8 us  [permute(): return lax.ppermute(value, ('dp', 'mp'), pairs)]
    unnamed x30 -> x48, local copies, waits for them, and re-layouts: 5.42 us -> 7.62 us
  transfers between devices with their start and end apart: 30 -> 32, of which waited for: 11 -> 13; matrix products, arithmetic and copies ran while one was open for 7% -> 7% of each run, Pallas kernels for 19% -> 18%
where the time goes in v4:
time: 301 us; the launch traced here: 300 us
  Pallas kernels  166 us (55%)
  starting transfers between devices  52.2 us (17%)
  waiting for transfers between devices  43.4 us (14%)
  local copies, waits for them, and re-layouts  18.8 us (6%)
  other arithmetic  18.6 us (6%)
    pallas_call x1, Pallas kernels, attention(): pl.pallas_call(attn_kernel, out_shape=(jax.ShapeDtypeStruct((n, POS, CH),...  52 us
    ppermute x30, starting transfers between devices, permute(): return lax.ppermute(value, ('dp', 'mp'), pairs)  42.8 us
    ppermute x30, waiting for transfers between devices, permute(): return lax.ppermute(value, ('dp', 'mp'), pairs)  35.9 us
    pallas_call x1, Pallas kernels, tap_gradients(): pl.pallas_call(functools.partial(taps_kernel, counts), out_shape=(jax.Sha...  27.3 us
    pallas_call x1, Pallas kernels, conv_forward(): pl.pallas_call(functools.partial(conv_kernel, chunks), out_shape=(jax.Sha...  25.2 us
    pallas_call x1, Pallas kernels, whole_backward(): pl.pallas_call(functools.partial(clip_kernel, clip), out_shape=(jax.Shape...  15.3 us
    pallas_call x1, Pallas kernels, acts_gradient(): pl.pallas_call(acts_grad_kernel, out_shape=jax.ShapeDtypeStruct((POS, CH)...  11.2 us
    pallas_call x1, Pallas kernels, acts_windows(): pl.pallas_call(acts_kernel, out_shape=(jax.ShapeDtypeStruct((n, 3, POS, C...  8.58 us
  transfers between devices with their start and end apart: 32, of which 13 were waited for; matrix products, arithmetic and copies ran while one was open for 7% of the time, Pallas kernels for 18%

profile of v4, /device:TPU:0, one launch (start us, length us, event | category | flops | bytes accessed | tf_op | source)
XLA Modules:
  0.0 300.0 jit_solution(10257092414605441553)
XLA Ops:
  2.8 4.1 %collective-permute-start.4 = (bf16[20,16,128]{2,1,0:T(8,128)(2,1)S(1)}, bf16[20,16,128]{2,1,0:T(8,128)(2,1)S(1)}, u32[]{:S(2)}, u32[]{:S(2)}) collective-permute-start(bf16[20,16,128]{2,1,0:T(8,128)(2,1)S(1)} %get-tuple-element.156), channel_id=1, source_target_pairs={{0,16},{1,17},{2,18},{3,19},{4,20},{5,21},{6,22},{7,23},{8,24},{9,... | collective-permute-start | bytes 245768 | tf_op jit(solution)/shard_map/ppermute | solution.py:1039
  18.5 5.4 %collective-permute-done.6 = bf16[4,20,16,128]{3,2,1,0:T(8,128)(2,1)S(1)} collective-permute-done((bf16[4,20,16,128]{3,2,1,0:T(8,128)(2,1)S(1)}, bf16[4,20,16,128]{3,2,1,0:T(8,128)(2,1)S(1)}, u32[]{:S(2)}, u32[]{:S(2)}) %collective-permute-start.6) | collective-permute-done | bytes 327712 | tf_op jit(solution)/shard_map/ppermute | solution.py:1039
  29.5 8.4 %inputs_stats.1 = (f32[2,1024,512]{2,1,0:T(8,128)}, bf16[2,1024,512]{2,1,0:T(8,128)(2,1)}, f32[2,8,512]{2,1,0:T(8,128)}, f32[2,8,512]{2,1,0:T(8,128)}) custom-call(s32[2]{0:T(128)} %frames_s.10, f32[2,2]{1,0:T(2,128)} %pad_maximum_fusion.5.trig_s, f32[2,1024,512]{2,1,0:T(8,128)} %clean.1, f32[2,1024,512]{2,1,0:T(8,128)} %noise.1, f32[2,1024,512]{2,1,0:T(8,128)} %cot.3), custom_call_target="tpu_custom_call" | custom-call | flops 1000000 | bytes 1000000 | tf_op jit(solution)/shard_map/inputs_stats/pallas_call | solution.py:159
  52.4 8.6 %acts.1 = (bf16[2,3,1024,512]{3,2,1,0:T(8,128)(2,1)}, bf16[2,3,1040,512]{3,2,1,0:T(8,128)(2,1)}, f32[8,512]{1,0:T(8,128)}) custom-call(s32[2]{0:T(128)} %frames_s.10, f32[2,1024,512]{2,1,0:T(8,128)} %get-tuple-element.79.inp, f32[2,8,512]{2,1,0:T(8,128)} %get-tuple-element.80.stats, bf16[8,20,16,128]{3,2,1,0:T(8,128)(2,1)} %copy-done.2, ...), custom_call_target="tpu_custom_call" | custom-call | flops 1000000 | bytes 1000000 | tf_op jit(solution)/shard_map/acts/pallas_call | solution.py:210
  65.4 25.2 %conv_forward.1 = (f32[2,1024,512]{2,1,0:T(8,128)}, bf16[2,1024,512]{2,1,0:T(8,128)(2,1)}, f32[2,8,512]{2,1,0:T(8,128)}, bf16[240,128,128]{2,1,0:T(8,128)(2,1)}) custom-call(s32[2]{0:T(128)} %frames_s.10, s32[2,32]{1,0:T(2,128)} %pad_add_fusion.dest_s, bf16[2,3,1024,512]{3,2,1,0:T(8,128)(2,1)} %get-tuple-element.82.e_ref, ...), custom_call_target="tpu_custom_call" | custom-call | flops 9663676416 | bytes 28068672 | tf_op jit(solution)/shard_map/conv_forward/pallas_call | solution.py:325
  90.6 52.0 %attention.1 = (f32[2,1024,512]{2,1,0:T(8,128)}, bf16[2,1024,512]{2,1,0:T(8,128)(2,1)}, bf16[80,128,128]{2,1,0:T(8,128)(2,1)}) custom-call(s32[2]{0:T(128)} %frames_s.10, bf16[2,1024,512]{2,1,0:T(8,128)(2,1)} %get-tuple-element.87.normed, bf16[2,512,768]{2,1,0:T(8,128)(2,1)} %tokens.1, bf16[2,768,512]{2,1,0:T(8,128)(2,1)} %bitcast.98, ...), custom_call_target="tpu_custom_call" | custom-call | flops 19327352832 | bytes 16777216 | tf_op jit(solution)/shard_map/attention/pallas_call | solution.py:491
  142.6 27.3 %tap_gradients.1 = (f32[2,1024,512]{2,1,0:T(8,128)}, f32[2,24,512]{2,1,0:T(8,128)}, bf16[2,3,1024,512]{3,2,1,0:T(8,128)(2,1)}, bf16[2,3,1040,512]{3,2,1,0:T(8,12...) custom-call(s32[2]{0:T(128)} %frames_s.10, ...), custom_call_target="tpu_custom_call" | custom-call | flops 10737418240 | bytes 51457280 | tf_op jit(solution)/shard_map/tap_gradients/pallas_call | solution.py:654
  170.4 6.2 %collective-permute-done.14 = bf16[112,128,128]{2,1,0:T(8,128)(2,1)S(1)} collective-permute-done((bf16[112,128,128]{2,1,0:T(8,128)(2,1)}, bf16[112,128,128]{2,1,0:T(8,128)(2,1)S(1)}, u32[]{:S(2)}, u32[]{:S(2)}) %collective-permute-start.14) | collective-permute-done | bytes 3670048 | tf_op jit(solution)/shard_map/ppermute | solution.py:1039
  176.7 4.3 %add_convert_fusion = bf16[112,128,128]{2,1,0:T(8,128)(2,1)S(1)} fusion(bf16[112,128,128]{2,1,0:T(8,128)(2,1)S(1)} %collective-permute-done.14, bf16[112,128,128]{2,1,0:T(8,128)(2,1)} %get-tuple-element.96), kind=kLoop, calls=%fused_computation | loop fusion | flops 7340032 | bytes 11010048 | tf_op jit(solution)/shard_map/convert_element_type | solution.py:1102
  185.9 4.4 %collective-permute-start.19 = (bf16[4,128,128]{2,1,0:T(8,128)(2,1)}, bf16[4,128,128]{2,1,0:T(8,128)(2,1)S(1)}, u32[]{:S(2)}, u32[]{:S(2)}) collective-permute-start(bf16[4,128,128]{2,1,0:T(8,128)(2,1)} %get-tuple-element.149), channel_id=1, source_target_pairs={{0,24},{1,25},{2,26},{3,27},{4,28},{5,29},{6,30},{7,31},{8,0},{9,1... | collective-permute-start | bytes 393224 | tf_op jit(solution)/shard_map/ppermute | solution.py:1039
  190.3 3.4 %collective-permute-start.18 = (bf16[4,128,128]{2,1,0:T(8,128)(2,1)}, bf16[4,128,128]{2,1,0:T(8,128)(2,1)S(1)}, u32[]{:S(2)}, u32[]{:S(2)}) collective-permute-start(bf16[4,128,128]{2,1,0:T(8,128)(2,1)} %get-tuple-element.150), channel_id=1, source_target_pairs={{0,16},{1,17},{2,18},{3,19},{4,20},{5,21},{6,22},{7,23},{8,24},{9,... | collective-permute-start | bytes 393224 | tf_op jit(solution)/shard_map/ppermute | solution.py:1039
  193.7 11.2 %acts_gradient.1.ag = f32[1024,512]{1,0:T(8,128)} custom-call(bf16[2,3,1024,512]{3,2,1,0:T(8,128)(2,1)} %get-tuple-element.115.e_ref, bf16[2,3,1040,512]{3,2,1,0:T(8,128)(2,1)} %get-tuple-element.101.o_ref, bf16[240,128,128]{2,1,0:T(8,128)(2,1)} %get-tuple-element.90.w), custom_call_target="tpu_custom_call" | custom-call | flops 4831838208 | bytes 12582912 | tf_op jit(solution)/shard_map/acts_gradient/pallas_call | solution.py:722
  212.0 7.1 %input_backward.1 = (f32[2,1024,512]{2,1,0:T(8,128)}, f32[1,16,512]{2,1,0:T(8,128)}) custom-call(s32[2]{0:T(128)} %frames_s.10, f32[1024,512]{1,0:T(8,128)} %acts_gradient.1.ag, f32[2,1024,512]{2,1,0:T(8,128)} %get-tuple-element.79.inp, f32[2,8,512]{2,1,0:T(8,128)} %get-tuple-element.80.stats, f32[2,1024,512]{2,1,0:T(8,128)} %get-tuple-element.109.rgrad, ...), custom_call_target="tpu_custom_call" | custom-call | flops 15728640 | bytes 10485760 | tf_op jit(solution)/shard_map/input_backward/pallas_call | solution.py:792
  219.1 3.3 %collective-permute-done.20 = bf16[28,128,128]{2,1,0:T(8,128)(2,1)S(1)} collective-permute-done((bf16[28,128,128]{2,1,0:T(8,128)(2,1)S(1)}, bf16[28,128,128]{2,1,0:T(8,128)(2,1)S(1)}, u32[]{:S(2)}, u32[]{:S(2)}) %collective-permute-start.20) | collective-permute-done | bytes 917536 | tf_op jit(solution)/shard_map/ppermute | solution.py:1039
  225.0 3.3 %collective-permute-start.24 = (bf16[7,128,128]{2,1,0:T(8,128)(2,1)S(1)}, bf16[7,128,128]{2,1,0:T(8,128)(2,1)S(1)}, u32[]{:S(2)}, u32[]{:S(2)}) collective-permute-start(bf16[7,128,128]{2,1,0:T(8,128)(2,1)S(1)} %get-tuple-element.143), channel_id=1, source_target_pairs={{0,24},{1,25},{2,26},{3,27},{4,28},{5,29},{6,30},{7,31},{8,0},{9,1... | collective-permute-start | bytes 688136 | tf_op jit(solution)/shard_map/ppermute | solution.py:1039
  228.3 3.7 %collective-permute-start.23 = (bf16[7,128,128]{2,1,0:T(8,128)(2,1)S(1)}, bf16[7,128,128]{2,1,0:T(8,128)(2,1)S(1)}, u32[]{:S(2)}, u32[]{:S(2)}) collective-permute-start(bf16[7,128,128]{2,1,0:T(8,128)(2,1)S(1)} %get-tuple-element.144), channel_id=1, source_target_pairs={{0,16},{1,17},{2,18},{3,19},{4,20},{5,21},{6,22},{7,23},{8,24},{9,... | collective-permute-start | bytes 688136 | tf_op jit(solution)/shard_map/ppermute | solution.py:1039
  232.0 15.3 %whole_backward.1 = (f32[2,1024,512]{2,1,0:T(8,128)}, f32[1,16,512]{2,1,0:T(8,128)}) custom-call(s32[2]{0:T(128)} %frames_s.10, bf16[2,3,1024,512]{3,2,1,0:T(8,128)(2,1)} %get-tuple-element.115.e_ref, bf16[2,3,1040,512]{3,2,1,0:T(8,128)(2,1)} %get-tuple-element.101.o_ref, ...), custom_call_target="tpu_custom_call", output_to_operand_aliasing={{0}: (8, {})} | custom-call | flops 4831838208 | bytes 12582912 | tf_op jit(solution)/shard_map/whole_backward/pallas_call | solution.py:820
  247.4 3.7 %collective-permute-done.23.refs_4_ = bf16[7,128,128]{2,1,0:T(8,128)(2,1)S(1)} collective-permute-done((bf16[7,128,128]{2,1,0:T(8,128)(2,1)S(1)}, bf16[7,128,128]{2,1,0:T(8,128)(2,1)S(1)}, u32[]{:S(2)}, u32[]{:S(2)}) %collective-permute-start.23) | collective-permute-done | bytes 229408 | tf_op jit(solution)/shard_map/ppermute | solution.py:1039
  251.8 4.6 %owner_step.1 = (bf16[8,8,16,128]{3,2,1,0:T(8,128)(2,1)}, bf16[8,25,16,128]{3,2,1,0:T(8,128)(2,1)}) custom-call(s32[2]{0:T(128)} %pad_add_fusion.4.dp_s, bf16[1,128,128]{2,1,0:T(8,128)(2,1)} %get-tuple-element.128.refs_0_, bf16[1,128,128]{2,1,0:T(8,128)(2,1)} %copy-done.13, bf16[7,128,128]{2,1,0:T(8,128)(2,1)} %get-tuple-element.120.refs_2_, ...), custom_call_target="tpu_custom_call" | custom-call | flops 134217728 | bytes 2621440 | tf_op jit(solution)/shard_map/owner_step/pallas_call | solution.py:943
  256.4 3.4 %all-to-all-start = ((bf16[8,8,16,128]{3,2,1,0:T(8,128)(2,1)}), bf16[8,8,16,128]{3,2,1,0:T(8,128)(2,1)S(1)}, u32[]{:S(2)}, u32[]{:S(2)}) async-start(bf16[8,8,16,128]{3,2,1,0:T(8,128)(2,1)} %get-tuple-element.130), calls=%async_computation | async-start | bytes 524288 | tf_op jit(solution)/shard_map/all_to_all | solution.py:1245
  265.8 3.4 %collective-permute-done.27.refs_1_ = f32[8,8,128]{2,1,0:T(8,128)S(1)} collective-permute-done((f32[8,8,128]{2,1,0:T(8,128)S(1)}, f32[8,8,128]{2,1,0:T(8,128)S(1)}, u32[]{:S(2)}, u32[]{:S(2)}) %collective-permute-start.27) | collective-permute-done | bytes 32800 | tf_op jit(solution)/shard_map/ppermute | solution.py:1039
  271.2 5.9 %all-to-all-start.1 = ((bf16[8,25,16,128]{3,2,1,0:T(8,128)(2,1)}), bf16[8,25,16,128]{3,2,1,0:T(8,128)(2,1)S(1)}, u32[]{:S(2)}, u32[]{:S(2)}) async-start(bf16[8,25,16,128]{3,2,1,0:T(8,128)(2,1)} %add_tiles.1), calls=%async_computation.1 | async-start | bytes 1638400 | tf_op jit(solution)/shard_map/all_to_all | solution.py:1251
  277.7 6.4 %collective-permute-done.28 = bf16[64,16,128]{2,1,0:T(8,128)(2,1)S(1)} collective-permute-done((bf16[64,16,128]{2,1,0:T(8,128)(2,1)S(1)}, bf16[64,16,128]{2,1,0:T(8,128)(2,1)S(1)}, u32[]{:S(2)}, u32[]{:S(2)}) %collective-permute-start.28) | collective-permute-done | bytes 262176 | tf_op jit(solution)/shard_map/ppermute | solution.py:1039
  289.8 7.5 %all-to-all-done.1 = bf16[8,25,16,128]{3,2,1,0:T(8,128)(2,1)S(1)} async-done(((bf16[8,25,16,128]{3,2,1,0:T(8,128)(2,1)}), bf16[8,25,16,128]{3,2,1,0:T(8,128)(2,1)S(1)}, u32[]{:S(2)}, u32[]{:S(2)}) %all-to-all-start.1) | async-done | bytes 819232 | tf_op jit(solution)/shard_map/all_to_all | solution.py:1251
  (157 shorter events, 70.6 us)
Async XLA Ops:
  2.8 11.2 %collective-permute-start.4 = (bf16[20,16,128]{2,1,0:T(8,128)(2,1)S(1)}, bf16[20,16,128]{2,1,0:T(8,128)(2,1)S(1)}, u32[]{:S(2)}, u32[]{:S(2)}) collective-permute-start(bf16[20,16,128]{2,1,0:T(8,128)(2,1)S(1)} %get-tuple-element.156), channel_id=1, source_target_pairs={{0,16},{1,17},{2,18},{3,19},{4,20},{5,21},{6,22},{7,23},{8,24},{9,... | collective-permute-start | bytes 245768 | tf_op jit(solution)/shard_map/ppermute | solution.py:1039
  6.9 9.9 %collective-permute-start.3 = (bf16[20,16,128]{2,1,0:T(8,128)(2,1)S(1)}, bf16[20,16,128]{2,1,0:T(8,128)(2,1)S(1)}, u32[]{:S(2)}, u32[]{:S(2)}) collective-permute-start(bf16[20,16,128]{2,1,0:T(8,128)(2,1)S(1)} %get-tuple-element.156), channel_id=1, source_target_pairs={{0,24},{1,25},{2,26},{3,27},{4,28},{5,29},{6,30},{7,31},{8,0},{9,1... | collective-permute-start | bytes 245768 | tf_op jit(solution)/shard_map/ppermute | solution.py:1039
  8.2 8.5 %collective-permute-start.5 = (bf16[20,16,128]{2,1,0:T(8,128)(2,1)S(1)}, bf16[20,16,128]{2,1,0:T(8,128)(2,1)S(1)}, u32[]{:S(2)}, u32[]{:S(2)}) collective-permute-start(bf16[20,16,128]{2,1,0:T(8,128)(2,1)S(1)} %get-tuple-element.156), channel_id=1, source_target_pairs={{0,8},{1,9},{2,10},{3,11},{4,12},{5,13},{6,14},{7,15},{8,16},{9,17... | collective-permute-start | bytes 245768 | tf_op jit(solution)/shard_map/ppermute | solution.py:1039
  8.9 16.7 %collective-permute-start.2 = (bf16[42,16,128]{2,1,0:T(8,128)(2,1)S(1)}, bf16[42,16,128]{2,1,0:T(8,128)(2,1)S(1)}, u32[]{:S(2)}, u32[]{:S(2)}) collective-permute-start(bf16[42,16,128]{2,1,0:T(8,128)(2,1)S(1)} %slice.134), channel_id=1, source_target_pairs={{0,8},{1,9},{2,10},{3,11},{4,12},{5,13},{6,14},{7,15},{8,16},{9,17... | collective-permute-start | bytes 516104 | tf_op jit(solution)/shard_map/ppermute | solution.py:1039
  10.5 15.7 %collective-permute-start.1 = (bf16[42,16,128]{2,1,0:T(8,128)(2,1)S(1)}, bf16[42,16,128]{2,1,0:T(8,128)(2,1)S(1)}, u32[]{:S(2)}, u32[]{:S(2)}) collective-permute-start(bf16[42,16,128]{2,1,0:T(8,128)(2,1)S(1)} %slice.134), channel_id=1, source_target_pairs={{0,16},{1,17},{2,18},{3,19},{4,20},{5,21},{6,22},{7,23},{8,24},{9,... | collective-permute-start | bytes 516104 | tf_op jit(solution)/shard_map/ppermute | solution.py:1039
  14.0 12.3 %collective-permute-start = (bf16[42,16,128]{2,1,0:T(8,128)(2,1)S(1)}, bf16[42,16,128]{2,1,0:T(8,128)(2,1)S(1)}, u32[]{:S(2)}, u32[]{:S(2)}) collective-permute-start(bf16[42,16,128]{2,1,0:T(8,128)(2,1)S(1)} %slice.134), channel_id=1, source_target_pairs={{0,24},{1,25},{2,26},{3,27},{4,28},{5,29},{6,30},{7,31},{8,0},{9,1... | collective-permute-start | bytes 516104 | tf_op jit(solution)/shard_map/ppermute | solution.py:1039
  16.8 7.1 %collective-permute-start.6 = (bf16[4,20,16,128]{3,2,1,0:T(8,128)(2,1)S(1)}, bf16[4,20,16,128]{3,2,1,0:T(8,128)(2,1)S(1)}, u32[]{:S(2)}, u32[]{:S(2)}) collective-permute-start(bf16[4,20,16,128]{3,2,1,0:T(8,128)(2,1)S(1)} %pad_maximum_fusion.2), channel_id=1, source_target_pairs={{0,4},{1,3},{2,6},{3,1},{4,0},{5,7},{6,2},{7,5},{8,12},{9,11},{10,... | collective-permute-start | bytes 983048 | tf_op jit(solution)/shard_map/ppermute | solution.py:1039
  24.0 16.8 %collective-permute-start.7 = (bf16[8,20,16,128]{3,2,1,0:T(8,128)(2,1)S(1)}, bf16[8,20,16,128]{3,2,1,0:T(8,128)(2,1)}, u32[]{:S(2)}, u32[]{:S(2)}) collective-permute-start(bf16[8,20,16,128]{3,2,1,0:T(8,128)(2,1)S(1)} %constant_dynamic-update-slice_fusion.refs_0_), channel_id=1, source_target_pairs={{0,2},{1,5},{2,0},{3,7},{4,6},{5,1},{6,4},{7,3},{8,10},{9,13},{10,... | collective-permute-start | bytes 1966088 | tf_op jit(solution)/shard_map/ppermute | solution.py:1039
  27.0 12.8 %collective-permute-start.10 = (bf16[4,42,16,128]{3,2,1,0:T(8,128)(2,1)S(1)}, bf16[4,42,16,128]{3,2,1,0:T(8,128)(2,1)S(1)}, u32[]{:S(2)}, u32[]{:S(2)}) collective-permute-start(bf16[4,42,16,128]{3,2,1,0:T(8,128)(2,1)S(1)} %pad_maximum_fusion), channel_id=1, source_target_pairs={{0,4},{1,3},{2,6},{3,1},{4,0},{5,7},{6,2},{7,5},{8,12},{9,11},{10,... | collective-permute-start | bytes 2064392 | tf_op jit(solution)/shard_map/ppermute | solution.py:1039
  40.8 20.2 %collective-permute-start.11 = (bf16[8,42,16,128]{3,2,1,0:T(8,128)(2,1)}, bf16[8,42,16,128]{3,2,1,0:T(8,128)(2,1)}, u32[]{:S(2)}, u32[]{:S(2)}) collective-permute-start(bf16[8,42,16,128]{3,2,1,0:T(8,128)(2,1)} %constant_dynamic-update-slice_fusion.5.refs_4_), channel_id=1, source_target_pairs={{0,2},{1,5},{2,0},{3,7},{4,6},{5,1},{6,4},{7,3},{8,10},{9,13},{10,... | collective-permute-start | bytes 4128776 | tf_op jit(solution)/shard_map/ppermute | solution.py:1039
  50.9 14.5 %collective-permute-start.12 = (bf16[8,42,16,128]{3,2,1,0:T(8,128)(2,1)}, bf16[8,42,16,128]{3,2,1,0:T(8,128)(2,1)}, u32[]{:S(2)}, u32[]{:S(2)}) collective-permute-start(bf16[8,42,16,128]{3,2,1,0:T(8,128)(2,1)} %constant_dynamic-update-slice_fusion.5.refs_4_), channel_id=1, source_target_pairs={{0,1},{1,0},{2,3},{3,2},{4,5},{5,4},{6,7},{7,6},{8,9},{9,8},{10,11... | collective-permute-start | bytes 4128776 | tf_op jit(solution)/shard_map/ppermute | solution.py:1039
  181.5 24.4 %collective-permute-start.15 = (bf16[56,128,128]{2,1,0:T(8,128)(2,1)S(1)}, bf16[56,128,128]{2,1,0:T(8,128)(2,1)}, u32[]{:S(2)}, u32[]{:S(2)}) collective-permute-start(bf16[56,128,128]{2,1,0:T(8,128)(2,1)S(1)} %get-tuple-element.139), channel_id=1, source_target_pairs={{0,2},{1,5},{2,0},{3,7},{4,6},{5,1},{6,4},{7,3},{8,10},{9,13},{10,... | collective-permute-start | bytes 5505032 | tf_op jit(solution)/shard_map/ppermute | solution.py:1039
  185.9 19.0 %collective-permute-start.19 = (bf16[4,128,128]{2,1,0:T(8,128)(2,1)}, bf16[4,128,128]{2,1,0:T(8,128)(2,1)S(1)}, u32[]{:S(2)}, u32[]{:S(2)}) collective-permute-start(bf16[4,128,128]{2,1,0:T(8,128)(2,1)} %get-tuple-element.149), channel_id=1, source_target_pairs={{0,24},{1,25},{2,26},{3,27},{4,28},{5,29},{6,30},{7,31},{8,0},{9,1... | collective-permute-start | bytes 393224 | tf_op jit(solution)/shard_map/ppermute | solution.py:1039
  190.3 15.6 %collective-permute-start.18 = (bf16[4,128,128]{2,1,0:T(8,128)(2,1)}, bf16[4,128,128]{2,1,0:T(8,128)(2,1)S(1)}, u32[]{:S(2)}, u32[]{:S(2)}) collective-permute-start(bf16[4,128,128]{2,1,0:T(8,128)(2,1)} %get-tuple-element.150), channel_id=1, source_target_pairs={{0,16},{1,17},{2,18},{3,19},{4,20},{5,21},{6,22},{7,23},{8,24},{9,... | collective-permute-start | bytes 393224 | tf_op jit(solution)/shard_map/ppermute | solution.py:1039
  193.7 12.2 %collective-permute-start.17 = (bf16[4,128,128]{2,1,0:T(8,128)(2,1)}, bf16[4,128,128]{2,1,0:T(8,128)(2,1)}, u32[]{:S(2)}, u32[]{:S(2)}) collective-permute-start(bf16[4,128,128]{2,1,0:T(8,128)(2,1)} %get-tuple-element.151), channel_id=1, source_target_pairs={{0,8},{1,9},{2,10},{3,11},{4,12},{5,13},{6,14},{7,15},{8,16},{9,17... | collective-permute-start | bytes 393224 | tf_op jit(solution)/shard_map/ppermute | solution.py:1039
  208.2 14.2 %collective-permute-start.20 = (bf16[28,128,128]{2,1,0:T(8,128)(2,1)S(1)}, bf16[28,128,128]{2,1,0:T(8,128)(2,1)S(1)}, u32[]{:S(2)}, u32[]{:S(2)}) collective-permute-start(bf16[28,128,128]{2,1,0:T(8,128)(2,1)S(1)} %get-tuple-element.141), channel_id=1, source_target_pairs={{0,4},{1,3},{2,6},{3,1},{4,0},{5,7},{6,2},{7,5},{8,12},{9,11},{10,... | collective-permute-start | bytes 2752520 | tf_op jit(solution)/shard_map/ppermute | solution.py:1039
  210.2 8.9 %collective-permute-start.21 = (bf16[2,128,128]{2,1,0:T(8,128)(2,1)S(1)}, bf16[2,128,128]{2,1,0:T(8,128)(2,1)S(1)}, u32[]{:S(2)}, u32[]{:S(2)}) collective-permute-start(bf16[2,128,128]{2,1,0:T(8,128)(2,1)S(1)} %get-tuple-element.153), channel_id=1, source_target_pairs={{0,2},{1,5},{2,0},{3,7},{4,6},{5,1},{6,4},{7,3},{8,10},{9,13},{10,... | collective-permute-start | bytes 196616 | tf_op jit(solution)/shard_map/ppermute | solution.py:1039
  224.1 23.2 %collective-permute-start.25 = (bf16[1,128,128]{2,1,0:T(8,128)(2,1)S(1)}, bf16[1,128,128]{2,1,0:T(8,128)(2,1)S(1)}, u32[]{:S(2)}, u32[]{:S(2)}) collective-permute-start(bf16[1,128,128]{2,1,0:T(8,128)(2,1)S(1)} %get-tuple-element.159), channel_id=1, source_target_pairs={{0,4},{1,3},{2,6},{3,1},{4,0},{5,7},{6,2},{7,5},{8,12},{9,11},{10,... | collective-permute-start | bytes 98312 | tf_op jit(solution)/shard_map/ppermute | solution.py:1039
  225.0 22.4 %collective-permute-start.24 = (bf16[7,128,128]{2,1,0:T(8,128)(2,1)S(1)}, bf16[7,128,128]{2,1,0:T(8,128)(2,1)S(1)}, u32[]{:S(2)}, u32[]{:S(2)}) collective-permute-start(bf16[7,128,128]{2,1,0:T(8,128)(2,1)S(1)} %get-tuple-element.143), channel_id=1, source_target_pairs={{0,24},{1,25},{2,26},{3,27},{4,28},{5,29},{6,30},{7,31},{8,0},{9,1... | collective-permute-start | bytes 688136 | tf_op jit(solution)/shard_map/ppermute | solution.py:1039
  228.3 22.8 %collective-permute-start.23 = (bf16[7,128,128]{2,1,0:T(8,128)(2,1)S(1)}, bf16[7,128,128]{2,1,0:T(8,128)(2,1)S(1)}, u32[]{:S(2)}, u32[]{:S(2)}) collective-permute-start(bf16[7,128,128]{2,1,0:T(8,128)(2,1)S(1)} %get-tuple-element.144), channel_id=1, source_target_pairs={{0,16},{1,17},{2,18},{3,19},{4,20},{5,21},{6,22},{7,23},{8,24},{9,... | collective-permute-start | bytes 688136 | tf_op jit(solution)/shard_map/ppermute | solution.py:1039
  232.0 19.0 %collective-permute-start.22 = (bf16[7,128,128]{2,1,0:T(8,128)(2,1)S(1)}, bf16[7,128,128]{2,1,0:T(8,128)(2,1)S(1)}, u32[]{:S(2)}, u32[]{:S(2)}) collective-permute-start(bf16[7,128,128]{2,1,0:T(8,128)(2,1)S(1)} %get-tuple-element.145), channel_id=1, source_target_pairs={{0,8},{1,9},{2,10},{3,11},{4,12},{5,13},{6,14},{7,15},{8,16},{9,17... | collective-permute-start | bytes 688136 | tf_op jit(solution)/shard_map/ppermute | solution.py:1039
  256.4 12.7 %all-to-all-start = ((bf16[8,8,16,128]{3,2,1,0:T(8,128)(2,1)}), bf16[8,8,16,128]{3,2,1,0:T(8,128)(2,1)S(1)}, u32[]{:S(2)}, u32[]{:S(2)}) async-start(bf16[8,8,16,128]{3,2,1,0:T(8,128)(2,1)} %get-tuple-element.130), calls=%async_computation | async-start | bytes 524288 | tf_op jit(solution)/shard_map/all_to_all | solution.py:1245
  271.2 26.1 %all-to-all-start.1 = ((bf16[8,25,16,128]{3,2,1,0:T(8,128)(2,1)}), bf16[8,25,16,128]{3,2,1,0:T(8,128)(2,1)S(1)}, u32[]{:S(2)}, u32[]{:S(2)}) async-start(bf16[8,25,16,128]{3,2,1,0:T(8,128)(2,1)} %add_tiles.1), calls=%async_computation.1 | async-start | bytes 1638400 | tf_op jit(solution)/shard_map/all_to_all | solution.py:1251
  277.2 6.9 %collective-permute-start.28 = (bf16[64,16,128]{2,1,0:T(8,128)(2,1)S(1)}, bf16[64,16,128]{2,1,0:T(8,128)(2,1)S(1)}, u32[]{:S(2)}, u32[]{:S(2)}) collective-permute-start(bf16[64,16,128]{2,1,0:T(8,128)(2,1)S(1)} %bitcast.100), channel_id=1, source_target_pairs={{0,2},{1,3},{2,0},{3,1},{4,6},{5,7},{6,4},{7,5},{8,10},{9,11},{10,... | collective-permute-start | bytes 786440 | tf_op jit(solution)/shard_map/ppermute | solution.py:1039
  (28 other events, 148.0 us)

commit v5 on v4

--- a/solution.py
+++ b/solution.py
@@ -238,37 +238,52 @@
     )(frames, inp, stats, *pieces)
 
 
-def conv_kernel(chunks, frames_s, dest_s, e_ref, o_ref, inp, emb, params, *refs):
-    pieces, (res, normed, stats, w_out, w, sem, sem_out) = refs[: -7], refs[-7:]
+def conv_kernel(chunks, frames_s, dest_s, e_hbm, o_hbm, inp_hbm, emb, params, *refs):
+    pieces, (res, normed, stats, w_out, w, e_ref, o_ref, inp, sem, sem_in, sem_out) = refs[:-11], refs[-11:]
     c = pl.program_id(0)
+    n = e_ref.shape[0]
     per_chunk = len(pieces) // len(chunks)
     row_share = pieces[0].shape[2]
+    copies = []
+    for j, (skip, start, count) in enumerate(chunks):
+        for a in range(per_chunk):
+            ref = pieces[j * per_chunk + a]
+            for p in range(ref.shape[0]):
+                i = a * ref.shape[0] + p
+                row = pl.multiple_of(dest_s[1, i], row_share)
+                where = w.at[pl.ds(dest_s[0, i] + start, count), pl.ds(row, row_share), :]
+                copies.append((i, pltpu.make_async_copy(ref.at[p, pl.ds(skip, count)], where, sem.at[len(copies)])))
+    clips = [
+        [
+            pltpu.make_async_copy(src.at[k], dst.at[k], sem_in.at[3 * k + j])
+            for j, (src, dst) in enumerate(((e_hbm, e_ref), (o_hbm, o_ref), (inp_hbm, inp)))
+        ]
+        for k in range(n)
+    ]
+
+    def weights(now, act):
+        for i, copy in copies:
+            pl.when((dest_s[0, i] < QUERY0) == now)(functools.partial(act, copy))
 
     @pl.when(c == 0)
     def _():
-        copies = []
-        for j, (skip, start, count) in enumerate(chunks):
-            for a in range(per_chunk):
-                ref = pieces[j * per_chunk + a]
-                for p in range(ref.shape[0]):
-                    i = a * ref.shape[0] + p
-                    first = dest_s[0, i] + start
-                    row = pl.multiple_of(dest_s[1, i], row_share)
-                    copies.append(
-                        pltpu.make_async_copy(
-                            ref.at[p, pl.ds(skip, count)],
-                            w.at[pl.ds(first, count), pl.ds(row, row_share), :],
-                            sem.at[len(copies)],
-                        )
-                    )
-        for copy in copies:
+        weights(True, lambda copy: copy.start())
+        for copy in clips[0]:
             copy.start()
-        for copy in copies:
-            copy.wait()
-        pltpu.make_async_copy(w, w_out, sem_out).start()
+        weights(False, lambda copy: copy.start())
+        for k in range(1, n):
+            for copy in clips[k]:
+                copy.start()
+        weights(True, lambda copy: copy.wait())
+
+    for k in range(n):
+        @pl.when(c == k)
+        def _(k=k):
+            for copy in clips[k]:
+                copy.wait()
 
     rows = frames_s[c] * BINS
-    R = 256
+    R = 512
     T = 64
     zero = jnp.zeros((8, CH), F32)
     inv_n = 1.0 / (rows * (CH // GROUPS)).astype(F32)
@@ -280,12 +295,18 @@
         acc = jnp.zeros((R, CH), F32)
         for t in range(9):
             df, db = divmod(t, 3)
-            acc = acc + nn(window(e_ref, o_ref, df, db, r, R), mat(w, t * SQ, 4, 4))
-        v = inp[0, pl.ds(r, R), :] + acc * CONV_SCALE + add
+            acc = acc + nn(window(e_ref, o_ref, df, db, r, R, (c,)), mat(w, t * SQ, 4, 4))
+        v = inp[c, pl.ds(r, R), :] + acc * CONV_SCALE + add
         res[0, pl.ds(r, R), :] = v
         return s + fold8(jnp.where(row_iota(r, R) < rows, v, 0.0))
 
     s = lax.fori_loop(0, POS // R, tile, zero)
+
+    @pl.when(c == 0)
+    def _():
+        weights(False, lambda copy: copy.wait())
+        pltpu.make_async_copy(w, w_out, sem_out).start()
+
     mean = group_sums(s) * inv_n
 
     def second(i, s):
@@ -334,9 +355,9 @@
             num_scalar_prefetch=2,
             grid=(n,),
             in_specs=[
-                per_clip((3, POS, CH)),
-                per_clip((3, POS + 16, CH)),
-                per_clip((POS, CH)),
+                pl.BlockSpec(memory_space=pl.ANY),
+                pl.BlockSpec(memory_space=pl.ANY),
+                pl.BlockSpec(memory_space=pl.ANY),
                 per_clip((16, CH)),
                 whole((8, CH)),
             ]
@@ -349,7 +370,11 @@
             ],
             scratch_shapes=[
                 pltpu.VMEM((NBLK, BS, BS), BF16),
+                pltpu.VMEM((n, 3, POS, CH), BF16),
+                pltpu.VMEM((n, 3, POS + 16, CH), BF16),
+                pltpu.VMEM((n, POS, CH), F32),
                 pltpu.SemaphoreType.DMA((copies,)),
+                pltpu.SemaphoreType.DMA((3 * n,)),
                 pltpu.SemaphoreType.DMA(()),
             ],
         ),
@@ -446,7 +471,12 @@
         return carry
 
     odq_s[...] = jnp.zeros_like(odq_s)
-    lax.fori_loop(0, steps, step, 0)
+    def four(i, carry):
+        for u in range(4):
+            carry = step(4 * i + u, carry)
+        return carry
+
+    lax.fori_loop(0, steps // 4, four, 0)
     back(steps - 1, 1)
     for slab in range(HEADS // 2):
         cols = slice(slab * BS, (slab + 1) * BS)
@@ -695,7 +725,7 @@
 
 
 def transposed_conv(e_ref, o_ref, w, out):
-    R = 256
+    R = 512
 
     def conv(i, carry):
         r = pl.multiple_of(i * R, R)

time: 301 us -> 295 us (0.980)
  Pallas kernels: 166 us -> 159 us
    pallas_call x1, Pallas kernels: 52 us -> 48 us  [attention(): pl.pallas_call(attn_kernel, out_shape=(jax.ShapeDtypeStruct((n, POS, CH),...]
  transfers between devices with their start and end apart: 32 -> 32, of which waited for: 13 -> 13; matrix products, arithmetic and copies ran while one was open for 7% -> 7% of each run, Pallas kernels for 18% -> 19%
where the time goes in v5:
time: 295 us; the launch traced here: 294 us
  Pallas kernels  159 us (54%)
  starting transfers between devices  52.1 us (18%)
  waiting for transfers between devices  44.4 us (15%)
  local copies, waits for them, and re-layouts  18.8 us (6%)
  other arithmetic  18.6 us (6%)
    pallas_call x1, Pallas kernels, attention(): pl.pallas_call(attn_kernel, out_shape=(jax.ShapeDtypeStruct((n, POS, CH),...  48 us
    ppermute x30, starting transfers between devices, permute(): return lax.ppermute(value, ('dp', 'mp'), pairs)  42.7 us
    ppermute x30, waiting for transfers between devices, permute(): return lax.ppermute(value, ('dp', 'mp'), pairs)  36.8 us
    pallas_call x1, Pallas kernels, tap_gradients(): pl.pallas_call(functools.partial(taps_kernel, counts), out_shape=(jax.Sha...  27.3 us
    pallas_call x1, Pallas kernels, conv_forward(): pl.pallas_call(functools.partial(conv_kernel, chunks), out_shape=(jax.Sha...  23.3 us
    pallas_call x1, Pallas kernels, whole_backward(): pl.pallas_call(functools.partial(clip_kernel, clip), out_shape=(jax.Shape...  14.9 us
    pallas_call x1, Pallas kernels, acts_gradient(): pl.pallas_call(acts_grad_kernel, out_shape=jax.ShapeDtypeStruct((POS, CH)...  10.8 us
    pallas_call x1, Pallas kernels, acts_windows(): pl.pallas_call(acts_kernel, out_shape=(jax.ShapeDtypeStruct((n, 3, POS, C...  8.58 us
  transfers between devices with their start and end apart: 32, of which 13 were waited for; matrix products, arithmetic and copies ran while one was open for 7% of the time, Pallas kernels for 19%

profile of v5, /device:TPU:0, one launch (start us, length us, event | category | flops | bytes accessed | tf_op | source)
XLA Modules:
  0.0 294.1 jit_solution(3283381569788106025)
XLA Ops:
  2.8 4.1 %collective-permute-start.4 = (bf16[20,16,128]{2,1,0:T(8,128)(2,1)S(1)}, bf16[20,16,128]{2,1,0:T(8,128)(2,1)S(1)}, u32[]{:S(2)}, u32[]{:S(2)}) collective-permute-start(bf16[20,16,128]{2,1,0:T(8,128)(2,1)S(1)} %get-tuple-element.156), channel_id=1, source_target_pairs={{0,16},{1,17},{2,18},{3,19},{4,20},{5,21},{6,22},{7,23},{8,24},{9,... | collective-permute-start | bytes 245768 | tf_op jit(solution)/shard_map/ppermute | solution.py:1069
  18.5 5.4 %collective-permute-done.6 = bf16[4,20,16,128]{3,2,1,0:T(8,128)(2,1)S(1)} collective-permute-done((bf16[4,20,16,128]{3,2,1,0:T(8,128)(2,1)S(1)}, bf16[4,20,16,128]{3,2,1,0:T(8,128)(2,1)S(1)}, u32[]{:S(2)}, u32[]{:S(2)}) %collective-permute-start.6) | collective-permute-done | bytes 327712 | tf_op jit(solution)/shard_map/ppermute | solution.py:1069
  29.5 8.4 %inputs_stats.1 = (f32[2,1024,512]{2,1,0:T(8,128)}, bf16[2,1024,512]{2,1,0:T(8,128)(2,1)}, f32[2,8,512]{2,1,0:T(8,128)}, f32[2,8,512]{2,1,0:T(8,128)}) custom-call(s32[2]{0:T(128)} %frames_s.10, f32[2,2]{1,0:T(2,128)} %pad_maximum_fusion.5.trig_s, f32[2,1024,512]{2,1,0:T(8,128)} %clean.1, f32[2,1024,512]{2,1,0:T(8,128)} %noise.1, f32[2,1024,512]{2,1,0:T(8,128)} %cot.3), custom_call_target="tpu_custom_call" | custom-call | flops 1000000 | bytes 1000000 | tf_op jit(solution)/shard_map/inputs_stats/pallas_call | solution.py:159
  52.4 8.6 %acts.1 = (bf16[2,3,1024,512]{3,2,1,0:T(8,128)(2,1)}, bf16[2,3,1040,512]{3,2,1,0:T(8,128)(2,1)}, f32[8,512]{1,0:T(8,128)}) custom-call(s32[2]{0:T(128)} %frames_s.10, f32[2,1024,512]{2,1,0:T(8,128)} %get-tuple-element.79.inp.inp_hbm, f32[2,8,512]{2,1,0:T(8,128)} %get-tuple-element.80.stats, bf16[8,20,16,128]{3,2,1,0:T(8,128)(2,1)} %copy-done.2, ...), custom_call_target="tpu_custom_call" | custom-call | flops 1000000 | bytes 1000000 | tf_op jit(solution)/shard_map/acts/pallas_call | solution.py:210
  65.4 23.3 %conv_forward.1 = (f32[2,1024,512]{2,1,0:T(8,128)}, bf16[2,1024,512]{2,1,0:T(8,128)(2,1)}, f32[2,8,512]{2,1,0:T(8,128)}, bf16[240,128,128]{2,1,0:T(8,128)(2,1)}) custom-call(s32[2]{0:T(128)} %frames_s.10, s32[2,32]{1,0:T(2,128)} %pad_add_fusion.dest_s, bf16[2,3,1024,512]{3,2,1,0:T(8,128)(2,1)} %get-tuple-element.82.e_hbm, ...), custom_call_target="tpu_custom_call" | custom-call | flops 9663676416 | bytes 28068672 | tf_op jit(solution)/shard_map/conv_forward/pallas_call | solution.py:346
  88.7 48.0 %attention.1 = (f32[2,1024,512]{2,1,0:T(8,128)}, bf16[2,1024,512]{2,1,0:T(8,128)(2,1)}, bf16[80,128,128]{2,1,0:T(8,128)(2,1)}) custom-call(s32[2]{0:T(128)} %frames_s.10, bf16[2,1024,512]{2,1,0:T(8,128)(2,1)} %get-tuple-element.87.normed, bf16[2,512,768]{2,1,0:T(8,128)(2,1)} %tokens.1, bf16[2,768,512]{2,1,0:T(8,128)(2,1)} %bitcast.98, ...), custom_call_target="tpu_custom_call" | custom-call | flops 19327352832 | bytes 16777216 | tf_op jit(solution)/shard_map/attention/pallas_call | solution.py:521
  136.6 27.3 %tap_gradients.1 = (f32[2,1024,512]{2,1,0:T(8,128)}, f32[2,24,512]{2,1,0:T(8,128)}, bf16[2,3,1024,512]{3,2,1,0:T(8,128)(2,1)}, bf16[2,3,1040,512]{3,2,1,0:T(8,12...) custom-call(s32[2]{0:T(128)} %frames_s.10, ...), custom_call_target="tpu_custom_call" | custom-call | flops 10737418240 | bytes 51457280 | tf_op jit(solution)/shard_map/tap_gradients/pallas_call | solution.py:684
  164.5 6.2 %collective-permute-done.14 = bf16[112,128,128]{2,1,0:T(8,128)(2,1)S(1)} collective-permute-done((bf16[112,128,128]{2,1,0:T(8,128)(2,1)}, bf16[112,128,128]{2,1,0:T(8,128)(2,1)S(1)}, u32[]{:S(2)}, u32[]{:S(2)}) %collective-permute-start.14) | collective-permute-done | bytes 3670048 | tf_op jit(solution)/shard_map/ppermute | solution.py:1069
  170.8 4.3 %add_convert_fusion = bf16[112,128,128]{2,1,0:T(8,128)(2,1)S(1)} fusion(bf16[112,128,128]{2,1,0:T(8,128)(2,1)S(1)} %collective-permute-done.14, bf16[112,128,128]{2,1,0:T(8,128)(2,1)} %get-tuple-element.96), kind=kLoop, calls=%fused_computation | loop fusion | flops 7340032 | bytes 11010048 | tf_op jit(solution)/shard_map/convert_element_type | solution.py:1132
  180.0 4.4 %collective-permute-start.19 = (bf16[4,128,128]{2,1,0:T(8,128)(2,1)}, bf16[4,128,128]{2,1,0:T(8,128)(2,1)S(1)}, u32[]{:S(2)}, u32[]{:S(2)}) collective-permute-start(bf16[4,128,128]{2,1,0:T(8,128)(2,1)} %get-tuple-element.149), channel_id=1, source_target_pairs={{0,24},{1,25},{2,26},{3,27},{4,28},{5,29},{6,30},{7,31},{8,0},{9,1... | collective-permute-start | bytes 393224 | tf_op jit(solution)/shard_map/ppermute | solution.py:1069
  184.4 3.4 %collective-permute-start.18 = (bf16[4,128,128]{2,1,0:T(8,128)(2,1)}, bf16[4,128,128]{2,1,0:T(8,128)(2,1)S(1)}, u32[]{:S(2)}, u32[]{:S(2)}) collective-permute-start(bf16[4,128,128]{2,1,0:T(8,128)(2,1)} %get-tuple-element.150), channel_id=1, source_target_pairs={{0,16},{1,17},{2,18},{3,19},{4,20},{5,21},{6,22},{7,23},{8,24},{9,... | collective-permute-start | bytes 393224 | tf_op jit(solution)/shard_map/ppermute | solution.py:1069
  187.8 10.8 %acts_gradient.1.ag = f32[1024,512]{1,0:T(8,128)} custom-call(bf16[2,3,1024,512]{3,2,1,0:T(8,128)(2,1)} %get-tuple-element.115.e_ref, bf16[2,3,1040,512]{3,2,1,0:T(8,128)(2,1)} %get-tuple-element.101.o_ref, bf16[240,128,128]{2,1,0:T(8,128)(2,1)} %get-tuple-element.90.w), custom_call_target="tpu_custom_call" | custom-call | flops 4831838208 | bytes 12582912 | tf_op jit(solution)/shard_map/acts_gradient/pallas_call | solution.py:752
  206.1 7.1 %input_backward.1 = (f32[2,1024,512]{2,1,0:T(8,128)}, f32[1,16,512]{2,1,0:T(8,128)}) custom-call(s32[2]{0:T(128)} %frames_s.10, f32[1024,512]{1,0:T(8,128)} %acts_gradient.1.ag, f32[2,1024,512]{2,1,0:T(8,128)} %get-tuple-element.79.inp.inp_hbm, f32[2,8,512]{2,1,0:T(8,128)} %get-tuple-element.80.stats, f32[2,1024,512]{2,1,0:T(8,128)} %get-tuple-element.109.rgrad, ...), custom_call_target="tpu_custom_call" | custom-call | flops 15728640 | bytes 10485760 | tf_op jit(solution)/shard_map/input_backward/pallas_call | solution.py:822
  213.2 3.3 %collective-permute-done.20 = bf16[28,128,128]{2,1,0:T(8,128)(2,1)S(1)} collective-permute-done((bf16[28,128,128]{2,1,0:T(8,128)(2,1)S(1)}, bf16[28,128,128]{2,1,0:T(8,128)(2,1)S(1)}, u32[]{:S(2)}, u32[]{:S(2)}) %collective-permute-start.20) | collective-permute-done | bytes 917536 | tf_op jit(solution)/shard_map/ppermute | solution.py:1069
  219.1 3.2 %collective-permute-start.24 = (bf16[7,128,128]{2,1,0:T(8,128)(2,1)S(1)}, bf16[7,128,128]{2,1,0:T(8,128)(2,1)S(1)}, u32[]{:S(2)}, u32[]{:S(2)}) collective-permute-start(bf16[7,128,128]{2,1,0:T(8,128)(2,1)S(1)} %get-tuple-element.143), channel_id=1, source_target_pairs={{0,24},{1,25},{2,26},{3,27},{4,28},{5,29},{6,30},{7,31},{8,0},{9,1... | collective-permute-start | bytes 688136 | tf_op jit(solution)/shard_map/ppermute | solution.py:1069
  222.3 3.7 %collective-permute-start.23 = (bf16[7,128,128]{2,1,0:T(8,128)(2,1)S(1)}, bf16[7,128,128]{2,1,0:T(8,128)(2,1)S(1)}, u32[]{:S(2)}, u32[]{:S(2)}) collective-permute-start(bf16[7,128,128]{2,1,0:T(8,128)(2,1)S(1)} %get-tuple-element.144), channel_id=1, source_target_pairs={{0,16},{1,17},{2,18},{3,19},{4,20},{5,21},{6,22},{7,23},{8,24},{9,... | collective-permute-start | bytes 688136 | tf_op jit(solution)/shard_map/ppermute | solution.py:1069
  226.0 14.9 %whole_backward.1 = (f32[2,1024,512]{2,1,0:T(8,128)}, f32[1,16,512]{2,1,0:T(8,128)}) custom-call(s32[2]{0:T(128)} %frames_s.10, bf16[2,3,1024,512]{3,2,1,0:T(8,128)(2,1)} %get-tuple-element.115.e_ref, bf16[2,3,1040,512]{3,2,1,0:T(8,128)(2,1)} %get-tuple-element.101.o_ref, ...), custom_call_target="tpu_custom_call", output_to_operand_aliasing={{0}: (8, {})} | custom-call | flops 4831838208 | bytes 12582912 | tf_op jit(solution)/shard_map/whole_backward/pallas_call | solution.py:850
  241.0 4.2 %collective-permute-done.23.refs_4_ = bf16[7,128,128]{2,1,0:T(8,128)(2,1)S(1)} collective-permute-done((bf16[7,128,128]{2,1,0:T(8,128)(2,1)S(1)}, bf16[7,128,128]{2,1,0:T(8,128)(2,1)S(1)}, u32[]{:S(2)}, u32[]{:S(2)}) %collective-permute-start.23) | collective-permute-done | bytes 229408 | tf_op jit(solution)/shard_map/ppermute | solution.py:1069
  245.9 4.6 %owner_step.1 = (bf16[8,8,16,128]{3,2,1,0:T(8,128)(2,1)}, bf16[8,25,16,128]{3,2,1,0:T(8,128)(2,1)}) custom-call(s32[2]{0:T(128)} %pad_add_fusion.4.dp_s, bf16[1,128,128]{2,1,0:T(8,128)(2,1)} %get-tuple-element.128.refs_0_, bf16[1,128,128]{2,1,0:T(8,128)(2,1)} %copy-done.13, bf16[7,128,128]{2,1,0:T(8,128)(2,1)} %get-tuple-element.120.refs_2_, ...), custom_call_target="tpu_custom_call" | custom-call | flops 134217728 | bytes 2621440 | tf_op jit(solution)/shard_map/owner_step/pallas_call | solution.py:973
  250.6 3.4 %all-to-all-start = ((bf16[8,8,16,128]{3,2,1,0:T(8,128)(2,1)}), bf16[8,8,16,128]{3,2,1,0:T(8,128)(2,1)S(1)}, u32[]{:S(2)}, u32[]{:S(2)}) async-start(bf16[8,8,16,128]{3,2,1,0:T(8,128)(2,1)} %get-tuple-element.130), calls=%async_computation | async-start | bytes 524288 | tf_op jit(solution)/shard_map/all_to_all | solution.py:1275
  259.9 3.4 %collective-permute-done.27.refs_1_ = f32[8,8,128]{2,1,0:T(8,128)S(1)} collective-permute-done((f32[8,8,128]{2,1,0:T(8,128)S(1)}, f32[8,8,128]{2,1,0:T(8,128)S(1)}, u32[]{:S(2)}, u32[]{:S(2)}) %collective-permute-start.27) | collective-permute-done | bytes 32800 | tf_op jit(solution)/shard_map/ppermute | solution.py:1069
  265.4 5.9 %all-to-all-start.1 = ((bf16[8,25,16,128]{3,2,1,0:T(8,128)(2,1)}), bf16[8,25,16,128]{3,2,1,0:T(8,128)(2,1)S(1)}, u32[]{:S(2)}, u32[]{:S(2)}) async-start(bf16[8,25,16,128]{3,2,1,0:T(8,128)(2,1)} %add_tiles.1), calls=%async_computation.1 | async-start | bytes 1638400 | tf_op jit(solution)/shard_map/all_to_all | solution.py:1281
  271.8 6.4 %collective-permute-done.28 = bf16[64,16,128]{2,1,0:T(8,128)(2,1)S(1)} collective-permute-done((bf16[64,16,128]{2,1,0:T(8,128)(2,1)S(1)}, bf16[64,16,128]{2,1,0:T(8,128)(2,1)S(1)}, u32[]{:S(2)}, u32[]{:S(2)}) %collective-permute-start.28) | collective-permute-done | bytes 262176 | tf_op jit(solution)/shard_map/ppermute | solution.py:1069
  283.9 7.5 %all-to-all-done.1 = bf16[8,25,16,128]{3,2,1,0:T(8,128)(2,1)S(1)} async-done(((bf16[8,25,16,128]{3,2,1,0:T(8,128)(2,1)}), bf16[8,25,16,128]{3,2,1,0:T(8,128)(2,1)S(1)}, u32[]{:S(2)}, u32[]{:S(2)}) %all-to-all-start.1) | async-done | bytes 819232 | tf_op jit(solution)/shard_map/all_to_all | solution.py:1281
  (157 shorter events, 71.0 us)
Async XLA Ops:
  2.8 11.2 %collective-permute-start.4 = (bf16[20,16,128]{2,1,0:T(8,128)(2,1)S(1)}, bf16[20,16,128]{2,1,0:T(8,128)(2,1)S(1)}, u32[]{:S(2)}, u32[]{:S(2)}) collective-permute-start(bf16[20,16,128]{2,1,0:T(8,128)(2,1)S(1)} %get-tuple-element.156), channel_id=1, source_target_pairs={{0,16},{1,17},{2,18},{3,19},{4,20},{5,21},{6,22},{7,23},{8,24},{9,... | collective-permute-start | bytes 245768 | tf_op jit(solution)/shard_map/ppermute | solution.py:1069
  6.9 9.9 %collective-permute-start.3 = (bf16[20,16,128]{2,1,0:T(8,128)(2,1)S(1)}, bf16[20,16,128]{2,1,0:T(8,128)(2,1)S(1)}, u32[]{:S(2)}, u32[]{:S(2)}) collective-permute-start(bf16[20,16,128]{2,1,0:T(8,128)(2,1)S(1)} %get-tuple-element.156), channel_id=1, source_target_pairs={{0,24},{1,25},{2,26},{3,27},{4,28},{5,29},{6,30},{7,31},{8,0},{9,1... | collective-permute-start | bytes 245768 | tf_op jit(solution)/shard_map/ppermute | solution.py:1069
  8.2 8.5 %collective-permute-start.5 = (bf16[20,16,128]{2,1,0:T(8,128)(2,1)S(1)}, bf16[20,16,128]{2,1,0:T(8,128)(2,1)S(1)}, u32[]{:S(2)}, u32[]{:S(2)}) collective-permute-start(bf16[20,16,128]{2,1,0:T(8,128)(2,1)S(1)} %get-tuple-element.156), channel_id=1, source_target_pairs={{0,8},{1,9},{2,10},{3,11},{4,12},{5,13},{6,14},{7,15},{8,16},{9,17... | collective-permute-start | bytes 245768 | tf_op jit(solution)/shard_map/ppermute | solution.py:1069
  8.9 16.7 %collective-permute-start.2 = (bf16[42,16,128]{2,1,0:T(8,128)(2,1)S(1)}, bf16[42,16,128]{2,1,0:T(8,128)(2,1)S(1)}, u32[]{:S(2)}, u32[]{:S(2)}) collective-permute-start(bf16[42,16,128]{2,1,0:T(8,128)(2,1)S(1)} %slice.134), channel_id=1, source_target_pairs={{0,8},{1,9},{2,10},{3,11},{4,12},{5,13},{6,14},{7,15},{8,16},{9,17... | collective-permute-start | bytes 516104 | tf_op jit(solution)/shard_map/ppermute | solution.py:1069
  10.5 15.7 %collective-permute-start.1 = (bf16[42,16,128]{2,1,0:T(8,128)(2,1)S(1)}, bf16[42,16,128]{2,1,0:T(8,128)(2,1)S(1)}, u32[]{:S(2)}, u32[]{:S(2)}) collective-permute-start(bf16[42,16,128]{2,1,0:T(8,128)(2,1)S(1)} %slice.134), channel_id=1, source_target_pairs={{0,16},{1,17},{2,18},{3,19},{4,20},{5,21},{6,22},{7,23},{8,24},{9,... | collective-permute-start | bytes 516104 | tf_op jit(solution)/shard_map/ppermute | solution.py:1069
  14.0 12.3 %collective-permute-start = (bf16[42,16,128]{2,1,0:T(8,128)(2,1)S(1)}, bf16[42,16,128]{2,1,0:T(8,128)(2,1)S(1)}, u32[]{:S(2)}, u32[]{:S(2)}) collective-permute-start(bf16[42,16,128]{2,1,0:T(8,128)(2,1)S(1)} %slice.134), channel_id=1, source_target_pairs={{0,24},{1,25},{2,26},{3,27},{4,28},{5,29},{6,30},{7,31},{8,0},{9,1... | collective-permute-start | bytes 516104 | tf_op jit(solution)/shard_map/ppermute | solution.py:1069
  16.8 7.1 %collective-permute-start.6 = (bf16[4,20,16,128]{3,2,1,0:T(8,128)(2,1)S(1)}, bf16[4,20,16,128]{3,2,1,0:T(8,128)(2,1)S(1)}, u32[]{:S(2)}, u32[]{:S(2)}) collective-permute-start(bf16[4,20,16,128]{3,2,1,0:T(8,128)(2,1)S(1)} %pad_maximum_fusion.2), channel_id=1, source_target_pairs={{0,4},{1,3},{2,6},{3,1},{4,0},{5,7},{6,2},{7,5},{8,12},{9,11},{10,... | collective-permute-start | bytes 983048 | tf_op jit(solution)/shard_map/ppermute | solution.py:1069
  24.0 16.8 %collective-permute-start.7 = (bf16[8,20,16,128]{3,2,1,0:T(8,128)(2,1)S(1)}, bf16[8,20,16,128]{3,2,1,0:T(8,128)(2,1)}, u32[]{:S(2)}, u32[]{:S(2)}) collective-permute-start(bf16[8,20,16,128]{3,2,1,0:T(8,128)(2,1)S(1)} %constant_dynamic-update-slice_fusion.refs_0_), channel_id=1, source_target_pairs={{0,2},{1,5},{2,0},{3,7},{4,6},{5,1},{6,4},{7,3},{8,10},{9,13},{10,... | collective-permute-start | bytes 1966088 | tf_op jit(solution)/shard_map/ppermute | solution.py:1069
  27.0 12.8 %collective-permute-start.10 = (bf16[4,42,16,128]{3,2,1,0:T(8,128)(2,1)S(1)}, bf16[4,42,16,128]{3,2,1,0:T(8,128)(2,1)S(1)}, u32[]{:S(2)}, u32[]{:S(2)}) collective-permute-start(bf16[4,42,16,128]{3,2,1,0:T(8,128)(2,1)S(1)} %pad_maximum_fusion), channel_id=1, source_target_pairs={{0,4},{1,3},{2,6},{3,1},{4,0},{5,7},{6,2},{7,5},{8,12},{9,11},{10,... | collective-permute-start | bytes 2064392 | tf_op jit(solution)/shard_map/ppermute | solution.py:1069
  40.8 20.2 %collective-permute-start.11 = (bf16[8,42,16,128]{3,2,1,0:T(8,128)(2,1)}, bf16[8,42,16,128]{3,2,1,0:T(8,128)(2,1)}, u32[]{:S(2)}, u32[]{:S(2)}) collective-permute-start(bf16[8,42,16,128]{3,2,1,0:T(8,128)(2,1)} %constant_dynamic-update-slice_fusion.5.refs_4_), channel_id=1, source_target_pairs={{0,2},{1,5},{2,0},{3,7},{4,6},{5,1},{6,4},{7,3},{8,10},{9,13},{10,... | collective-permute-start | bytes 4128776 | tf_op jit(solution)/shard_map/ppermute | solution.py:1069
  50.9 14.5 %collective-permute-start.12 = (bf16[8,42,16,128]{3,2,1,0:T(8,128)(2,1)}, bf16[8,42,16,128]{3,2,1,0:T(8,128)(2,1)}, u32[]{:S(2)}, u32[]{:S(2)}) collective-permute-start(bf16[8,42,16,128]{3,2,1,0:T(8,128)(2,1)} %constant_dynamic-update-slice_fusion.5.refs_4_), channel_id=1, source_target_pairs={{0,1},{1,0},{2,3},{3,2},{4,5},{5,4},{6,7},{7,6},{8,9},{9,8},{10,11... | collective-permute-start | bytes 4128776 | tf_op jit(solution)/shard_map/ppermute | solution.py:1069
  175.6 24.4 %collective-permute-start.15 = (bf16[56,128,128]{2,1,0:T(8,128)(2,1)S(1)}, bf16[56,128,128]{2,1,0:T(8,128)(2,1)}, u32[]{:S(2)}, u32[]{:S(2)}) collective-permute-start(bf16[56,128,128]{2,1,0:T(8,128)(2,1)S(1)} %get-tuple-element.139), channel_id=1, source_target_pairs={{0,2},{1,5},{2,0},{3,7},{4,6},{5,1},{6,4},{7,3},{8,10},{9,13},{10,... | collective-permute-start | bytes 5505032 | tf_op jit(solution)/shard_map/ppermute | solution.py:1069
  180.0 18.6 %collective-permute-start.19 = (bf16[4,128,128]{2,1,0:T(8,128)(2,1)}, bf16[4,128,128]{2,1,0:T(8,128)(2,1)S(1)}, u32[]{:S(2)}, u32[]{:S(2)}) collective-permute-start(bf16[4,128,128]{2,1,0:T(8,128)(2,1)} %get-tuple-element.149), channel_id=1, source_target_pairs={{0,24},{1,25},{2,26},{3,27},{4,28},{5,29},{6,30},{7,31},{8,0},{9,1... | collective-permute-start | bytes 393224 | tf_op jit(solution)/shard_map/ppermute | solution.py:1069
  184.4 15.6 %collective-permute-start.18 = (bf16[4,128,128]{2,1,0:T(8,128)(2,1)}, bf16[4,128,128]{2,1,0:T(8,128)(2,1)S(1)}, u32[]{:S(2)}, u32[]{:S(2)}) collective-permute-start(bf16[4,128,128]{2,1,0:T(8,128)(2,1)} %get-tuple-element.150), channel_id=1, source_target_pairs={{0,16},{1,17},{2,18},{3,19},{4,20},{5,21},{6,22},{7,23},{8,24},{9,... | collective-permute-start | bytes 393224 | tf_op jit(solution)/shard_map/ppermute | solution.py:1069
  187.8 12.2 %collective-permute-start.17 = (bf16[4,128,128]{2,1,0:T(8,128)(2,1)}, bf16[4,128,128]{2,1,0:T(8,128)(2,1)}, u32[]{:S(2)}, u32[]{:S(2)}) collective-permute-start(bf16[4,128,128]{2,1,0:T(8,128)(2,1)} %get-tuple-element.151), channel_id=1, source_target_pairs={{0,8},{1,9},{2,10},{3,11},{4,12},{5,13},{6,14},{7,15},{8,16},{9,17... | collective-permute-start | bytes 393224 | tf_op jit(solution)/shard_map/ppermute | solution.py:1069
  202.4 14.2 %collective-permute-start.20 = (bf16[28,128,128]{2,1,0:T(8,128)(2,1)S(1)}, bf16[28,128,128]{2,1,0:T(8,128)(2,1)S(1)}, u32[]{:S(2)}, u32[]{:S(2)}) collective-permute-start(bf16[28,128,128]{2,1,0:T(8,128)(2,1)S(1)} %get-tuple-element.141), channel_id=1, source_target_pairs={{0,4},{1,3},{2,6},{3,1},{4,0},{5,7},{6,2},{7,5},{8,12},{9,11},{10,... | collective-permute-start | bytes 2752520 | tf_op jit(solution)/shard_map/ppermute | solution.py:1069
  204.3 8.9 %collective-permute-start.21 = (bf16[2,128,128]{2,1,0:T(8,128)(2,1)S(1)}, bf16[2,128,128]{2,1,0:T(8,128)(2,1)S(1)}, u32[]{:S(2)}, u32[]{:S(2)}) collective-permute-start(bf16[2,128,128]{2,1,0:T(8,128)(2,1)S(1)} %get-tuple-element.153), channel_id=1, source_target_pairs={{0,2},{1,5},{2,0},{3,7},{4,6},{5,1},{6,4},{7,3},{8,10},{9,13},{10,... | collective-permute-start | bytes 196616 | tf_op jit(solution)/shard_map/ppermute | solution.py:1069
  218.3 22.7 %collective-permute-start.25 = (bf16[1,128,128]{2,1,0:T(8,128)(2,1)S(1)}, bf16[1,128,128]{2,1,0:T(8,128)(2,1)S(1)}, u32[]{:S(2)}, u32[]{:S(2)}) collective-permute-start(bf16[1,128,128]{2,1,0:T(8,128)(2,1)S(1)} %get-tuple-element.159), channel_id=1, source_target_pairs={{0,4},{1,3},{2,6},{3,1},{4,0},{5,7},{6,2},{7,5},{8,12},{9,11},{10,... | collective-permute-start | bytes 98312 | tf_op jit(solution)/shard_map/ppermute | solution.py:1069
  219.1 21.9 %collective-permute-start.24 = (bf16[7,128,128]{2,1,0:T(8,128)(2,1)S(1)}, bf16[7,128,128]{2,1,0:T(8,128)(2,1)S(1)}, u32[]{:S(2)}, u32[]{:S(2)}) collective-permute-start(bf16[7,128,128]{2,1,0:T(8,128)(2,1)S(1)} %get-tuple-element.143), channel_id=1, source_target_pairs={{0,24},{1,25},{2,26},{3,27},{4,28},{5,29},{6,30},{7,31},{8,0},{9,1... | collective-permute-start | bytes 688136 | tf_op jit(solution)/shard_map/ppermute | solution.py:1069
  222.3 22.9 %collective-permute-start.23 = (bf16[7,128,128]{2,1,0:T(8,128)(2,1)S(1)}, bf16[7,128,128]{2,1,0:T(8,128)(2,1)S(1)}, u32[]{:S(2)}, u32[]{:S(2)}) collective-permute-start(bf16[7,128,128]{2,1,0:T(8,128)(2,1)S(1)} %get-tuple-element.144), channel_id=1, source_target_pairs={{0,16},{1,17},{2,18},{3,19},{4,20},{5,21},{6,22},{7,23},{8,24},{9,... | collective-permute-start | bytes 688136 | tf_op jit(solution)/shard_map/ppermute | solution.py:1069
  226.0 19.2 %collective-permute-start.22 = (bf16[7,128,128]{2,1,0:T(8,128)(2,1)S(1)}, bf16[7,128,128]{2,1,0:T(8,128)(2,1)S(1)}, u32[]{:S(2)}, u32[]{:S(2)}) collective-permute-start(bf16[7,128,128]{2,1,0:T(8,128)(2,1)S(1)} %get-tuple-element.145), channel_id=1, source_target_pairs={{0,8},{1,9},{2,10},{3,11},{4,12},{5,13},{6,14},{7,15},{8,16},{9,17... | collective-permute-start | bytes 688136 | tf_op jit(solution)/shard_map/ppermute | solution.py:1069
  250.6 12.7 %all-to-all-start = ((bf16[8,8,16,128]{3,2,1,0:T(8,128)(2,1)}), bf16[8,8,16,128]{3,2,1,0:T(8,128)(2,1)S(1)}, u32[]{:S(2)}, u32[]{:S(2)}) async-start(bf16[8,8,16,128]{3,2,1,0:T(8,128)(2,1)} %get-tuple-element.130), calls=%async_computation | async-start | bytes 524288 | tf_op jit(solution)/shard_map/all_to_all | solution.py:1275
  265.4 26.1 %all-to-all-start.1 = ((bf16[8,25,16,128]{3,2,1,0:T(8,128)(2,1)}), bf16[8,25,16,128]{3,2,1,0:T(8,128)(2,1)S(1)}, u32[]{:S(2)}, u32[]{:S(2)}) async-start(bf16[8,25,16,128]{3,2,1,0:T(8,128)(2,1)} %add_tiles.1), calls=%async_computation.1 | async-start | bytes 1638400 | tf_op jit(solution)/shard_map/all_to_all | solution.py:1281
  271.3 6.9 %collective-permute-start.28 = (bf16[64,16,128]{2,1,0:T(8,128)(2,1)S(1)}, bf16[64,16,128]{2,1,0:T(8,128)(2,1)S(1)}, u32[]{:S(2)}, u32[]{:S(2)}) collective-permute-start(bf16[64,16,128]{2,1,0:T(8,128)(2,1)S(1)} %bitcast.100), channel_id=1, source_target_pairs={{0,2},{1,3},{2,0},{3,1},{4,6},{5,7},{6,4},{7,5},{8,10},{9,11},{10,... | collective-permute-start | bytes 786440 | tf_op jit(solution)/shard_map/ppermute | solution.py:1069
  (28 other events, 149.1 us)
